TPU v7x, 32 devices: a whole 2x2x4 slice. The times are simulated.
32 devices in a mesh: dp: 4 (over z), row: 4 (over x, core), col: 2 (over y).
Axes of the slice: x: 2, y: 2, z: 4, core: 2. Of those that a mesh axis runs over, the one named last changes fastest.
Arguments:
- inputs: bfloat16 [2048, 4096], P('row', ('dp', 'col')), may hold values from -6 to 6
- cotangent: bfloat16 [2048, 4096], P('row', ('dp', 'col')), may hold values from -6 to 6
- starts: int32 [4096], P(('dp', 'row')), may hold values from 0 to 1, as said below
- x_proj: bfloat16 [2048, 2560], P('row', 'col'), may hold values from -0.125 to 0.125
- y_proj: bfloat16 [2048, 2560], P('row', 'col'), may hold values from -0.125 to 0.125
- out_proj: bfloat16 [2560, 2048], P('col', 'row'), may hold values from -0.15625 to 0.15625
- gate_proj: bfloat16 [2048, 6144], P('row', 'col'), may hold values from -0.125 to 0.125
- up_proj: bfloat16 [2048, 6144], P('row', 'col'), may hold values from -0.125 to 0.125
- down_proj: bfloat16 [2048, 6144], P('row', 'col'), may hold values from -0.15625 to 0.15625
- mix_gain: float32 [2048], P('row'), may hold values from 0.5 to 1.5
- mlp_gain: float32 [2048], P('row'), may hold values from 0.5 to 1.5
- x_bias: float32 [2560], P('col'), may hold values from -3 to 3
- y_bias: float32 [2560], P('col'), may hold values from -3 to 3
- conv_w: float32 [4, 2560], P(None, 'col'), may hold values from -3 to 3
- conv_b: float32 [2560], P('col'), may hold values from -2 to 2
- rec_gate_w: bfloat16 [16, 160, 160], P('col'), may hold values from -0.5 to 0.5
- in_gate_w: bfloat16 [16, 160, 160], P('col'), may hold values from -0.5 to 0.5
- rec_gate_b: float32 [2560], P('col'), may hold values from -3 to 3
- in_gate_b: float32 [2560], P('col'), may hold values from -3 to 3
- decay_param: float32 [2560], P('col'), may hold values from -7 to -2
Outputs:
- output: bfloat16 [2048, 4096], P('row', ('dp', 'col'))
- inputs_grad: float32 [2048, 4096], P('row', ('dp', 'col'))
- x_proj_grad: float32 [2048, 2560], P('row', 'col')
- y_proj_grad: float32 [2048, 2560], P('row', 'col')
- out_proj_grad: float32 [2560, 2048], P('col', 'row')
- gate_proj_grad: float32 [2048, 6144], P('row', 'col')
- up_proj_grad: float32 [2048, 6144], P('row', 'col')
- down_proj_grad: float32 [2048, 6144], P('row', 'col')
- mix_gain_grad: float32 [2048], P('row')
- mlp_gain_grad: float32 [2048], P('row')
- x_bias_grad: float32 [2560], P('col')
- y_bias_grad: float32 [2560], P('col')
- conv_w_grad: float32 [4, 2560], P(None, 'col')
- conv_b_grad: float32 [2560], P('col')
- rec_gate_w_grad: float32 [16, 160, 160], P('col')
- in_gate_w_grad: float32 [16, 160, 160], P('col')
- rec_gate_b_grad: float32 [2560], P('col')
- in_gate_b_grad: float32 [2560], P('col')
- decay_param_grad: float32 [2560], P('col')
Inputs may be any that keep to these rules, and one draw needn't show every extreme that they name: `starts`: each packed sequence of 1024 tokens is filled in order with documents of 60 to 800 tokens, the last cut by the sequence's end; every sequence begins with 1.
All inputs are finite; a program needn't handle non-finite values.
Results may differ from a plain program's by a relative error of at most 0.019.
Values may be sent and summed in bfloat16 or wider, within the bound.
A program may use at most 256 MiB of HBM per device.

v0:
```python
import jax
import jax.numpy as jnp
from jax import lax
from jax.sharding import PartitionSpec as P

D = 2048


EPS = 1e-06
GATE_C = 8.0
CONTRACT_ROWS = (((0,), (0,)), ((), ()))
CONTRACT_COLS = (((1,), (1,)), ((), ()))
CONTRACT_PLAIN = (((1,), (0,)), ((), ()))


def from_behind(value, axis, by):
    count = lax.axis_size(axis)
    pairs = [(i, i + by) for i in range(count) if 0 <= i + by < count]
    return lax.ppermute(value, axis, pairs)


def carried_in(value, axis, join, neutral, backward):
    count, mine = (lax.axis_size(axis), lax.axis_index(axis))
    pieces = jax.tree.map(lambda part: lax.all_gather(part, axis), value)
    if backward:
        pieces = jax.tree.map(lambda part: part[::-1], pieces)
        mine = count - 1 - mine
    subtotal = jax.tree.map(
        lambda part, zero: jnp.full_like(part, 0) + jnp.asarray(zero, part.dtype), value, neutral
    )

    def hop(position, subtotal):
        longer = join(subtotal, jax.tree.map(lambda part: part[position], pieces))
        return jax.tree.map(lambda new, old: jnp.where(position < mine, new, old), longer, subtotal)

    return lax.fori_loop(0, count - 1, hop, subtotal)


def chain(earlier, later):
    return (earlier[0] * later[0], later[0] * earlier[1] + later[1])


def adjoint_chain(earlier, later):
    return (later[0] * earlier[0], later[1] + later[0] * earlier[1])


def gelu_tanh(values):
    return jax.nn.gelu(values, approximate=True)


def glu_piece(gate_vals, up_vals):
    return gelu_tanh(gate_vals) * up_vals


def causal_conv(values, conv_w, conv_b, segment_ids):
    result = values * conv_w[0] + conv_b
    for offset in range(1, conv_w.shape[0]):
        lagged = jnp.pad(values, ((offset, 0), (0, 0)))[:-offset]
        earlier_ids = jnp.pad(segment_ids, (offset, 0), constant_values=-1)[:-offset]
        result = (
            result + jnp.where((earlier_ids == segment_ids)[:, None], lagged, 0.0) * conv_w[offset]
        )
    return result


def local_recurrence(rec_pre, in_pre, conv_vals, decay_param, flags):
    rec_gate = jax.nn.sigmoid(rec_pre)
    in_gate = jax.nn.sigmoid(in_pre)
    log_keep = -GATE_C * rec_gate * jax.nn.softplus(decay_param)
    keep_rate = jnp.exp(log_keep)
    fresh = (flags == 1)[:, None]
    multiplier = jnp.where(fresh, 1.0, jnp.sqrt(-jnp.expm1(2.0 * log_keep)))
    driven = conv_vals * in_gate * multiplier
    carried = jnp.where(fresh, 0.0, keep_rate)
    cum_keep, states = lax.associative_scan(chain, (carried, driven), axis=0)
    return (cum_keep, states)


def row_sums(values):
    return lax.psum(values, "row")


def norm_forward(values, norm_gain):
    squares = row_sums(jnp.sum(values * values, axis=1))
    inv_rms = lax.rsqrt(squares / D + EPS)
    return (values * inv_rms[:, None] * norm_gain, inv_rms)


def norm_backward(values, inv_rms, norm_gain, incoming):
    scaled = norm_gain * incoming
    dots = row_sums(jnp.sum(scaled * values, axis=1))
    values_grad = inv_rms[:, None] * scaled - values * (inv_rms**3 * dots / D)[:, None]
    gain_grad = jnp.sum(incoming * values * inv_rms[:, None], axis=0)
    return (values_grad, gain_grad)


def gather_edge(values):
    return lax.all_gather(values, "col", axis=0, tiled=True)


def gather_mid(values):
    return lax.all_gather(values, "row", axis=0, tiled=True)


def row_partial(whole, weight, dims):
    return lax.psum_scatter(
        lax.dot_general(whole, weight, dims, preferred_element_type=jnp.float32),
        "row",
        scatter_dimension=0,
        tiled=True,
    )


def col_partial(whole, weight, dims):
    return lax.psum_scatter(
        lax.dot_general(whole, weight, dims, preferred_element_type=jnp.float32),
        "col",
        scatter_dimension=0,
        tiled=True,
    )


def project_in(normed, weight):
    whole = gather_edge(normed)
    result = row_partial(whole, weight, CONTRACT_PLAIN)
    return (result, whole)


def weight_grad(left, right):
    return lax.dot_general(left, right, CONTRACT_ROWS, preferred_element_type=jnp.float32)


def local(
    inputs,
    cotangent,
    starts,
    x_proj,
    y_proj,
    out_proj,
    gate_proj,
    up_proj,
    down_proj,
    mix_gain,
    mlp_gain,
    x_bias,
    y_bias,
    conv_w,
    conv_b,
    rec_gate_w,
    in_gate_w,
    rec_gate_b,
    in_gate_b,
    decay_param,
):
    rows_mid = starts.shape[0]
    rec_width = x_proj.shape[1]
    ff_width = gate_proj.shape[1]
    head_count = rec_gate_w.shape[0]
    margin = conv_w.shape[0] - 1
    mix_weights = jnp.concatenate([x_proj, y_proj], axis=1)
    mlp_weights = jnp.concatenate([gate_proj, up_proj], axis=1)
    cot_rows = cotangent.T
    resid = inputs.astype(jnp.float32).T
    normed_mix, inv_rms_mix = norm_forward(resid, mix_gain)
    normed_mix = normed_mix.astype(jnp.bfloat16)
    pre_both, whole_mix = project_in(normed_mix, mix_weights)
    x_pre = pre_both[:, :rec_width] + x_bias
    y_pre = pre_both[:, rec_width:] + y_bias
    x_tail, flag_tail = from_behind(
        (x_pre[rows_mid - margin :], starts[rows_mid - margin :].astype(jnp.float32)), "row", 1
    )
    ext_flags = jnp.concatenate([flag_tail.astype(jnp.int32), starts])
    ext_ids = jnp.cumsum(ext_flags, dtype=jnp.int32)
    ext_x = jnp.concatenate([x_tail, x_pre], axis=0)

    def conv_piece(values, taps, offsets):
        return causal_conv(values, taps, offsets, ext_ids)[margin:]

    conv_vals, conv_pull = jax.vjp(conv_piece, ext_x, conv_w, conv_b)
    conv_low = conv_vals.astype(jnp.bfloat16)
    conv_heads = conv_low.reshape(rows_mid, head_count, -1)
    rec_pre = (
        jnp.einsum(
            "thk,hkj->thj", conv_heads, rec_gate_w, preferred_element_type=jnp.float32
        ).reshape(rows_mid, rec_width)
        + rec_gate_b
    )
    in_pre = (
        jnp.einsum(
            "thk,hkj->thj", conv_heads, in_gate_w, preferred_element_type=jnp.float32
        ).reshape(rows_mid, rec_width)
        + in_gate_b
    )

    def scan_piece(rec_vals, in_vals, conv_input, decay_vals):
        return local_recurrence(rec_vals, in_vals, conv_input, decay_vals, starts)

    (cum_keep, local_states), scan_pull = jax.vjp(
        scan_piece, rec_pre, in_pre, conv_low.astype(jnp.float32), decay_param
    )
    ones_row = jnp.ones((rec_width,), jnp.float32)
    zeros_row = jnp.zeros((rec_width,), jnp.float32)
    incoming = carried_in(
        (cum_keep[rows_mid - 1], local_states[rows_mid - 1]),
        "row",
        chain,
        (ones_row, zeros_row),
        False,
    )
    state_prev = incoming[1]
    states = local_states + cum_keep * state_prev
    y_act, y_pull = jax.vjp(gelu_tanh, y_pre)
    mixed = (states * y_act).astype(jnp.bfloat16)
    whole_mixed = gather_mid(mixed)
    resid_mid = resid + col_partial(whole_mixed, out_proj, CONTRACT_PLAIN)
    normed_mlp, inv_rms_mlp = norm_forward(resid_mid, mlp_gain)
    normed_mlp = normed_mlp.astype(jnp.bfloat16)
    gate_up, whole_mlp = project_in(normed_mlp, mlp_weights)
    activ, activ_pull = jax.vjp(glu_piece, gate_up[:, :ff_width], gate_up[:, ff_width:])
    activ = activ.astype(jnp.bfloat16)
    whole_activ = gather_mid(activ)
    output = (resid_mid + col_partial(whole_activ, down_proj, CONTRACT_COLS)).astype(jnp.bfloat16)
    cot_whole = gather_edge(cot_rows)
    d_activ = row_partial(cot_whole, down_proj, CONTRACT_PLAIN)
    activ_rows = gather_mid(activ)
    grad_down = weight_grad(cot_whole, activ_rows)
    d_gate, d_up = activ_pull(d_activ)
    d_gate_up = jnp.concatenate([d_gate, d_up], axis=1).astype(jnp.bfloat16)
    d_gate_up_whole = gather_mid(d_gate_up)
    d_normed_mlp = col_partial(d_gate_up_whole, mlp_weights, CONTRACT_COLS)
    mlp_rows = gather_edge(normed_mlp)
    grad_gate_up = weight_grad(mlp_rows, d_gate_up_whole)
    d_norm_mid, grad_mlp_gain = norm_backward(resid_mid, inv_rms_mlp, mlp_gain, d_normed_mlp)
    d_resid_mid = cot_rows.astype(jnp.float32) + d_norm_mid
    d_branch = d_resid_mid.astype(jnp.bfloat16)
    branch_whole = gather_edge(d_branch)
    d_mixed = row_partial(branch_whole, out_proj, CONTRACT_COLS)
    mixed_rows = gather_mid(mixed)
    grad_out = weight_grad(mixed_rows, branch_whole)
    d_state = d_mixed * y_act
    (d_y_pre,) = y_pull(d_mixed * states)
    own_sens = jnp.sum(d_state * cum_keep, axis=0)
    outgoing = carried_in(
        (cum_keep[rows_mid - 1], own_sens), "row", adjoint_chain, (ones_row, zeros_row), True
    )
    d_total = d_state + jnp.pad(outgoing[1][None, :], ((rows_mid - 1, 0), (0, 0)))
    d_rec_pre, d_in_pre, d_conv_direct, grad_decay = scan_pull((d_total * state_prev, d_total))
    d_rec_low = d_rec_pre.astype(jnp.bfloat16)
    d_in_low = d_in_pre.astype(jnp.bfloat16)
    d_rec_heads = d_rec_low.reshape(rows_mid, head_count, -1)
    d_in_heads = d_in_low.reshape(rows_mid, head_count, -1)
    d_conv = d_conv_direct + jnp.einsum(
        "thj,hkj->thk", d_rec_heads, rec_gate_w, preferred_element_type=jnp.float32
    ).reshape(rows_mid, rec_width)
    d_conv = d_conv + jnp.einsum(
        "thj,hkj->thk", d_in_heads, in_gate_w, preferred_element_type=jnp.float32
    ).reshape(rows_mid, rec_width)
    grad_rec_w = jnp.einsum(
        "thk,thj->hkj", conv_heads, d_rec_heads, preferred_element_type=jnp.float32
    )
    grad_in_w = jnp.einsum(
        "thk,thj->hkj", conv_heads, d_in_heads, preferred_element_type=jnp.float32
    )
    grad_rec_b = jnp.sum(d_rec_low.astype(jnp.float32), axis=0)
    grad_in_b = jnp.sum(d_in_low.astype(jnp.float32), axis=0)
    d_ext, grad_conv_w, grad_conv_b = conv_pull(d_conv)
    d_from_next = from_behind(d_ext[:margin], "row", -1)
    d_x_pre = d_ext[margin:] + jnp.pad(d_from_next, ((rows_mid - margin, 0), (0, 0)))
    d_pre = jnp.concatenate([d_x_pre, d_y_pre], axis=1).astype(jnp.bfloat16)
    bias_sums = jnp.sum(d_pre.astype(jnp.float32), axis=0)
    d_pre_whole = gather_mid(d_pre)
    d_normed_mix = col_partial(d_pre_whole, mix_weights, CONTRACT_COLS)
    mix_rows = gather_edge(normed_mix)
    grad_mix = weight_grad(mix_rows, d_pre_whole)
    d_norm_in, grad_mix_gain = norm_backward(resid, inv_rms_mix, mix_gain, d_normed_mix)
    inputs_grad = d_resid_mid + d_norm_in
    grad_mix, grad_out, grad_gate_up, grad_down = (
        lax.psum(grad_mix.astype(jnp.bfloat16), "dp").astype(jnp.float32),
        lax.psum(grad_out.astype(jnp.bfloat16), "dp").astype(jnp.float32),
        lax.psum(grad_gate_up.astype(jnp.bfloat16), "dp").astype(jnp.float32),
        lax.psum(grad_down.astype(jnp.bfloat16), "dp").astype(jnp.float32),
    )
    (
        bias_sums,
        grad_conv_w,
        grad_conv_b,
        grad_rec_w,
        grad_in_w,
        grad_rec_b,
        grad_in_b,
        grad_decay,
    ) = (
        lax.psum(bias_sums.astype(jnp.bfloat16), ("dp", "row")).astype(jnp.float32),
        lax.psum(grad_conv_w.astype(jnp.bfloat16), ("dp", "row")).astype(jnp.float32),
        lax.psum(grad_conv_b.astype(jnp.bfloat16), ("dp", "row")).astype(jnp.float32),
        lax.psum(grad_rec_w.astype(jnp.bfloat16), ("dp", "row")).astype(jnp.float32),
        lax.psum(grad_in_w.astype(jnp.bfloat16), ("dp", "row")).astype(jnp.float32),
        lax.psum(grad_rec_b.astype(jnp.bfloat16), ("dp", "row")).astype(jnp.float32),
        lax.psum(grad_in_b.astype(jnp.bfloat16), ("dp", "row")).astype(jnp.float32),
        lax.psum(grad_decay.astype(jnp.bfloat16), ("dp", "row")).astype(jnp.float32),
    )
    grad_mix_gain, grad_mlp_gain = lax.psum((grad_mix_gain, grad_mlp_gain), ("dp", "col"))
    return (
        output.T,
        inputs_grad.T,
        grad_mix[:, :rec_width],
        grad_mix[:, rec_width:],
        grad_out,
        grad_gate_up[:, :ff_width],
        grad_gate_up[:, ff_width:],
        grad_down,
        grad_mix_gain,
        grad_mlp_gain,
        bias_sums[:rec_width],
        bias_sums[rec_width:],
        grad_conv_w,
        grad_conv_b,
        grad_rec_w,
        grad_in_w,
        grad_rec_b,
        grad_in_b,
        grad_decay,
    )


def solution(mesh):
    placed = (
        P("row", ("dp", "col")),
        P("row", ("dp", "col")),
        P(("dp", "row")),
        P("row", "col"),
        P("row", "col"),
        P("col", "row"),
        P("row", "col"),
        P("row", "col"),
        P("row", "col"),
        P("row"),
        P("row"),
        P("col"),
        P("col"),
        P(None, "col"),
        P("col"),
        P("col", None, None),
        P("col", None, None),
        P("col"),
        P("col"),
        P("col"),
    )
    return jax.shard_map(
        local,
        mesh=mesh,
        in_specs=placed,
        out_specs=(
            P("row", ("dp", "col")),
            P("row", ("dp", "col")),
            P("row", "col"),
            P("row", "col"),
            P("col", "row"),
            P("row", "col"),
            P("row", "col"),
            P("row", "col"),
            P("row"),
            P("row"),
            P("col"),
            P("col"),
            P(None, "col"),
            P("col"),
            P("col", None, None),
            P("col", None, None),
            P("col"),
            P("col"),
            P("col"),
        ),
        check_vma=False,
    )
```

profile of v0, /device:TPU:0, one launch (start us, length us, event | category | flops | bytes accessed | tf_op | source)
XLA Modules:
  0.0 2005.3 jit_solution(3085095908571088030)
XLA Ops:
  10.7 8.3 psum.126
  25.4 18.0 all-gather.13.cloned.1.call-done
  43.4 8.9 fusion.99
  56.3 81.5 %reduce-scatter.9.cloned.1.call-done = f32[256,2560]{1,0:T(8,128)} async-done(((f32[1024,2560]{1,0:T(8,128)}), f32[256,2560]{1,0:T(8,128)}) %reduce-scatter.9.cloned.1.call-update) | async-done | bytes 2621456 | tf_op jit(solution)/shard_map/reduce_scatter | solution.py:106
  159.4 5.0 fusion.37
  168.6 4.2 slice.465
  172.8 4.3 slice.463
  263.9 4.4 slice.462
  268.3 4.3 slice.519
  330.5 4.8 pad.549
  335.4 4.8 pad.550
  341.0 6.1 all-gather.2
  349.7 4.8 pad.565
  354.5 4.8 pad.566
  360.1 5.8 all-gather.1
  366.5 8.1 while.28
  374.7 5.0 multiply_convert_fusion.2
  379.7 27.1 %all-gather.15.cloned.1.call-done = bf16[1024,1280]{1,0:T(8,128)(2,1)} async-done(((bf16[256,1280]{1,0:T(8,128)(2,1)}), bf16[1024,1280]{1,0:T(8,128)(2,1)}) %all-gather.15.cloned.1.call-update) | async-done | bytes 2621456 | tf_op jit(solution)/shard_map/all_gather | solution.py:102
  406.8 5.0 fusion.102
  414.0 29.8 %reduce-scatter.11.cloned.1.call-done = f32[512,512]{1,0:T(8,128)} async-done(((f32[1024,512]{1,0:T(8,128)}), f32[512,512]{1,0:T(8,128)}) %reduce-scatter.11.cloned.1.call-update) | async-done | bytes 1048592 | tf_op jit(solution)/shard_map/reduce_scatter | solution.py:115
  446.8 7.6 psum.127
  457.9 8.7 all-gather.21.cloned.1.call-done
  466.6 7.6 fusion.105
  480.3 9.7 all-gather.17.cloned.1.call-done
  490.0 18.5 fusion.103
  508.6 83.2 %reduce-scatter.17.cloned.1.call-done = f32[256,3072]{1,0:T(8,128)} async-done(((f32[1024,3072]{1,0:T(8,128)}), f32[256,3072]{1,0:T(8,128)}) %reduce-scatter.17.cloned.1.call-update) | async-done | bytes 3145744 | tf_op jit(solution)/shard_map/reduce_scatter | solution.py:106
  591.9 183.2 %reduce-scatter.13.cloned.1.call-done = f32[256,6144]{1,0:T(8,128)} async-done(((f32[1024,6144]{1,0:T(8,128)}), f32[256,6144]{1,0:T(8,128)}) %reduce-scatter.13.cloned.1.call-update) | async-done | bytes 6291472 | tf_op jit(solution)/shard_map/reduce_scatter | solution.py:106
  775.1 5.9 fusion.7
  783.0 82.2 %all-gather.23.cloned.1.call-done = bf16[1024,6144]{1,0:T(8,128)(2,1)} async-done(((bf16[256,6144]{1,0:T(8,128)(2,1)}), bf16[1024,6144]{1,0:T(8,128)(2,1)}) %all-gather.23.cloned.1.call-update) | async-done | bytes 12582928 | tf_op jit(solution)/shard_map/all_gather | solution.py:102
  865.3 12.5 fusion.106
  878.0 31.7 %reduce-scatter.19.cloned.1.call-done = f32[512,512]{1,0:T(8,128)} async-done(((f32[1024,512]{1,0:T(8,128)}), f32[512,512]{1,0:T(8,128)}) %reduce-scatter.19.cloned.1.call-update) | async-done | bytes 1048592 | tf_op jit(solution)/shard_map/reduce_scatter | solution.py:115
  912.2 7.6 psum.128
  923.9 20.5 %all-gather.25.cloned.1.call-done = bf16[1024,512]{1,0:T(8,128)(2,1)} async-done(((bf16[512,512]{1,0:T(8,128)(2,1)}), bf16[1024,512]{1,0:T(8,128)(2,1)}) %all-gather.25.cloned.1.call-update) | async-done | bytes 1048592 | tf_op jit(solution)/shard_map/all_gather | solution.py:98
  944.4 5.6 fusion.107
  950.0 5.1 rev.7
  955.1 46.4 %reduce-scatter.21.cloned.1.call-done = f32[256,1280]{1,0:T(8,128)} async-done(((f32[1024,1280]{1,0:T(8,128)}), f32[256,1280]{1,0:T(8,128)}) %reduce-scatter.21.cloned.1.call-update) | async-done | bytes 1310736 | tf_op jit(solution)/shard_map/reduce_scatter | solution.py:106
  1004.2 5.2 all-gather.3
  1010.0 5.1 rev.6
  1015.1 8.1 while.29
  1024.0 4.5 broadcast_multiply_fusion
  1030.1 4.3 slice.540
  1194.2 4.9 pad.619
  1201.7 4.8 pad.620
  1206.6 4.8 pad.673
  1211.4 4.8 pad.672
  1216.2 5.0 pad.570
  1221.2 4.9 pad.623
  1226.2 6.3 multiply_reduce_fusion.4
  1250.8 4.5 add_add_fusion
  1266.5 38.1 %all-gather.27.cloned.1.call-done = bf16[1024,2560]{1,0:T(8,128)(2,1)} async-done(((bf16[256,2560]{1,0:T(8,128)(2,1)}), bf16[1024,2560]{1,0:T(8,128)(2,1)}) %all-gather.27.cloned.1.call-update) | async-done | bytes 5242896 | tf_op jit(solution)/shard_map/all_gather | solution.py:102
  1304.6 7.5 fusion.108
  1312.2 40.8 %all-gather.19.cloned.1.call-done = bf16[1024,3072]{1,0:T(8,128)(2,1)} async-done(((bf16[256,3072]{1,0:T(8,128)(2,1)}), bf16[1024,3072]{1,0:T(8,128)(2,1)}) %all-gather.19.cloned.1.call-update) | async-done | bytes 6291472 | tf_op jit(solution)/shard_map/all_gather | solution.py:102
  1353.0 7.5 fusion.104
  1360.8 8.5 fusion
  1369.3 13.5 convolution_convert_fusion
  1389.8 61.3 %all-reduce.124 = (bf16[2560]{0:T(1024)(128)(2,1)S(1)}, bf16[4,1280]{1,0:T(4,128)(2,1)S(1)}, bf16[1280]{0:T(1024)(128)(2,1)S(1)}, bf16[1280]{0:T(1024)(128)(2,1)...) all-reduce(bf16[2560]{0:T(1024)(128)(2,1)S(1)} %get-tuple-element.4, ...), channel_id=1, replica_groups=mesh['dp'=4,'row'=4,'col'=2] {'dp','row'}, use_global_device_ids=true, to_apply=%region_32.33 | all-reduce | flops 12800 | bytes 51200 | tf_op jit(solution)/shard_map/psum | solution.py:293
  1458.3 27.0 %reduce-scatter.23.cloned.1.call-done = f32[512,512]{1,0:T(8,128)} async-done(((f32[1024,512]{1,0:T(8,128)}), f32[512,512]{1,0:T(8,128)}) %reduce-scatter.23.cloned.1.call-update) | async-done | bytes 1048592 | tf_op jit(solution)/shard_map/reduce_scatter | solution.py:115
  1487.1 6.9 psum.129
  1494.0 25.9 %reduce-scatter.15.cloned.1.call-done = f32[512,512]{1,0:T(8,128)} async-done(((f32[1024,512]{1,0:T(8,128)}), f32[512,512]{1,0:T(8,128)}) %reduce-scatter.15.cloned.1.call-update) | async-done | bytes 1048592 | tf_op jit(solution)/shard_map/reduce_scatter | solution.py:115
  1528.6 21.7 %all-reduce.123 = (f32[512]{0:T(512)}, f32[512]{0:T(512)}) all-reduce(f32[512]{0:T(512)S(1)} %get-tuple-element.304, f32[512]{0:T(512)S(1)} %copy-done.138), channel_id=1, replica_groups=mesh['dp'=4,'row'=4,'col'=2] {'dp','col'}, use_global_device_ids=true, to_apply=%region_28.29 | all-reduce | flops 1024 | bytes 8192 | tf_op jit(solution)/shard_map/psum | solution.py:302
  1550.3 426.9 %all-reduce.132.cloned.1.call-done = (bf16[512,2560]{1,0:T(8,128)(2,1)}, bf16[512,6144]{1,0:T(8,128)(2,1)}, bf16[512,3072]{0,1:T(8,128)(2,1)}, bf16[1280,512]{1,0:T(8,128)(2,1)}) async-done(((bf16[512,2560]{1,0:T(8,128)(2,1)}, bf16[512,6144]{1,0:T(8,128)(2,1)}, bf16[512,3072]{0,1:T(8,128)(2,1)}, bf16[1280,512]{1,0:T(8,128)(2,1)}), (bf16[512,2560]{1,0:T(8,128)(2,1)}, bf16[512,6144]{1,0:T(8,128)(2,1)}, ...) | async-done | bytes 13369360 | tf_op jit(solution)/shard_map/psum | solution.py:278
  1977.2 9.3 fusion.70
  1986.5 5.4 copy.85
  1991.8 4.6 fusion.71
  (693 shorter events, 452.0 us)
Async XLA Ops:
  7.2 459.5 %copy-start = (bf16[512,3072]{1,0:T(8,128)(2,1)S(1)}, bf16[512,3072]{1,0:T(8,128)(2,1)}, u32[]{:S(2)}) copy-start(bf16[512,3072]{1,0:T(8,128)(2,1)} %param.32) | copy-start | bytes 9437188
  7.2 12.4 copy-start.130
  7.2 36.2 %all-gather.13.cloned.1.call-start = ((), (), s32[]{:S(2)}) async-start(), calls=%async_computation.8 | async-start | bytes 1572864 | tf_op jit(solution)/shard_map/all_gather | solution.py:98
  21.7 116.2 %reduce-scatter.9.cloned.1.call-start = ((), (), s32[]{:S(2)}) async-start(), calls=%async_computation.9 | async-start | bytes 13107200 | tf_op jit(solution)/shard_map/reduce_scatter | solution.py:106
  52.3 85.5 %copy-start.136 = (f32[1280]{0:T(1024)S(1)}, f32[1280]{0:T(1024)}, u32[]{:S(2)}) copy-start(f32[1280]{0:T(1024)} %param.35) | copy-start | bytes 15364
  52.4 354.5 %all-gather.15.cloned.1.call-start = ((), (), s32[]{:S(2)}) async-start(), calls=%async_computation.10 | async-start | bytes 3276800 | tf_op jit(solution)/shard_map/all_gather | solution.py:102
  53.1 2.5 collective-permute-start.1
  54.9 87.6 %copy-start.101 = (f32[1280]{0:T(1024)}, f32[1280]{0:T(1024)S(1)}, u32[]{:S(2)}) copy-start(f32[1280]{0:T(1024)S(1)} %get-tuple-element.311) | copy-start | bytes 15364
  54.9 87.6 %copy-start.103 = (f32[1280]{0:T(1024)}, f32[1280]{0:T(1024)S(1)}, u32[]{:S(2)}) copy-start(f32[1280]{0:T(1024)S(1)} %get-tuple-element.312) | copy-start | bytes 15364
  54.9 87.6 %copy-start.105 = (f32[1280]{0:T(1024)}, f32[1280]{0:T(1024)S(1)}, u32[]{:S(2)}) copy-start(f32[1280]{0:T(1024)S(1)} %get-tuple-element.313) | copy-start | bytes 15364
  54.9 87.6 %copy-start.107 = (f32[1280]{0:T(1024)}, f32[1280]{0:T(1024)S(1)}, u32[]{:S(2)}) copy-start(f32[1280]{0:T(1024)S(1)} %get-tuple-element.314) | copy-start | bytes 15364
  55.0 104.4 %copy-start.139 = (pred[256]{0:T(512)(128)(4,1)}, pred[256]{0:T(512)(128)(4,1)S(1)}, u32[]{:S(2)}) copy-start(pred[256]{0:T(512)(128)(4,1)S(1)} %broadcast_compare_fusion) | copy-start | bytes 772
  55.0 104.3 %copy-start.81 = (f32[1280]{0:T(1024)}, f32[1280]{0:T(1024)S(1)}, u32[]{:S(2)}) copy-start(f32[1280]{0:T(1024)S(1)} %broadcast_multiply_fusion.1) | copy-start | bytes 15364
  139.3 2.6 collective-permute-start
  204.4 44.2 %copy-start.50 = (f32[16,1280]{1,0:T(8,128)}, f32[16,1280]{1,0:T(8,128)S(1)}, u32[]{:S(2)}) copy-start(f32[16,1280]{1,0:T(8,128)S(1)} %slice.482) | copy-start | bytes 245764
  209.1 43.9 %copy-start.33 = (f32[64,1280]{1,0:T(8,128)S(1)}, f32[64,1280]{1,0:T(8,128)}, u32[]{:S(2)}) copy-start(f32[64,1280]{1,0:T(8,128)} %get-tuple-element.438) | copy-start | bytes 983044
  263.8 11.6 copy-start.121
  263.8 11.6 copy-start.122
  263.9 11.6 copy-start.123
  263.9 11.6 copy-start.124
  263.9 11.7 copy-start.113
  263.9 11.7 copy-start.112
  263.9 11.8 copy-start.87
  263.9 11.8 copy-start.100
  263.9 12.3 copy-start.127
  284.5 11.3 copy-start.28
  285.5 10.3 copy-start.30
  379.7 64.1 %reduce-scatter.11.cloned.1.call-start = ((), (), s32[]{:S(2)}) async-start(), calls=%async_computation.11 | async-start | bytes 3145728 | tf_op jit(solution)/shard_map/reduce_scatter | solution.py:115
  411.8 54.8 %all-gather.21.cloned.1.call-start = ((), (), s32[]{:S(2)}) async-start(), calls=%async_computation.16 | async-start | bytes 1572864 | tf_op jit(solution)/shard_map/all_gather | solution.py:98
  414.0 76.1 %all-gather.17.cloned.1.call-start = ((), (), s32[]{:S(2)}) async-start(), calls=%async_computation.12 | async-start | bytes 1572864 | tf_op jit(solution)/shard_map/all_gather | solution.py:98
  457.9 134.0 %reduce-scatter.17.cloned.1.call-start = ((), (), s32[]{:S(2)}) async-start(), calls=%async_computation.17 | async-start | bytes 15728640 | tf_op jit(solution)/shard_map/reduce_scatter | solution.py:106
  474.3 300.9 %reduce-scatter.13.cloned.1.call-start = ((), (), s32[]{:S(2)}) async-start(), calls=%async_computation.13 | async-start | bytes 31457280 | tf_op jit(solution)/shard_map/reduce_scatter | solution.py:106
  508.6 356.7 %all-gather.23.cloned.1.call-start = ((), (), s32[]{:S(2)}) async-start(), calls=%async_computation.18 | async-start | bytes 15728640 | tf_op jit(solution)/shard_map/all_gather | solution.py:102
  783.0 126.8 %reduce-scatter.19.cloned.1.call-start = ((), (), s32[]{:S(2)}) async-start(), calls=%async_computation.19 | async-start | bytes 3145728 | tf_op jit(solution)/shard_map/reduce_scatter | solution.py:115
  877.8 66.6 %all-gather.25.cloned.1.call-start = ((), (), s32[]{:S(2)}) async-start(), calls=%async_computation.20 | async-start | bytes 1572864 | tf_op jit(solution)/shard_map/all_gather | solution.py:98
  923.9 77.7 %reduce-scatter.21.cloned.1.call-start = ((), (), s32[]{:S(2)}) async-start(), calls=%async_computation.21 | async-start | bytes 6553600 | tf_op jit(solution)/shard_map/reduce_scatter | solution.py:106
  950.0 354.6 %all-gather.27.cloned.1.call-start = ((), (), s32[]{:S(2)}) async-start(), calls=%async_computation.22 | async-start | bytes 6553600 | tf_op jit(solution)/shard_map/all_gather | solution.py:102
  1094.5 18.1 copy-start.80
  1098.5 30.6 %copy-start.68 = (f32[8,1280]{1,0:T(8,128)S(1)}, f32[8,1280]{1,0:T(8,128)}, u32[]{:S(2)}) copy-start(f32[8,1280]{1,0:T(8,128)} %slice.488) | copy-start | bytes 122884
  1098.5 30.6 %copy-start.69 = (f32[8,1280]{1,0:T(8,128)S(1)}, f32[8,1280]{1,0:T(8,128)}, u32[]{:S(2)}) copy-start(f32[8,1280]{1,0:T(8,128)} %slice.491) | copy-start | bytes 122884
  1100.2 31.6 %copy-start.70 = (f32[8,1280]{1,0:T(8,128)S(1)}, f32[8,1280]{1,0:T(8,128)}, u32[]{:S(2)}) copy-start(f32[8,1280]{1,0:T(8,128)} %slice.487) | copy-start | bytes 122884
  1101.7 24.1 %copy-start.99 = (f32[3,1280]{1,0:T(4,128)S(1)}, f32[3,1280]{1,0:T(4,128)}, u32[]{:S(2)}) copy-start(f32[3,1280]{1,0:T(4,128)} %get-tuple-element.484) | copy-start | bytes 46084
  1103.3 38.0 %copy-start.51 = (f32[16,1280]{1,0:T(8,128)S(1)}, f32[16,1280]{1,0:T(8,128)}, u32[]{:S(2)}) copy-start(f32[16,1280]{1,0:T(8,128)} %copy-done.50) | copy-start | bytes 245764
  1103.3 38.0 %copy-start.52 = (f32[16,1280]{1,0:T(8,128)S(1)}, f32[16,1280]{1,0:T(8,128)}, u32[]{:S(2)}) copy-start(f32[16,1280]{1,0:T(8,128)} %slice.485) | copy-start | bytes 245764
  1127.1 17.5 copy-start.53
  1141.4 14.2 slice-start.6
  1141.4 14.2 slice-start.7
  1143.2 11.0 copy-start.71
  1257.4 3.2 collective-permute-start.2
  1262.0 91.0 %all-gather.19.cloned.1.call-start = ((), (), s32[]{:S(2)}) async-start(), calls=%async_computation.14 | async-start | bytes 7864320 | tf_op jit(solution)/shard_map/all_gather | solution.py:102
  1262.6 192.1 %all-reduce.130.cloned.1.call-start = ((), (), s32[]{:S(2)}) async-start(), calls=%async_computation.24 | async-start | bytes 2621440 | tf_op jit(solution)/shard_map/psum | solution.py:296
  1266.5 218.8 %reduce-scatter.23.cloned.1.call-start = ((), (), s32[]{:S(2)}) async-start(), calls=%async_computation.23 | async-start | bytes 3145728 | tf_op jit(solution)/shard_map/reduce_scatter | solution.py:115
  1312.2 207.8 %reduce-scatter.15.cloned.1.call-start = ((), (), s32[]{:S(2)}) async-start(), calls=%async_computation.15 | async-start | bytes 3145728 | tf_op jit(solution)/shard_map/reduce_scatter | solution.py:115
  1360.6 616.6 %all-reduce.132.cloned.1.call-start = ((), (), s32[]{:S(2)}) async-start(), calls=%async_computation.25 | async-start | bytes 26738688 | tf_op jit(solution)/shard_map/psum | solution.py:278
  1360.8 24.6 %slice-start.8 = ((s8[5242880]{0:T(1024)(128)(4,1)}), s8[4194304]{0:T(1024)(128)(4,1)S(1)}, s32[]{:S(2)}) async-start(s8[5242880]{0:T(1024)(128)(4,1)} %bitcast.124), calls=%async_computation.34 | async-start | bytes 8388608
  1369.3 13.5 copy-start.148
  1369.3 13.5 copy-start.151
  1369.3 16.1 slice-start.9
  1457.1 28.2 %copy-start.115 = (f32[512]{0:T(512)S(1)}, f32[512]{0:T(512)}, u32[]{:S(2)}) copy-start(f32[512]{0:T(512)} %copy-done.114) | copy-start | bytes 6148
  1457.1 28.2 %copy-start.131 = (f32[512]{0:T(512)S(1)}, f32[512]{0:T(512)}, u32[]{:S(2)}) copy-start(f32[512]{0:T(512)} %param.33) | copy-start | bytes 6148
  1457.1 36.9 %copy-start.133 = (f32[512]{0:T(512)S(1)}, f32[512]{0:T(512)}, u32[]{:S(2)}) copy-start(f32[512]{0:T(512)} %copy-done.132) | copy-start | bytes 6148
  1457.1 62.8 %copy-start.111 = (f32[512]{0:T(512)S(1)}, f32[512]{0:T(512)}, u32[]{:S(2)}) copy-start(f32[512]{0:T(512)} %copy-done.110) | copy-start | bytes 6148
  1457.1 62.8 %copy-start.118 = (f32[512]{0:T(512)S(1)}, f32[512]{0:T(512)}, u32[]{:S(2)}) copy-start(f32[512]{0:T(512)} %param.34) | copy-start | bytes 6148
  1457.1 62.8 %copy-start.135 = (f32[512]{0:T(512)S(1)}, f32[512]{0:T(512)}, u32[]{:S(2)}) copy-start(f32[512]{0:T(512)} %copy-done.134) | copy-start | bytes 6148
  (119 other events, 531.8 us)
Sparse Core Ops, SparseCore 0:
  21.8 21.6 all-gather.12
  52.5 85.2 reduce-scatter.8
  379.8 26.9 all-gather.14
  412.0 31.8 reduce-scatter.10
  445.3 21.3 all-gather.20
  468.7 21.2 all-gather.16
  492.8 99.0 reduce-scatter.16
  594.6 180.4 reduce-scatter.12
  783.1 82.1 all-gather.22
  877.9 31.8 reduce-scatter.18
  924.0 20.3 all-gather.24
  950.1 51.3 reduce-scatter.20
  1262.2 42.3 all-gather.26
  1306.6 46.3 all-gather.18
  1357.0 93.8 all-reduce.129
  1453.6 31.6 reduce-scatter.22
  1488.1 31.8 reduce-scatter.14
  1523.3 453.8 all-reduce.131
where the time goes:
time: 2020 us; the launch traced here: 2010 us
  waiting for transfers between devices  1180 us (58%)
  local copies, waits for them, and re-layouts  377 us (19%)
  other arithmetic  174 us (9%)
  blocking collectives  130 us (6%)
  matrix products  117 us (6%)
    psum x1, waiting for transfers between devices, local(): lax.psum(grad_mix.astype(jnp.bfloat16), 'dp').astype(jnp.float32)  427 us
    reduce_scatter x4, waiting for transfers between devices, row_partial(): lax.psum_scatter(lax.dot_general(whole, weight, dims, preferred_element_t...  394 us
    all_gather x4, waiting for transfers between devices, gather_mid(): return lax.all_gather(values, 'row', axis=0, tiled=True)  188 us
    pad x82, local copies, waits for them, and re-layouts, local_recurrence(): cum_keep, states = lax.associative_scan(chain, (carried, driven), axis=0)  150 us
    slice x80, local copies, waits for them, and re-layouts, local_recurrence(): cum_keep, states = lax.associative_scan(chain, (carried, driven), axis=0)  138 us
    reduce_scatter x4, waiting for transfers between devices, col_partial(): lax.psum_scatter(lax.dot_general(whole, weight, dims, preferred_element_t...  114 us
    psum x1, blocking collectives, local(): lax.psum(bias_sums.astype(jnp.bfloat16), ('dp', 'row')).astype(jnp.float32)  61.3 us
    all_gather x4, waiting for transfers between devices, gather_edge(): return lax.all_gather(values, 'col', axis=0, tiled=True)  56.9 us
  transfers between devices with their start and end apart: 21, of which 20 were waited for; matrix products, arithmetic and copies ran while one was open for 6% of the time, Pallas kernels for 0%

commit v1 on v0

--- a/solution.py
+++ b/solution.py
@@ -1,7 +1,13 @@
+import functools
+
 import jax
 import jax.numpy as jnp
 from jax import lax
+from jax.experimental import pallas as pl
+from jax.experimental.pallas import tpu as pltpu
 from jax.sharding import PartitionSpec as P
+
+MESH = pl.DeviceIdType.MESH
 
 D = 2048
 
@@ -323,6 +329,1179 @@
     )
 
 
+GATHER_ID, FORWARD_ID, BACKWARD_ID, FINISH_ID, REDUCE_ID = (0, 1, 2, 3, 4)
+BLOCK = 128
+VMEM_BYTES = 56 << 20
+
+
+def one_minus_exp(rate):
+    series = rate * (1.0 - rate * (0.5 - rate * (1.0 / 6.0 - rate * (1.0 / 24.0 - rate / 120.0))))
+    return jnp.where(rate < 0.1, series, 1.0 - jnp.exp(-rate))
+
+
+GELU_C = 0.7978845608028654
+
+
+def gelu_both(values):
+    squared = values * values
+    inner = jnp.tanh(GELU_C * values * (1.0 + 0.044715 * squared))
+    value = 0.5 * values * (1.0 + inner)
+    slope = 0.5 * (1.0 + inner) + 0.5 * values * (1.0 - inner * inner) * GELU_C * (
+        1.0 + 3.0 * 0.044715 * squared
+    )
+    return (value, slope)
+
+
+def down_rows(values, by):
+    return pltpu.roll(values, by, 0)
+
+
+def up_rows(values, by):
+    return pltpu.roll(values, values.shape[0] - by, 0)
+
+
+def scan_down(keep, add):
+    rows = keep.shape[0]
+    position = lax.broadcasted_iota(jnp.int32, keep.shape, 0)
+    step = 1
+    while step < rows:
+        if step < 8:
+            inside = position >= step
+            before_keep = jnp.where(inside, down_rows(keep, step), 1.0)
+            before_add = jnp.where(inside, down_rows(add, step), 0.0)
+            add = add + keep * before_add
+            keep = keep * before_keep
+        else:
+            add = jnp.concatenate([add[:step], add[step:] + keep[step:] * add[:-step]], axis=0)
+            keep = jnp.concatenate([keep[:step], keep[step:] * keep[:-step]], axis=0)
+        step *= 2
+    return (keep, add)
+
+
+def scan_up(keep, add):
+    rows = keep.shape[0]
+    position = lax.broadcasted_iota(jnp.int32, keep.shape, 0)
+    step = 1
+    while step < rows:
+        if step < 8:
+            inside = position < rows - step
+            after_keep = jnp.where(inside, up_rows(keep, step), 1.0)
+            after_add = jnp.where(inside, up_rows(add, step), 0.0)
+            add = add + keep * after_add
+            keep = keep * after_keep
+        else:
+            add = jnp.concatenate([add[:-step] + keep[:-step] * add[step:], add[-step:]], axis=0)
+            keep = jnp.concatenate([keep[:-step] * keep[step:], keep[-step:]], axis=0)
+        step *= 2
+    return (keep, add)
+
+
+def mixer_forward_kernel(
+    pre, masks, vec, rec_w, in_w, mixed, x_pre, conv, rec_gate, in_gate, states, tail, carry
+):
+    width = x_pre.shape[1]
+
+    @pl.when(pl.program_id(0) == 0)
+    def _():
+        tail[...] = jnp.zeros_like(tail)
+        carry[...] = jnp.zeros_like(carry)
+
+    marks = masks[...]
+    x = pre[:, :width] + vec[0:1, :]
+    x_pre[...] = x
+    longer = jnp.concatenate([tail[...], x], axis=0)
+    tail[...] = x[BLOCK - 8 :]
+    total = x * vec[2:3, :] + vec[6:7, :]
+    for tap in range(1, 4):
+        total = total + marks[:, tap : tap + 1] * down_rows(longer, tap)[8:] * vec[
+            2 + tap : 3 + tap, :
+        ]
+    low = total.astype(jnp.bfloat16)
+    conv[...] = low
+    rec = jax.nn.sigmoid(
+        jnp.dot(low, rec_w[...], preferred_element_type=jnp.float32) + vec[7:8, :]
+    )
+    inn = jax.nn.sigmoid(
+        jnp.dot(low, in_w[...], preferred_element_type=jnp.float32) + vec[8:9, :]
+    )
+    rec_gate[...] = rec
+    in_gate[...] = inn
+    log_keep = rec * vec[9:10, :]
+    fresh = marks[:, 0:1]
+    scale = jnp.where(fresh > 0.5, 1.0, jnp.sqrt(one_minus_exp(-2.0 * log_keep)))
+    driven = low.astype(jnp.float32) * inn * scale
+    keep, add = scan_down(jnp.exp(log_keep) * (1.0 - fresh), driven)
+    state = add + keep * carry[0:1, :]
+    carry[...] = jnp.broadcast_to(state[BLOCK - 1 :, :], carry.shape)
+    states[...] = state
+    y = pre[:, width:] + vec[1:2, :]
+    mixed[:, :width] = (state * gelu_both(y)[0]).astype(jnp.bfloat16)
+    mixed[:, width:] = jnp.zeros((BLOCK, mixed.shape[1] - width), jnp.bfloat16)
+
+
+def mixer_forward(pre, masks, vec, rec_w, in_w, padded):
+    tokens, width = (pre.shape[0], rec_w.shape[0])
+
+    def block(columns):
+        return pl.BlockSpec((BLOCK, columns), lambda i: (i, 0))
+
+    def whole(array):
+        return pl.BlockSpec(array.shape, lambda i: (0, 0))
+
+    def out(columns, kind):
+        return jax.ShapeDtypeStruct((tokens, columns), kind)
+
+    return pl.pallas_call(
+        mixer_forward_kernel,
+        grid=(tokens // BLOCK,),
+        in_specs=[block(2 * width), block(8), whole(vec), whole(rec_w), whole(in_w)],
+        out_specs=[block(padded)] + [block(width)] * 5,
+        out_shape=[
+            out(padded, jnp.bfloat16),
+            out(width, jnp.float32),
+            out(width, jnp.bfloat16),
+            out(width, jnp.float32),
+            out(width, jnp.float32),
+            out(width, jnp.float32),
+        ],
+        scratch_shapes=[pltpu.VMEM((8, width), jnp.float32), pltpu.VMEM((8, width), jnp.float32)],
+        compiler_params=pltpu.CompilerParams(vmem_limit_bytes=32 << 20),
+        name="mixer_forward",
+    )(pre, masks, vec, rec_w, in_w)
+
+
+def mixer_backward_kernel(
+    d_mixed,
+    pre,
+    masks,
+    vec,
+    rec_w,
+    in_w,
+    x_pre,
+    x_before,
+    conv,
+    rec_gate,
+    in_gate,
+    states,
+    state_before,
+    d_pre,
+    d_gates,
+    sums,
+    edge,
+    carry,
+):
+    width = x_pre.shape[1]
+
+    @pl.when(pl.program_id(0) == 0)
+    def _():
+        edge[...] = jnp.zeros_like(edge)
+        carry[...] = jnp.zeros_like(carry)
+        sums[...] = jnp.zeros_like(sums)
+
+    position = lax.broadcasted_iota(jnp.int32, (BLOCK, width), 0)
+    marks = masks[...]
+    fresh = marks[:, 0:1]
+    stale = 1.0 - fresh
+    gelu, slope = gelu_both(pre[:, width:] + vec[1:2, :])
+    state = states[...]
+    incoming = d_mixed[...]
+    d_y = (incoming * state * slope).astype(jnp.bfloat16)
+    rec, inn = (rec_gate[...], in_gate[...])
+    conv_vals = conv[...].astype(jnp.float32)
+    log_keep = rec * vec[9:10, :]
+    keep_rate = jnp.exp(log_keep)
+    scale = jnp.where(fresh > 0.5, 1.0, jnp.sqrt(one_minus_exp(-2.0 * log_keep)))
+    carried = keep_rate * stale
+    after = jnp.where(position == BLOCK - 1, carry[1:2, :], up_rows(carried, 1))
+    keep, add = scan_up(after, incoming * gelu)
+    adjoint = add + keep * carry[0:1, :]
+    carry[0:1, :] = adjoint[0:1]
+    carry[1:2, :] = carried[0:1]
+    earlier = jnp.where(position == 0, state_before[7:8, :], down_rows(state, 1))
+    drive = adjoint * scale
+    d_log = stale * (
+        adjoint * earlier * keep_rate
+        - adjoint * inn * conv_vals * keep_rate * keep_rate / scale
+    )
+    d_rec = (d_log * vec[9:10, :] * rec * (1.0 - rec)).astype(jnp.bfloat16)
+    d_in = (drive * conv_vals * inn * (1.0 - inn)).astype(jnp.bfloat16)
+    d_gates[:, :width] = d_rec
+    d_gates[:, width:] = d_in
+    d_conv = drive * inn
+    d_conv = d_conv + lax.dot_general(
+        d_rec, rec_w[...], CONTRACT_COLS, preferred_element_type=jnp.float32
+    )
+    d_conv = d_conv + lax.dot_general(
+        d_in, in_w[...], CONTRACT_COLS, preferred_element_type=jnp.float32
+    )
+    x = x_pre[...]
+    longer = jnp.concatenate([x_before[...], x], axis=0)
+
+    def column(values):
+        return jnp.sum(values, axis=0, keepdims=True)
+
+    d_x = d_conv * vec[2:3, :]
+    taps = [column(d_conv * x)]
+    for tap in range(1, 4):
+        part = marks[:, tap : tap + 1] * d_conv
+        taps.append(column(part * down_rows(longer, tap)[8:]))
+        beyond = jnp.concatenate([part, edge[8 * tap - 8 : 8 * tap, :]], axis=0)
+        d_x = d_x + vec[2 + tap : 3 + tap, :] * up_rows(beyond, tap)[:BLOCK]
+        edge[8 * tap - 8 : 8 * tap, :] = part[:8]
+    d_x = d_x.astype(jnp.bfloat16)
+    d_pre[:, :width] = d_x
+    d_pre[:, width:] = d_y
+    parts = (
+        [column(d_x.astype(jnp.float32)), column(d_y.astype(jnp.float32))]
+        + taps
+        + [
+            column(d_conv),
+            column(d_rec.astype(jnp.float32)),
+            column(d_in.astype(jnp.float32)),
+            column(d_log * rec) * vec[10:11, :],
+        ]
+    )
+    for place, part in enumerate(parts):
+        sums[place : place + 1, :] += part
+
+
+def mixer_backward(d_mixed, pre, masks, vec, rec_w, in_w, x_pre, conv, rec_gate, in_gate, states):
+    tokens, width = x_pre.shape
+    last = tokens // BLOCK - 1
+
+    def block(columns):
+        return pl.BlockSpec((BLOCK, columns), lambda i: (last - i, 0))
+
+    def before():
+        return pl.BlockSpec(
+            (8, width), lambda i: (jnp.maximum((last - i) * (BLOCK // 8) - 1, 0), 0)
+        )
+
+    def whole(array):
+        return pl.BlockSpec(array.shape, lambda i: (0, 0))
+
+    return pl.pallas_call(
+        mixer_backward_kernel,
+        grid=(tokens // BLOCK,),
+        in_specs=[
+            block(width),
+            block(2 * width),
+            block(8),
+            whole(vec),
+            whole(rec_w),
+            whole(in_w),
+            block(width),
+            before(),
+            block(width),
+            block(width),
+            block(width),
+            block(width),
+            before(),
+        ],
+        out_specs=[block(2 * width), block(2 * width), pl.BlockSpec((16, width), lambda i: (0, 0))],
+        out_shape=[
+            jax.ShapeDtypeStruct((tokens, 2 * width), jnp.bfloat16),
+            jax.ShapeDtypeStruct((tokens, 2 * width), jnp.bfloat16),
+            jax.ShapeDtypeStruct((16, width), jnp.float32),
+        ],
+        scratch_shapes=[pltpu.VMEM((24, width), jnp.float32), pltpu.VMEM((8, width), jnp.float32)],
+        compiler_params=pltpu.CompilerParams(vmem_limit_bytes=32 << 20),
+        name="mixer_backward",
+    )(d_mixed, pre, masks, vec, rec_w, in_w, x_pre, x_pre, conv, rec_gate, in_gate, states, states)
+
+
+def here():
+    return (lax.axis_index("dp"), lax.axis_index("row"), lax.axis_index("col"))
+
+
+def flip(index):
+    return index + 1 - 2 * (index % 2)
+
+
+def across(row):
+    return (row + 2) % 4
+
+
+def greet(peers):
+    barrier = pltpu.get_barrier_semaphore()
+    for peer in peers:
+        pl.semaphore_signal(barrier, inc=1, device_id=peer, device_id_type=MESH)
+    pl.semaphore_wait(barrier, len(peers))
+
+
+class Copies:
+    def __init__(self, send, recv):
+        self.send, self.recv, self.used, self.sent = (send, recv, 0, [])
+
+    def make(self, source, target, device):
+        place = self.used
+        self.used += 1
+        if device is None:
+            copy = pltpu.make_async_copy(source, target, self.recv.at[place])
+        else:
+            copy = pltpu.make_async_remote_copy(
+                src_ref=source,
+                dst_ref=target,
+                send_sem=self.send.at[place],
+                recv_sem=self.recv.at[place],
+                device_id=device,
+                device_id_type=MESH,
+            )
+            self.sent.append(copy)
+        return copy
+
+    def go(self, source, target, device):
+        copy = self.make(source, target, device)
+        copy.start()
+        return copy
+
+    def finish(self):
+        for copy in self.sent:
+            copy.wait_send()
+
+
+def arrived(copy):
+    copy.wait_recv()
+
+
+def spread(copies, own, place, halves):
+    z, r, c = here()
+    twin, side, top = ((z, flip(r), c), (z, across(r), c), (z, r, 1 - c))
+    to_side = copies.go(own, place(r, c), side)
+    to_top = copies.go(own, place(r, c), top)
+    to_twin = copies.go(own, place(r, c), twin)
+    arrived(to_side)
+    from_side = place(across(r), c)
+    on_top = copies.go(halves(from_side, 0), halves(from_side, 0), top)
+    late = [to_twin, copies.go(from_side, from_side, twin)]
+    arrived(to_top)
+    from_top = place(r, 1 - c)
+    on_side = copies.go(halves(from_top, 1), halves(from_top, 1), side)
+    late.append(copies.go(from_top, from_top, twin))
+    far = place(across(r), 1 - c)
+    for half, copy in enumerate((on_top, on_side)):
+        arrived(copy)
+        late.append(copies.go(halves(far, half), halves(far, half), twin))
+    return late
+
+
+def gather_kernel(*refs):
+    x_in, c_in, s_in, mix_in, out_in, *mlp_in = refs[:8]
+    x_all, c_all, s_all, mix_all, out_all, *mlp_all = refs[8:16]
+    send, recv = refs[16:]
+    z, r, c = here()
+    twin, side, cross, top, pair = (
+        (z, flip(r), c),
+        (z, across(r), c),
+        (z, flip(across(r)), c),
+        (z, r, 1 - c),
+        (flip(z), r, c),
+    )
+    greet((twin, side, cross, top, pair))
+    copies = Copies(send, recv)
+    rows, columns = x_in.shape
+    depth, width = (mlp_in[0].shape[0], mlp_in[0].shape[1] // 4)
+    rec = out_in.shape[0] // 4
+
+    def part(start, size, step):
+        return pl.ds(pl.multiple_of(start * step, step), size)
+
+    matrices = [
+        (lambda to: mix_in.at[to], lambda of: mix_all.at[part(of, depth, depth), :], depth),
+        (
+            lambda to: out_in.at[part(to, rec, rec), :],
+            lambda of: out_all.at[:, part(of, columns, columns)],
+            rec,
+        ),
+    ] + [
+        (
+            lambda to, source=source: source.at[:, part(to, width, width)],
+            lambda of, target=target: target.at[part(of, depth, depth), :],
+            depth,
+        )
+        for source, target in zip(mlp_in, mlp_all)
+    ]
+
+    def half(ref, which, size):
+        return ref.at[part(which, size // 2, size // 2), :]
+
+    def block(ref):
+        return lambda row, col: ref.at[part(col, rows, rows), part(row, columns, columns)]
+
+    def halves(ref, which):
+        return ref.at[pl.ds(which * (rows // 2), rows // 2), :]
+
+    locals_ = [
+        copies.go(x_in, block(x_all)(r, c), None),
+        copies.go(c_in, block(c_all)(r, c), None),
+        copies.go(s_in, s_all.at[r], None),
+    ]
+    late = []
+    for peer in (twin, side, cross):
+        late.append(copies.go(s_in, s_all.at[r], peer))
+    mine = z % 2
+    first = []
+    for source, target, size in matrices:
+        locals_.append(copies.go(source(r), target(r), None))
+        late.append(copies.go(source(flip(r)), target(r), twin))
+        for peer in (side, cross):
+            first.append(
+                copies.make(half(source(peer[1]), mine, size), half(target(r), mine, size), peer)
+            )
+    for copy in first[:4]:
+        copy.start()
+    late.extend(spread(copies, x_in, block(x_all), halves))
+    for copy in first[4:]:
+        copy.start()
+    for place, (source, target, size) in enumerate(matrices):
+        for which, peer in enumerate((side, cross)):
+            arrived(first[2 * place + which])
+            piece = half(target(peer[1]), mine, size)
+            late.append(copies.go(piece, piece, pair))
+    late.extend(spread(copies, c_in, block(c_all), halves))
+    for copy in late:
+        arrived(copy)
+    for copy in locals_:
+        copy.wait()
+    copies.finish()
+
+
+def gather(x_in, c_in, s_in, mix_in, out_in, mlp_in):
+    rows, columns = x_in.shape
+    depth, width = (mlp_in[0].shape[0], mlp_in[0].shape[1] // 4)
+
+    def shape(*dims, kind=jnp.bfloat16):
+        return jax.ShapeDtypeStruct(dims, kind)
+
+    outs = [
+        shape(2 * rows, 4 * columns),
+        shape(2 * rows, 4 * columns),
+        shape(4, *s_in.shape, kind=s_in.dtype),
+        shape(4 * depth, mix_in.shape[2]),
+        shape(out_in.shape[0] // 4, 4 * columns),
+    ] + [shape(4 * depth, width)] * 3
+    return pl.pallas_call(
+        gather_kernel,
+        in_specs=[pl.BlockSpec(memory_space=pl.ANY)] * 8,
+        out_specs=[pl.BlockSpec(memory_space=pl.ANY)] * 8,
+        out_shape=outs,
+        scratch_shapes=[pltpu.SemaphoreType.DMA((64,)), pltpu.SemaphoreType.DMA((64,))],
+        compiler_params=pltpu.CompilerParams(collective_id=GATHER_ID, has_side_effects=True),
+        name="gather",
+    )(x_in, c_in, s_in, mix_in, out_in, *mlp_in)
+
+
+STRIP = 16
+
+
+def strips(count, body):
+    def run(index, nothing):
+        body(pl.multiple_of(index * STRIP, STRIP))
+        return nothing
+
+    lax.fori_loop(0, count // STRIP, run, 0)
+
+
+def token_shard(row, col):
+    return col * 4 + row
+
+
+def reduce_shards(copies, parts, twin_in, sums, side_in, top_in, hop_in):
+    z, r, c = here()
+    twin, side, top = ((z, flip(r), c), (z, across(r), c), (z, r, 1 - c))
+    size = side_in.shape[0]
+    half = size // 2
+
+    def shard(row, col):
+        return pl.multiple_of(token_shard(row, col) * size, size)
+
+    spots = [(across(r), 1 - c), (across(r), c), (r, 1 - c), (r, c)]
+    from_twin = [
+        copies.go(parts.at[pl.ds(shard(flip(row), col), size), :], twin_in.at[place], twin)
+        for place, (row, col) in enumerate(spots)
+    ]
+
+    def add_twin(place):
+        arrived(from_twin[place])
+        start = shard(*spots[place])
+
+        def body(at):
+            total = parts[pl.ds(start + at, STRIP), :].astype(jnp.float32) + twin_in[
+                place, pl.ds(at, STRIP), :
+            ].astype(jnp.float32)
+            sums[place, pl.ds(at, STRIP), :] = total.astype(jnp.bfloat16)
+
+        strips(size, body)
+
+    def add_hop(place, which, hop):
+        def body(at):
+            rows = pl.ds(which * half + at, STRIP)
+            total = sums[place, rows, :].astype(jnp.float32) + hop_in[
+                hop, pl.ds(at, STRIP), :
+            ].astype(jnp.float32)
+            sums[place, rows, :] = total.astype(jnp.bfloat16)
+
+        strips(half, body)
+
+    def rows_of(ref, which):
+        return ref.at[pl.ds(which * half, half), :]
+
+    add_twin(0)
+    hop_side = copies.go(rows_of(sums.at[0], 0), hop_in.at[0], side)
+    hop_top = copies.go(rows_of(sums.at[0], 1), hop_in.at[1], top)
+    add_twin(1)
+    waits = [copies.go(rows_of(sums.at[1], 0), rows_of(side_in, 0), side)]
+    add_twin(2)
+    waits.append(copies.go(rows_of(sums.at[2], 1), rows_of(top_in, 1), top))
+    add_twin(3)
+    arrived(hop_top)
+    add_hop(1, 1, 1)
+    waits.append(copies.go(rows_of(sums.at[1], 1), rows_of(side_in, 1), side))
+    arrived(hop_side)
+    add_hop(2, 0, 0)
+    waits.append(copies.go(rows_of(sums.at[2], 0), rows_of(top_in, 0), top))
+    for copy in waits:
+        arrived(copy)
+
+    def total(at):
+        rows = pl.ds(at, STRIP)
+        return (
+            sums[3, rows, :].astype(jnp.float32)
+            + side_in[rows, :].astype(jnp.float32)
+            + top_in[rows, :].astype(jnp.float32)
+        )
+
+    return total
+
+
+def reduce_scratch(size, width):
+    return [
+        pltpu.VMEM((4, size, width), jnp.bfloat16),
+        pltpu.VMEM((4, size, width), jnp.bfloat16),
+        pltpu.VMEM((size, width), jnp.bfloat16),
+        pltpu.VMEM((size, width), jnp.bfloat16),
+        pltpu.VMEM((2, size // 2, width), jnp.bfloat16),
+    ]
+
+
+def near():
+    z, r, c = here()
+    return ((z, flip(r), c), (z, across(r), c), (z, r, 1 - c))
+
+
+def spread_rows(copies, mine, full):
+    z, r, c = here()
+    size = mine.shape[0]
+    half = size // 2
+
+    def place(row, col):
+        return full.at[pl.ds(pl.multiple_of(token_shard(row, col) * size, size), size), :]
+
+    local = copies.go(mine, place(r, c), None)
+    late = spread(
+        copies, mine, place, lambda ref, which: ref.at[pl.ds(which * half, half), :]
+    )
+    for copy in late:
+        arrived(copy)
+    local.wait()
+
+
+def forward_kernel(parts, resid, gain, full, resid_mid, *scratch):
+    *buffers, mine, send, recv = scratch
+    greet(near())
+    copies = Copies(send, recv)
+    total = reduce_shards(copies, parts, *buffers)
+
+    def body(at):
+        rows = pl.ds(at, STRIP)
+        values = resid[rows, :].astype(jnp.float32) + total(at)
+        resid_mid[rows, :] = values
+        scale = lax.rsqrt(jnp.mean(values * values, axis=1, keepdims=True) + EPS)
+        mine[rows, :] = (values * scale * gain[...]).astype(jnp.bfloat16)
+
+    strips(mine.shape[0], body)
+    spread_rows(copies, mine, full)
+    copies.finish()
+
+
+def norm_pull(values, gain, incoming):
+    scale = lax.rsqrt(jnp.mean(values * values, axis=1, keepdims=True) + EPS)
+    scaled = gain * incoming
+    dots = jnp.sum(scaled * values, axis=1, keepdims=True)
+    grad = scale * scaled - values * (scale * scale * scale * dots / values.shape[1])
+    return (grad, jnp.sum(incoming * values * scale, axis=0, keepdims=True))
+
+
+def backward_kernel(parts, resid_mid, cot, gain, full, d_resid, gain_grad, *scratch):
+    *buffers, mine, send, recv = scratch
+    greet(near())
+    copies = Copies(send, recv)
+    total = reduce_shards(copies, parts, *buffers)
+    gain_grad[...] = jnp.zeros_like(gain_grad)
+
+    def body(at):
+        rows = pl.ds(at, STRIP)
+        grad, part = norm_pull(resid_mid[rows, :], gain[...], total(at))
+        grad = grad + cot[rows, :].astype(jnp.float32)
+        gain_grad[...] += part
+        d_resid[rows, :] = grad
+        mine[rows, :] = grad.astype(jnp.bfloat16)
+
+    strips(mine.shape[0], body)
+    spread_rows(copies, mine, full)
+    copies.finish()
+
+
+def finish_kernel(
+    parts, out_parts, resid, resid_mid, d_resid, gain, grad, output, gain_grad, *scratch
+):
+    buffers, more = (scratch[:5], scratch[5:10])
+    mine, mine_out, send, recv = scratch[10:]
+    z, r, c = here()
+    twin, side, top = near()
+    cross = (z, flip(across(r)), c)
+    greet((twin, side, top, cross))
+    copies = Copies(send, recv)
+    columns = grad.shape[1]
+    size = mine.shape[0]
+    gain_grad[...] = jnp.zeros_like(gain_grad)
+
+    def hand_out(source, target):
+        def piece(row):
+            return source.at[:, pl.ds(pl.multiple_of(row * columns, columns), columns)]
+
+        spot = target.at[pl.ds(pl.multiple_of(r * size, size), size), :]
+        waits = [copies.go(piece(peer[1]), spot, peer) for peer in (side, cross, twin)]
+        return (copies.go(piece(r), spot, None), waits)
+
+    total = reduce_shards(copies, out_parts, *more)
+
+    def body_out(at):
+        rows = pl.ds(at, STRIP)
+        mine_out[rows, :] = (resid_mid[rows, :] + total(at)).astype(jnp.bfloat16)
+
+    strips(size, body_out)
+    moves = [hand_out(mine_out, output)]
+    total_back = reduce_shards(copies, parts, *buffers)
+
+    def body(at):
+        rows = pl.ds(at, STRIP)
+        values, part = norm_pull(resid[rows, :].astype(jnp.float32), gain[...], total_back(at))
+        gain_grad[...] += part
+        mine[rows, :] = (d_resid[rows, :] + values).astype(jnp.bfloat16)
+
+    strips(size, body)
+    moves.append(hand_out(mine, grad))
+    for local, waits in moves:
+        for copy in waits:
+            arrived(copy)
+        local.wait()
+    copies.finish()
+
+
+def vmem_call(kernel, name, place, arrays, outs, spaces, scratch, count):
+    return pl.pallas_call(
+        kernel,
+        in_specs=[pl.BlockSpec(memory_space=pltpu.VMEM)] * len(arrays),
+        out_specs=[pl.BlockSpec(memory_space=space) for space in spaces],
+        out_shape=outs,
+        scratch_shapes=scratch
+        + [pltpu.SemaphoreType.DMA((count,)), pltpu.SemaphoreType.DMA((count,))],
+        compiler_params=pltpu.CompilerParams(
+            collective_id=place, has_side_effects=True, vmem_limit_bytes=VMEM_BYTES
+        ),
+        name=name,
+    )(*arrays)
+
+
+CHUNK = 16
+
+
+def reduce_kernel(count, *refs):
+    sources, (out, own, left, right, move_send, move_recv) = (refs[:count], refs[count : count + 6])
+    end_send, low_recv, high_recv, out_recv, mid_send, first_send, last_send, local, on_send = refs[
+        count + 6 :
+    ]
+    z, r, c = here()
+    twin, side, cross = ((z, flip(r), c), (z, across(r), c), (z, flip(across(r)), c))
+    is_end = (z == 0) | (z == 3)
+    near_z = jnp.where(z == 0, 1, 2)
+    end_z = jnp.where(z == 1, 0, 3)
+    barrier = pltpu.get_barrier_semaphore()
+    for peer in (twin, side, cross):
+        pl.semaphore_signal(barrier, inc=1, device_id=peer, device_id_type=MESH)
+
+    @pl.when(is_end)
+    def _():
+        pl.semaphore_signal(barrier, inc=1, device_id=(near_z, r, c), device_id_type=MESH)
+        pl.semaphore_wait(barrier, 4)
+
+    @pl.when(jnp.logical_not(is_end))
+    def _():
+        pl.semaphore_signal(barrier, inc=1, device_id=(end_z, r, c), device_id_type=MESH)
+        pl.semaphore_signal(barrier, inc=1, device_id=(3 - z, r, c), device_id_type=MESH)
+        pl.semaphore_wait(barrier, 5)
+
+    rows = own.shape[1]
+    half = rows // 2
+    per = half // CHUNK
+    chunks = 4 * per
+    moves = []
+    for which, peer in ((1, twin), (2, side), (3, cross)):
+        start = 0
+        group = []
+        for place, source in enumerate(sources):
+            width = source.shape[1]
+            copy = pltpu.make_async_remote_copy(
+                src_ref=source.at[pl.ds(pl.multiple_of(peer[1] * rows, rows), rows), :],
+                dst_ref=own.at[r, :, pl.ds(start, width)],
+                send_sem=move_send.at[which, place],
+                recv_sem=move_recv.at[which, place],
+                device_id=peer,
+                device_id_type=MESH,
+            )
+            copy.start()
+            group.append(copy)
+            start += width
+        moves.append(group)
+    start = 0
+    group = []
+    for place, source in enumerate(sources):
+        width = source.shape[1]
+        copy = pltpu.make_async_copy(
+            source.at[pl.ds(pl.multiple_of(r * rows, rows), rows), :],
+            own.at[r, :, pl.ds(start, width)],
+            move_recv.at[0, place],
+        )
+        copy.start()
+        group.append(copy)
+        start += width
+
+    def piece_arrived(index):
+        @pl.when(index == 0)
+        def _():
+            for copy in group:
+                copy.wait()
+
+        for which in (1, 2, 3):
+
+            @pl.when(index == which * per)
+            def _():
+                for copy in moves[which - 1]:
+                    copy.wait_recv()
+
+    def slot(index):
+        step = index // per
+        return (r // 2 + step // 2) % 2 * 2 + (r % 2 + step % 2) % 2
+
+    def strip_of(index):
+        return pl.multiple_of(index % per * CHUNK, CHUNK)
+
+    def own_at(index, part):
+        return own.at[slot(index), pl.ds(part * half + strip_of(index), CHUNK), :]
+
+    def out_at(index, part):
+        return out.at[slot(index), pl.ds(part * half + strip_of(index), CHUNK), :]
+
+    def remote(source, target, sender, receiver, device):
+        return pltpu.make_async_remote_copy(
+            src_ref=source,
+            dst_ref=target,
+            send_sem=sender,
+            recv_sem=receiver,
+            device_id=device,
+            device_id_type=MESH,
+        )
+
+    def loop(count, body):
+        def run(index, nothing):
+            body(index)
+            return nothing
+
+        lax.fori_loop(0, count, run, 0)
+
+    @pl.when(is_end)
+    def _():
+        low = z // 3
+        peer = (near_z, r, c)
+
+        def send_low(index):
+            return remote(
+                own_at(index, low),
+                left.at[index],
+                end_send.at[0, index],
+                low_recv.at[index],
+                peer,
+            )
+
+        def send_high(index):
+            return remote(
+                own_at(index, 1 - low),
+                right.at[1, index],
+                end_send.at[1, index],
+                high_recv.at[1, index],
+                peer,
+            )
+
+        def begin(index):
+            piece_arrived(index)
+            send_low(index).start()
+            send_high(index).start()
+
+        def end(index):
+            send_low(index).wait_send()
+            send_high(index).wait_send()
+            for part in (0, 1):
+                spot = out_at(index, part)
+                remote(
+                    spot, spot, end_send.at[0, index], out_recv.at[part, index], peer
+                ).wait_recv()
+
+        loop(chunks, begin)
+        loop(chunks, end)
+
+    @pl.when(jnp.logical_not(is_end))
+    def _():
+        low = z - 1
+        other, outer = ((3 - z, r, c), (end_z, r, c))
+
+        def to_other(index):
+            return remote(
+                own_at(index, 1 - low),
+                right.at[0, index],
+                mid_send.at[index],
+                high_recv.at[0, index],
+                other,
+            )
+
+        def from_outer(index):
+            return remote(
+                own_at(index, 1 - low),
+                right.at[1, index],
+                mid_send.at[index],
+                high_recv.at[1, index],
+                outer,
+            )
+
+        def from_low(index):
+            return remote(
+                own_at(index, low), left.at[index], mid_send.at[index], low_recv.at[index], outer
+            )
+
+        def final(index):
+            mine = own_at(index, low)
+            spot = out_at(index, low)
+            return (
+                pltpu.make_async_copy(mine, spot, local.at[index]),
+                remote(mine, spot, first_send.at[index], out_recv.at[low, index], outer),
+                remote(mine, spot, last_send.at[index], out_recv.at[low, index], other),
+            )
+
+        def onward(index):
+            spot = out_at(index, 1 - low)
+            return remote(spot, spot, on_send.at[index], out_recv.at[1 - low, index], outer)
+
+        def rows_at(index, part):
+            return pl.ds(pl.multiple_of(part * half + strip_of(index), CHUNK), CHUNK)
+
+        def step(index):
+            @pl.when(index < chunks)
+            def _():
+                piece_arrived(index)
+                from_outer(index).wait_recv()
+                spot = rows_at(index, 1 - low)
+                total = own[slot(index), spot, :].astype(jnp.float32) + right[1, index].astype(
+                    jnp.float32
+                )
+                own[slot(index), spot, :] = total.astype(jnp.bfloat16)
+                to_other(index).start()
+
+            @pl.when((index >= 2) & (index < chunks + 2))
+            def _():
+                back = index - 2
+                from_low(back).wait_recv()
+                to_other(back).wait_recv()
+                spot = rows_at(back, low)
+                total = (
+                    own[slot(back), spot, :].astype(jnp.float32)
+                    + left[back].astype(jnp.float32)
+                    + right[0, back].astype(jnp.float32)
+                )
+                own[slot(back), spot, :] = total.astype(jnp.bfloat16)
+                for copy in final(back):
+                    copy.start()
+
+            @pl.when(index >= 4)
+            def _():
+                back = index - 4
+                onward(back).wait_recv()
+                onward(back).start()
+
+        def end(index):
+            to_other(index).wait_send()
+            here_copy, first, last = final(index)
+            here_copy.wait()
+            first.wait_send()
+            last.wait_send()
+            onward(index).wait_send()
+
+        loop(chunks + 4, step)
+        loop(chunks, end)
+
+    for moved in moves:
+        for copy in moved:
+            copy.wait_send()
+
+
+def reduce_grads(sources):
+    rows = sources[0].shape[0] // 4
+    width = sum(source.shape[1] for source in sources)
+    chunks = 4 * (rows // 2 // CHUNK)
+    dma = pltpu.SemaphoreType.DMA
+    count = len(sources)
+    return pl.pallas_call(
+        functools.partial(reduce_kernel, count),
+        in_specs=[pl.BlockSpec(memory_space=pl.ANY)] * count,
+        out_specs=pl.BlockSpec(memory_space=pl.ANY),
+        out_shape=jax.ShapeDtypeStruct((4, rows, width), jnp.bfloat16),
+        scratch_shapes=[
+            pltpu.VMEM((4, rows, width), jnp.bfloat16),
+            pltpu.VMEM((chunks, CHUNK, width), jnp.bfloat16),
+            pltpu.VMEM((2, chunks, CHUNK, width), jnp.bfloat16),
+            dma((4, count)),
+            dma((4, count)),
+            dma((2, chunks)),
+            dma((chunks,)),
+            dma((2, chunks)),
+            dma((2, chunks)),
+            dma((chunks,)),
+            dma((chunks,)),
+            dma((chunks,)),
+            dma((chunks,)),
+            dma((chunks,)),
+        ],
+        compiler_params=pltpu.CompilerParams(
+            collective_id=REDUCE_ID, has_side_effects=True, vmem_limit_bytes=VMEM_BYTES
+        ),
+        name="reduce_grads",
+    )(*sources)
+
+
+def dot(left, right, dims, kind=jnp.float32):
+    return lax.dot_general(left, right, dims, preferred_element_type=jnp.float32).astype(kind)
+
+
+def local_plane(
+    inputs,
+    cotangent,
+    starts,
+    x_proj,
+    y_proj,
+    out_proj,
+    gate_proj,
+    up_proj,
+    down_proj,
+    mix_gain,
+    mlp_gain,
+    x_bias,
+    y_bias,
+    conv_w,
+    conv_b,
+    rec_gate_w,
+    in_gate_w,
+    rec_gate_b,
+    in_gate_b,
+    decay_param,
+):
+    z, r, c = here()
+    depth = x_proj.shape[0]
+    rec = x_proj.shape[1] // 4
+    width = gate_proj.shape[1] // 4
+    heads, head = (rec_gate_w.shape[0] // 4, rec_gate_w.shape[1])
+    padded = (rec + 127) // 128 * 128
+    low = jnp.bfloat16
+
+    def mine(array, size, axis=0):
+        return lax.dynamic_slice_in_dim(array, r * size, size, axis)
+
+    mix_in = jnp.concatenate(
+        [x_proj.reshape(depth, 4, rec), y_proj.reshape(depth, 4, rec)], axis=2
+    ).transpose(1, 0, 2)
+    flags = jnp.pad(starts.astype(jnp.float32).reshape(-1, 128), ((0, 6), (0, 0)))
+    x_all, c_all, s_all, mix_w, out_w, gate_w, up_w, down_w = gather(
+        inputs.T, cotangent.T, flags, mix_in, out_proj, (gate_proj, up_proj, down_proj)
+    )
+    tokens, model = x_all.shape
+    gain_mix, gain_mlp = (
+        lax.all_gather(mix_gain, "row", axis=0, tiled=True)[None, :],
+        lax.all_gather(mlp_gain, "row", axis=0, tiled=True)[None, :],
+    )
+    fresh = s_all[:, :2, :].reshape(tokens)
+    stale = 1.0 - fresh
+    stale_one = jnp.concatenate([jnp.zeros((1,), jnp.float32), stale[:-1]])
+    stale_two = jnp.concatenate([jnp.zeros((2,), jnp.float32), stale[:-2]])
+    nothing = jnp.zeros_like(fresh)
+    masks = jnp.stack(
+        [fresh, stale, stale * stale_one, stale * stale_one * stale_two] + [nothing] * 4, axis=1
+    )
+    vectors = jnp.concatenate(
+        [
+            x_bias[None],
+            y_bias[None],
+            conv_w,
+            conv_b[None],
+            rec_gate_b[None],
+            in_gate_b[None],
+            -GATE_C * jax.nn.softplus(decay_param)[None],
+            -GATE_C * jax.nn.sigmoid(decay_param)[None],
+            jnp.zeros((5, x_bias.shape[0]), jnp.float32),
+        ],
+        axis=0,
+    )
+    vec = mine(vectors, rec, 1)
+
+    def diagonal(blocks):
+        blocks = mine(blocks, heads)
+        rows = [jnp.pad(blocks[i], ((0, 0), (i * head, rec - (i + 1) * head))) for i in range(heads)]
+        return jnp.concatenate(rows, axis=0)
+
+    rec_w, in_w = (diagonal(rec_gate_w), diagonal(in_gate_w))
+    values = x_all.astype(jnp.float32)
+    scale = lax.rsqrt(jnp.mean(values * values, axis=1, keepdims=True) + EPS)
+    normed_mix = (values * scale * gain_mix).astype(low)
+    pre = dot(normed_mix, mix_w, CONTRACT_PLAIN)
+    mixed, x_pre, conv, rec_gate, in_gate, states = mixer_forward(
+        pre, masks, vec, rec_w, in_w, padded
+    )
+    size = tokens // 8
+    shard = token_shard(r, c) * size
+    resid = lax.dynamic_slice_in_dim(x_all, shard, size, 0)
+    cot = lax.dynamic_slice_in_dim(c_all, shard, size, 0)
+    full = jax.ShapeDtypeStruct((tokens, model), low)
+    part = jax.ShapeDtypeStruct((size, model), jnp.float32)
+    line = jax.ShapeDtypeStruct((1, model), jnp.float32)
+    piece = pltpu.VMEM((size, model), low)
+    block = jax.ShapeDtypeStruct((inputs.shape[1], inputs.shape[0]), low)
+    normed_mlp, resid_mid = vmem_call(
+        forward_kernel,
+        "forward_norm",
+        FORWARD_ID,
+        (dot(mixed[:, :rec], out_w, CONTRACT_PLAIN, low), resid, gain_mlp),
+        [full, part],
+        [pl.ANY, pltpu.VMEM],
+        reduce_scratch(size, model) + [piece],
+        24,
+    )
+    gate = dot(normed_mlp, gate_w, CONTRACT_PLAIN)
+    up = dot(normed_mlp, up_w, CONTRACT_PLAIN)
+    d_activ = dot(c_all, down_w, CONTRACT_PLAIN)
+    gelu, slope = gelu_both(gate)
+    activ = (gelu * up).astype(low)
+    d_gate = (d_activ * up * slope).astype(low)
+    d_up = (d_activ * gelu).astype(low)
+    d_normed = lax.dot_general(
+        d_gate, gate_w, CONTRACT_COLS, preferred_element_type=jnp.float32
+    ) + lax.dot_general(d_up, up_w, CONTRACT_COLS, preferred_element_type=jnp.float32)
+    d_branch, d_resid, grad_mlp_gain = vmem_call(
+        backward_kernel,
+        "backward_norm",
+        BACKWARD_ID,
+        (d_normed.astype(low), resid_mid, cot, gain_mlp),
+        [full, part, line],
+        [pl.ANY, pltpu.VMEM, pltpu.VMEM],
+        reduce_scratch(size, model) + [piece],
+        24,
+    )
+    d_mixed = dot(d_branch, out_w, CONTRACT_COLS)
+    d_pre, d_gates, sums = mixer_backward(
+        d_mixed, pre, masks, vec, rec_w, in_w, x_pre, conv, rec_gate, in_gate, states
+    )
+    grad_in, output, grad_mix_gain = vmem_call(
+        finish_kernel,
+        "finish_norm",
+        FINISH_ID,
+        (
+            dot(d_pre, mix_w, CONTRACT_COLS, low),
+            dot(activ, down_w, CONTRACT_COLS, low),
+            resid,
+            resid_mid,
+            d_resid,
+            gain_mix,
+        ),
+        [block, block, line],
+        [pltpu.VMEM] * 3,
+        reduce_scratch(size, model) * 2 + [piece, piece],
+        40,
+    )
+    grads = reduce_grads(
+        (
+            dot(normed_mlp, d_gate, CONTRACT_ROWS, low),
+            dot(normed_mlp, d_up, CONTRACT_ROWS, low),
+            dot(c_all, activ, CONTRACT_ROWS, low),
+            dot(normed_mix, d_pre, CONTRACT_ROWS, low),
+            dot(d_branch, mixed, CONTRACT_ROWS, low),
+        )
+    )
+    gate_grads = dot(conv, d_gates, CONTRACT_ROWS, low)
+
+    def spots(array, axis):
+        shape = list(array.shape)
+        length = shape[axis]
+        shape[axis] = 4 * length
+        return lax.dynamic_update_slice_in_dim(
+            jnp.zeros(shape, array.dtype), array, r * length, axis
+        )
+
+    def blocks(array):
+        return jnp.stack(
+            [array[i * head : (i + 1) * head, i * head : (i + 1) * head] for i in range(heads)]
+        )
+
+    grad_rec_w = spots(blocks(gate_grads[:, :rec]), 0)
+    grad_in_w = spots(blocks(gate_grads[:, rec:]), 0)
+    vec_sums, grad_rec_w, grad_in_w = (
+        item.astype(jnp.float32)
+        for item in lax.psum((spots(sums.astype(low), 1), grad_rec_w, grad_in_w), ("dp", "row"))
+    )
+    gains = lax.psum(
+        jnp.concatenate([grad_mix_gain, grad_mlp_gain], axis=0), ("dp", "row", "col")
+    )
+    gains = lax.dynamic_slice_in_dim(gains, r * depth, depth, 1)
+
+    def columns(first, length):
+        piece = grads[:, :, first : first + length].astype(jnp.float32)
+        return piece.transpose(1, 0, 2).reshape(depth, 4 * length)
+
+    after = 3 * width
+    grad_out = grads[:, :, after + 2 * rec : after + 3 * rec].astype(jnp.float32)
+    grad_out = grad_out.transpose(0, 2, 1).reshape(4 * rec, depth)
+    return (
+        output.T,
+        grad_in.astype(jnp.float32).T,
+        columns(after, rec),
+        columns(after + rec, rec),
+        grad_out,
+        columns(0, width),
+        columns(width, width),
+        columns(2 * width, width),
+        gains[0],
+        gains[1],
+        vec_sums[0],
+        vec_sums[1],
+        vec_sums[2:6],
+        vec_sums[6],
+        grad_rec_w,
+        grad_in_w,
+        vec_sums[7],
+        vec_sums[8],
+        vec_sums[9],
+    )
+
+
+def fits(mesh):
+    return mesh.shape["dp"] == 4 and mesh.shape["row"] == 4 and mesh.shape["col"] == 2
+
+
 def solution(mesh):
     placed = (
         P("row", ("dp", "col")),
@@ -347,7 +1526,7 @@
         P("col"),
     )
     return jax.shard_map(
-        local,
+        local_plane if fits(mesh) else local,
         mesh=mesh,
         in_specs=placed,
         out_specs=(

time: 2020 us -> 968 us (0.48)
  waiting for transfers between devices: 1180 us -> 0.02 us
  Pallas kernels: 0 us -> 650 us
  local copies, waits for them, and re-layouts: 377 us -> 75.6 us
  other arithmetic: 174 us -> 28.5 us
  matrix products: 117 us -> 82.4 us
  blocking collectives: 130 us -> 108 us
    pallas_call x0 -> x7, Pallas kernels: none -> 650 us  [the longest x1 335 us: reduce_grads(): pl.pallas_call(functools.partial(reduce_kernel, count), in_specs=[pl.Bloc...]
    reduce_scatter x8 -> x0, waiting for transfers between devices: 509 us -> none  [the longest x4 394 us: row_partial(): lax.psum_scatter(lax.dot_general(whole, weight, dims, preferred_element_t...]
    psum x2 -> x1, waiting for transfers between devices: 427 us -> 0.01 us  [local_plane(): lax.psum((spots(sums.astype(low), 1), grad_rec_w, grad_in_w), ('dp', 'row'))]
    all_gather x8 -> x0, waiting for transfers between devices: 245 us -> none  [the longest x4 188 us: gather_mid(): return lax.all_gather(values, 'row', axis=0, tiled=True)]
    slice x88 -> x3, local copies, waits for them, and re-layouts: 155 us -> 1.95 us  [the longest x1 0.68 us: local_plane(): vec_sums[9]]
    pad x82 -> x1, local copies, waits for them, and re-layouts: 150 us -> 0.6 us  [local_plane(): jnp.pad(starts.astype(jnp.float32).reshape(-1, 128), ((0, 6), (0, 0)))]
    add x29 -> x0, other arithmetic: 36.4 us -> none  [the longest x14 18 us: chain(): return (earlier[0] * later[0], later[0] * earlier[1] + later[1])]
    dot_general x18 -> x16, matrix products: 117 us -> 82.4 us  [the longest x14 74 us: dot(): lax.dot_general(left, right, dims, preferred_element_type=jnp.float32)]
  transfers between devices with their start and end apart: 21 -> 1, of which waited for: 20 -> 0; matrix products, arithmetic and copies ran while one was open for 6% -> 12% of each run, Pallas kernels for 0% -> 41%
where the time goes in v1:
time: 968 us; the launch traced here: 960 us
  Pallas kernels  650 us (67%)
  blocking collectives  108 us (11%)
  matrix products  82.4 us (9%)
  local copies, waits for them, and re-layouts  75.6 us (8%)
  other arithmetic  28.5 us (3%)
  between operations  15.2 us (2%)
    pallas_call x1, Pallas kernels, reduce_grads(): pl.pallas_call(functools.partial(reduce_kernel, count), in_specs=[pl.Bloc...  335 us
    pallas_call x3, Pallas kernels, vmem_call(): pl.pallas_call(kernel, in_specs=[pl.BlockSpec(memory_space=pltpu.VMEM)] *...  158 us
    pallas_call x1, Pallas kernels, gather(): pl.pallas_call(gather_kernel, in_specs=[pl.BlockSpec(memory_space=pl.ANY)...  138 us
    dot_general x14, matrix products, dot(): lax.dot_general(left, right, dims, preferred_element_type=jnp.float32)  74 us
    psum x1, blocking collectives, local_plane(): lax.psum((spots(sums.astype(low), 1), grad_rec_w, grad_in_w), ('dp', 'row'))  60 us
    unnamed x95, local copies, waits for them, and re-layouts  38.1 us
    psum x1, blocking collectives, local_plane(): lax.psum(jnp.concatenate([grad_mix_gain, grad_mlp_gain], axis=0), ('dp',...  37.4 us
    reshape x5, local copies, waits for them, and re-layouts, columns(): return piece.transpose(1, 0, 2).reshape(depth, 4 * length)  24.2 us
  transfers between devices with their start and end apart: 1, of which 0 were waited for; matrix products, arithmetic and copies ran while one was open for 12% of the time, Pallas kernels for 41%

profile of v1, /device:TPU:0, one launch (start us, length us, event | category | flops | bytes accessed | tf_op | source)
XLA Modules:
  0.0 960.2 jit_solution(11725196905240605461)
XLA Ops:
  7.2 1.6 copy.70
  8.9 0.9 copy.72
  9.7 2.4 copy.71
  12.2 1.8 copy.73
  14.0 2.0 copy.68
  16.1 2.0 copy.69
  18.1 2.5 maximum_bitcast_fusion.refs_3_
  20.6 0.6 pad.19.refs_2_
  21.2 138.5 %gather.1 = (bf16[1024,2048]{1,0:T(8,128)(2,1)}, bf16[1024,2048]{1,0:T(8,128)(2,1)}, f32[4,8,128]{2,1,0:T(8,128)}, bf16[2048,640]{1,0:T(8,128)(2,1)}, bf16[320,2...) custom-call(bf16[512,512]{1,0:T(8,128)(2,1)} %bitcast.95, ...), custom_call_target="tpu_custom_call" | custom-call | tf_op jit(solution)/shard_map/gather/pallas_call | solution.py:783
  159.8 0.8 broadcast_subtract_fusion
  160.9 3.1 fusion
  164.0 5.2 all-gather
  169.4 1.9 constant_dynamic-slice_fusion.2.resid
  171.3 5.6 all-gather.1
  176.9 1.9 constant_dynamic-slice_fusion.1.cot
  178.8 8.2 fusion.16
  187.0 1.0 dynamic-slice_bitcast_fusion.1
  188.4 6.7 fusion.4.pre
  195.1 7.0 mixer_forward.1
  202.2 4.4 convolution_convert_fusion.1.parts
  206.6 49.9 %forward_norm.1 = (bf16[1024,2048]{1,0:T(8,128)(2,1)}, f32[128,2048]{1,0:T(8,128)}) custom-call(bf16[1024,2048]{1,0:T(8,128)(2,1)} %convolution_convert_fusion.1.parts, bf16[128,2048]{1,0:T(8,128)(2,1)} %constant_dynamic-slice_fusion.2.resid, f32[1,2048]{1,0:T(1,128)} %bitcast.102), custom_call_target="tpu_custom_call" | custom-call | tf_op jit(solution)/shard_map/forward_norm/pallas_call | solution.py:1003
  256.5 6.3 fusion.17
  262.9 6.2 multiply_convert_fusion
  269.1 3.4 fusion.18
  272.5 5.0 add_convert_fusion.parts
  277.5 49.3 %backward_norm.1 = (bf16[1024,2048]{1,0:T(8,128)(2,1)}, f32[128,2048]{1,0:T(8,128)}, f32[1,2048]{1,0:T(1,128)}) custom-call(bf16[1024,2048]{1,0:T(8,128)(2,1)} %add_convert_fusion.parts, f32[128,2048]{1,0:T(8,128)} %get-tuple-element.54.resid_mid, bf16[128,2048]{1,0:T(8,128)(2,1)} %constant_dynamic-slice_fusion.1.cot, f32[1,2048]{1,0:T(1,128)} %bitcast.103), custom_call_target="tpu_custom_call" | custom-call | tf_op jit(solution)/shard_map/backward_norm/pallas_call | solution.py:1003
  326.9 5.1 fusion.19.d_mixed
  332.0 11.5 %mixer_backward.1 = (bf16[1024,640]{1,0:T(8,128)(2,1)S(1)}, bf16[1024,640]{1,0:T(8,128)(2,1)S(1)}, f32[16,320]{1,0:T(8,128)S(1)}) custom-call(f32[1024,320]{1,0:T(8,128)S(1)} %fusion.19.d_mixed, f32[1024,640]{1,0:T(8,128)S(1)} %fusion.4.pre, f32[1024,8]{1,0:T(8,128)S(1)} %copy.74.masks, f32[16,320]{1,0:T(8,128)S(1)} %constant_dynamic-slice_fusion.3.vec, ...), custom_call_target="tpu_custom_call" | custom-call | tf_op jit(solution)/shard_map/mixer_backward/pallas_call | solution.py:583
  343.5 0.7 convolution_convert_fusion.8
  344.6 0.7 copy-done.13
  345.3 0.2 copy-done.12
  345.5 5.9 convolution_convert_fusion.7.refs_4_
  351.4 5.0 convolution_convert_fusion.parts
  356.5 5.3 convolution_convert_fusion.6.refs_3_
  361.8 4.9 convolution_convert_fusion.4.refs_1_
  366.8 5.2 convolution_convert_fusion.5.refs_0_
  371.9 5.1 convolution_convert_fusion.2.out_parts
  377.0 5.0 convolution_convert_fusion.3.refs_2_
  382.0 335.0 %reduce_grads.1 = bf16[4,512,3328]{2,1,0:T(8,128)(2,1)} custom-call(bf16[2048,768]{1,0:T(8,128)(2,1)} %convolution_convert_fusion.5.refs_0_, bf16[2048,768]{1,0:T(8,128)(2,1)} %convolution_convert_fusion.4.refs_1_, bf16[2048,768]{1,0:T(8,128)(2,1)} %convolution_convert_fusion.3.refs_2_, bf16[2048,640]{1,0:T(8,128)(2,1)} %convolution_convert_fusion.6.refs_3_, ...), custom_call_target="tpu_custom_call" | custom-call | tf_op jit(solution)/shard_map/reduce_grads/pallas_call | solution.py:1262
  717.1 9.2 convert_bitcast_fusion
  726.2 6.8 convert_bitcast_fusion.3
  733.0 0.3 dynamic_update_slice.9
  733.3 60.0 %psum.29 = bf16[16,1280]{1,0:T(8,128)(2,1)S(1)} all-reduce(bf16[16,1280]{1,0:T(8,128)(2,1)S(1)} %dynamic_update_slice.9), channel_id=1, replica_groups=mesh['dp'=4,'row'=4,'col'=2] {'dp','row'}, use_global_device_ids=true, to_apply=%region_2.3 | all-reduce | flops 20480 | bytes 81920 | tf_op jit(solution)/shard_map/psum | solution.py:1464
  793.4 0.6 slice.116
  794.0 6.6 copy.80
  800.6 6.6 copy.87
  807.2 6.6 copy.81
  813.8 6.6 copy.88
  820.3 6.6 copy.82
  826.9 6.7 copy.89
  833.6 2.2 copy.77
  835.8 3.4 copy.85
  839.2 2.2 copy.78
  841.4 3.4 copy.86
  844.8 2.2 copy.79
  847.0 59.1 %finish_norm.1 = (bf16[512,512]{1,0:T(8,128)(2,1)}, bf16[512,512]{1,0:T(8,128)(2,1)}, f32[1,2048]{1,0:T(1,128)}) custom-call(bf16[1024,2048]{1,0:T(8,128)(2,1)} %convolution_convert_fusion.parts, bf16[1024,2048]{1,0:T(8,128)(2,1)} %convolution_convert_fusion.2.out_parts, bf16[128,2048]{1,0:T(8,128)(2,1)} %constant_dynamic-slice_fusion.2.resid, ...), custom_call_target="tpu_custom_call" | custom-call | tf_op jit(solution)/shard_map/finish_norm/pallas_call | solution.py:1003
  906.1 1.2 convert_bitcast_fusion.6
  907.3 1.3 copy.84
  908.7 1.0 copy.83
  909.7 37.4 %psum.28 = f32[2,2048]{1,0:T(2,128)S(1)} all-reduce(f32[2,2048]{1,0:T(2,128)S(1)} %pad_maximum_fusion), channel_id=1, replica_groups=mesh['dp'=4,'row'=4,'col'=2] {'dp','row','col'}, use_global_device_ids=true, to_apply=%region_1.2 | all-reduce | flops 4096 | bytes 32768 | tf_op jit(solution)/shard_map/psum | solution.py:1466
  947.1 0.7 fusion.15
  947.7 0.7 slice_reduce_fusion
  948.4 2.3 convert_element_type.93
  950.7 2.3 convert_element_type.94
  (114 shorter events, 1.4 us)
Async XLA Ops:
  7.2 941.2 %all-reduce.9.cloned.1.call-start = ((), (), s32[]{:S(2)}) async-start(), calls=%async_computation | async-start | bytes 2621440 | tf_op jit(solution)/shard_map/psum | solution.py:1464
  12.2 6.0 copy-start.28
  159.7 4.4 copy-start.26
  159.7 9.5 copy-start.18
  159.7 9.6 copy-start.19
  159.7 9.6 copy-start.20
  159.7 9.6 copy-start.21
  159.7 9.6 copy-start.22
  159.7 9.6 %copy-start.23 = (f32[1280]{0:T(1024)S(1)}, f32[1280]{0:T(1024)}, u32[]{:S(2)}) copy-start(f32[1280]{0:T(1024)} %param.38) | copy-start | bytes 15364
  159.8 11.5 %copy-start.27 = (f32[512]{0:T(512)S(1)}, f32[512]{0:T(512)}, u32[]{:S(2)}) copy-start(f32[512]{0:T(512)} %param.30) | copy-start | bytes 6148
  169.2 187.3 %copy-start.16 = (f32[4,1,512]{2,1,0:T(1,128)}, f32[4,1,512]{2,1,0:T(1,128)S(1)}, u32[]{:S(2)}) copy-start(f32[4,1,512]{2,1,0:T(1,128)S(1)} %all-gather) | copy-start | bytes 24580
  178.8 9.5 copy-start.17
  195.1 7.1 copy-start.35
  202.2 4.4 copy-start
  202.2 4.4 copy-start.2
  202.2 4.4 copy-start.6
  256.5 6.3 copy-start.29
  256.5 6.3 copy-start.32
  256.5 6.3 copy-start.38
  262.8 6.2 copy-start.33
  269.1 3.5 copy-start.36
  269.1 3.5 copy-start.39
  326.8 5.1 copy-start.1
  326.9 5.1 copy-start.3
  343.4 1.1 copy-start.4
  343.4 2.1 copy-start.7
  344.4 0.8 copy-start.13
  344.5 0.9 copy-start.12
  345.5 5.9 copy-start.5
  345.5 5.9 copy-start.34
  351.4 5.1 copy-start.11
  356.5 5.3 copy-start.30
  356.5 5.3 copy-start.40
  361.8 4.9 copy-start.37
  366.8 5.2 copy-start.31
  366.8 5.2 copy-start.41
  371.9 5.1 copy-start.15
  826.9 6.7 copy-start.10
  835.8 3.4 copy-start.9
  841.4 3.4 copy-start.8
  906.1 2.6 copy-start.14
  906.1 3.6 copy-start.24
  906.1 3.6 copy-start.25
Sparse Core Ops, SparseCore 0:
  345.6 95.7 all-reduce.8

commit v2 on v1

--- a/solution.py
+++ b/solution.py
@@ -396,17 +396,10 @@
     return (keep, add)
 
 
-def mixer_forward_kernel(
-    pre, masks, vec, rec_w, in_w, mixed, x_pre, conv, rec_gate, in_gate, states, tail, carry
+def mixer_forward_step(
+    pre, marks, vec, rec_w, in_w, mixed, x_pre, conv, rec_gate, in_gate, states, tail, carry
 ):
     width = x_pre.shape[1]
-
-    @pl.when(pl.program_id(0) == 0)
-    def _():
-        tail[...] = jnp.zeros_like(tail)
-        carry[...] = jnp.zeros_like(carry)
-
-    marks = masks[...]
     x = pre[:, :width] + vec[0:1, :]
     x_pre[...] = x
     longer = jnp.concatenate([tail[...], x], axis=0)
@@ -437,37 +430,6 @@
     y = pre[:, width:] + vec[1:2, :]
     mixed[:, :width] = (state * gelu_both(y)[0]).astype(jnp.bfloat16)
     mixed[:, width:] = jnp.zeros((BLOCK, mixed.shape[1] - width), jnp.bfloat16)
-
-
-def mixer_forward(pre, masks, vec, rec_w, in_w, padded):
-    tokens, width = (pre.shape[0], rec_w.shape[0])
-
-    def block(columns):
-        return pl.BlockSpec((BLOCK, columns), lambda i: (i, 0))
-
-    def whole(array):
-        return pl.BlockSpec(array.shape, lambda i: (0, 0))
-
-    def out(columns, kind):
-        return jax.ShapeDtypeStruct((tokens, columns), kind)
-
-    return pl.pallas_call(
-        mixer_forward_kernel,
-        grid=(tokens // BLOCK,),
-        in_specs=[block(2 * width), block(8), whole(vec), whole(rec_w), whole(in_w)],
-        out_specs=[block(padded)] + [block(width)] * 5,
-        out_shape=[
-            out(padded, jnp.bfloat16),
-            out(width, jnp.float32),
-            out(width, jnp.bfloat16),
-            out(width, jnp.float32),
-            out(width, jnp.float32),
-            out(width, jnp.float32),
-        ],
-        scratch_shapes=[pltpu.VMEM((8, width), jnp.float32), pltpu.VMEM((8, width), jnp.float32)],
-        compiler_params=pltpu.CompilerParams(vmem_limit_bytes=32 << 20),
-        name="mixer_forward",
-    )(pre, masks, vec, rec_w, in_w)
 
 
 def mixer_backward_kernel(
@@ -664,31 +626,103 @@
     copy.wait_recv()
 
 
-def spread(copies, own, place, halves):
+def spread(copies, own, place, halves, between=lambda: None):
     z, r, c = here()
     twin, side, top = ((z, flip(r), c), (z, across(r), c), (z, r, 1 - c))
     to_side = copies.go(own, place(r, c), side)
     to_top = copies.go(own, place(r, c), top)
     to_twin = copies.go(own, place(r, c), twin)
+    between()
     arrived(to_side)
     from_side = place(across(r), c)
     on_top = copies.go(halves(from_side, 0), halves(from_side, 0), top)
     late = [to_twin, copies.go(from_side, from_side, twin)]
+    between()
     arrived(to_top)
     from_top = place(r, 1 - c)
     on_side = copies.go(halves(from_top, 1), halves(from_top, 1), side)
     late.append(copies.go(from_top, from_top, twin))
     far = place(across(r), 1 - c)
+    between()
     for half, copy in enumerate((on_top, on_side)):
         arrived(copy)
         late.append(copies.go(halves(far, half), halves(far, half), twin))
     return late
 
 
-def gather_kernel(*refs):
-    x_in, c_in, s_in, mix_in, out_in, *mlp_in = refs[:8]
-    x_all, c_all, s_all, mix_all, out_all, *mlp_all = refs[8:16]
-    send, recv = refs[16:]
+def part(start, size, step):
+    return pl.ds(pl.multiple_of(start * step, step), size)
+
+
+class Moves:
+    def __init__(self, copies, matrices, cuts):
+        self.copies = copies
+        z, r, c = here()
+        self.mine = z % 2
+        self.sides = ((z, across(r), c), (z, flip(across(r)), c))
+        self.pair = (flip(z), r, c)
+        self.locals, self.late, self.flying = ([], [], [])
+        self.groups = [(matrix, cut) for matrix in matrices for cut in range(cuts)]
+        self.cuts, self.begun = (cuts, 0)
+        for source, target, size in matrices:
+            self.locals.append(copies.go(source(r), target(r), None))
+            self.late.append(copies.go(source(flip(r)), target(r), (z, flip(r), c)))
+
+    def piece(self, ref, size, cut):
+        length = size // 2 // self.cuts
+        return ref.at[part(self.mine * self.cuts + cut, length, length), :]
+
+    def step(self):
+        if len(self.flying) == 2 or self.begun == len(self.groups):
+            if self.flying:
+                (source, target, size), cut, group = self.flying.pop(0)
+                for peer, copy in zip(self.sides, group):
+                    arrived(copy)
+                    piece = self.piece(target(peer[1]), size, cut)
+                    self.late.append(self.copies.go(piece, piece, self.pair))
+        if self.begun < len(self.groups):
+            (source, target, size), cut = self.groups[self.begun]
+            self.begun += 1
+            group = [
+                self.copies.go(
+                    self.piece(source(peer[1]), size, cut),
+                    self.piece(target(here()[1]), size, cut),
+                    peer,
+                )
+                for peer in self.sides
+            ]
+            self.flying.append(((source, target, size), cut, group))
+
+    def finish(self):
+        while self.flying:
+            self.step()
+        for copy in self.late:
+            arrived(copy)
+        for copy in self.locals:
+            copy.wait()
+
+
+def block_of(ref, rows, columns):
+    return lambda row, col: ref.at[part(col, rows, rows), part(row, columns, columns)]
+
+
+def halves_of(rows):
+    return lambda ref, which: ref.at[pl.ds(which * (rows // 2), rows // 2), :]
+
+
+def mlp_matrices(sources, targets):
+    depth, width = (sources[0].shape[0], sources[0].shape[1] // 4)
+    return [
+        (
+            lambda to, source=source: source.at[:, part(to, width, width)],
+            lambda of, target=target: target.at[part(of, depth, depth), :],
+            depth,
+        )
+        for source, target in zip(sources, targets)
+    ]
+
+
+def gather_kernel(x_in, s_in, g_in, mix_in, out_in, x_all, s_all, g_all, mix_all, out_all, send, recv):
     z, r, c = here()
     twin, side, cross, top, pair = (
         (z, flip(r), c),
@@ -700,12 +734,7 @@
     greet((twin, side, cross, top, pair))
     copies = Copies(send, recv)
     rows, columns = x_in.shape
-    depth, width = (mlp_in[0].shape[0], mlp_in[0].shape[1] // 4)
-    rec = out_in.shape[0] // 4
-
-    def part(start, size, step):
-        return pl.ds(pl.multiple_of(start * step, step), size)
-
+    depth, rec = (mix_in.shape[1], out_in.shape[0] // 4)
     matrices = [
         (lambda to: mix_in.at[to], lambda of: mix_all.at[part(of, depth, depth), :], depth),
         (
@@ -713,52 +742,23 @@
             lambda of: out_all.at[:, part(of, columns, columns)],
             rec,
         ),
-    ] + [
-        (
-            lambda to, source=source: source.at[:, part(to, width, width)],
-            lambda of, target=target: target.at[part(of, depth, depth), :],
-            depth,
-        )
-        for source, target in zip(mlp_in, mlp_all)
     ]
-
-    def half(ref, which, size):
-        return ref.at[part(which, size // 2, size // 2), :]
-
-    def block(ref):
-        return lambda row, col: ref.at[part(col, rows, rows), part(row, columns, columns)]
-
-    def halves(ref, which):
-        return ref.at[pl.ds(which * (rows // 2), rows // 2), :]
-
+    small = g_all.at[:, part(r, depth, depth)]
     locals_ = [
-        copies.go(x_in, block(x_all)(r, c), None),
-        copies.go(c_in, block(c_all)(r, c), None),
+        copies.go(x_in, block_of(x_all, rows, columns)(r, c), None),
         copies.go(s_in, s_all.at[r], None),
+        copies.go(g_in, small, None),
     ]
     late = []
     for peer in (twin, side, cross):
         late.append(copies.go(s_in, s_all.at[r], peer))
-    mine = z % 2
-    first = []
-    for source, target, size in matrices:
-        locals_.append(copies.go(source(r), target(r), None))
-        late.append(copies.go(source(flip(r)), target(r), twin))
-        for peer in (side, cross):
-            first.append(
-                copies.make(half(source(peer[1]), mine, size), half(target(r), mine, size), peer)
-            )
-    for copy in first[:4]:
-        copy.start()
-    late.extend(spread(copies, x_in, block(x_all), halves))
-    for copy in first[4:]:
-        copy.start()
-    for place, (source, target, size) in enumerate(matrices):
-        for which, peer in enumerate((side, cross)):
-            arrived(first[2 * place + which])
-            piece = half(target(peer[1]), mine, size)
-            late.append(copies.go(piece, piece, pair))
-    late.extend(spread(copies, c_in, block(c_all), halves))
+        late.append(copies.go(g_in, small, peer))
+    moves = Moves(copies, matrices, 2)
+    moves.step()
+    late.extend(
+        spread(copies, x_in, block_of(x_all, rows, columns), halves_of(rows), moves.step)
+    )
+    moves.finish()
     for copy in late:
         arrived(copy)
     for copy in locals_:
@@ -766,29 +766,29 @@
     copies.finish()
 
 
-def gather(x_in, c_in, s_in, mix_in, out_in, mlp_in):
+def gather(x_in, s_in, g_in, mix_in, out_in):
     rows, columns = x_in.shape
-    depth, width = (mlp_in[0].shape[0], mlp_in[0].shape[1] // 4)
+    depth = mix_in.shape[1]
 
     def shape(*dims, kind=jnp.bfloat16):
         return jax.ShapeDtypeStruct(dims, kind)
 
     outs = [
         shape(2 * rows, 4 * columns),
-        shape(2 * rows, 4 * columns),
         shape(4, *s_in.shape, kind=s_in.dtype),
+        shape(g_in.shape[0], 4 * depth, kind=g_in.dtype),
         shape(4 * depth, mix_in.shape[2]),
         shape(out_in.shape[0] // 4, 4 * columns),
-    ] + [shape(4 * depth, width)] * 3
+    ]
     return pl.pallas_call(
         gather_kernel,
-        in_specs=[pl.BlockSpec(memory_space=pl.ANY)] * 8,
-        out_specs=[pl.BlockSpec(memory_space=pl.ANY)] * 8,
+        in_specs=[pl.BlockSpec(memory_space=pl.ANY)] * 5,
+        out_specs=[pl.BlockSpec(memory_space=pl.ANY)] * 5,
         out_shape=outs,
-        scratch_shapes=[pltpu.SemaphoreType.DMA((64,)), pltpu.SemaphoreType.DMA((64,))],
+        scratch_shapes=[pltpu.SemaphoreType.DMA((48,)), pltpu.SemaphoreType.DMA((48,))],
         compiler_params=pltpu.CompilerParams(collective_id=GATHER_ID, has_side_effects=True),
         name="gather",
-    )(x_in, c_in, s_in, mix_in, out_in, *mlp_in)
+    )(x_in, s_in, g_in, mix_in, out_in)
 
 
 STRIP = 16
@@ -806,7 +806,7 @@
     return col * 4 + row
 
 
-def reduce_shards(copies, parts, twin_in, sums, side_in, top_in, hop_in):
+def reduce_shards(copies, parts, twin_in, sums, side_in, top_in, hop_in, between=lambda: None):
     z, r, c = here()
     twin, side, top = ((z, flip(r), c), (z, across(r), c), (z, r, 1 - c))
     size = side_in.shape[0]
@@ -854,12 +854,14 @@
     add_twin(2)
     waits.append(copies.go(rows_of(sums.at[2], 1), rows_of(top_in, 1), top))
     add_twin(3)
+    between()
     arrived(hop_top)
     add_hop(1, 1, 1)
     waits.append(copies.go(rows_of(sums.at[1], 1), rows_of(side_in, 1), side))
     arrived(hop_side)
     add_hop(2, 0, 0)
     waits.append(copies.go(rows_of(sums.at[2], 0), rows_of(top_in, 0), top))
+    between()
     for copy in waits:
         arrived(copy)
 
@@ -889,7 +891,7 @@
     return ((z, flip(r), c), (z, across(r), c), (z, r, 1 - c))
 
 
-def spread_rows(copies, mine, full):
+def spread_rows(copies, mine, full, between=lambda: None):
     z, r, c = here()
     size = mine.shape[0]
     half = size // 2
@@ -899,28 +901,94 @@
 
     local = copies.go(mine, place(r, c), None)
     late = spread(
-        copies, mine, place, lambda ref, which: ref.at[pl.ds(which * half, half), :]
+        copies, mine, place, lambda ref, which: ref.at[pl.ds(which * half, half), :], between
     )
     for copy in late:
         arrived(copy)
     local.wait()
 
 
-def forward_kernel(parts, resid, gain, full, resid_mid, *scratch):
-    *buffers, mine, send, recv = scratch
-    greet(near())
+def forward_kernel(x_all, masks, vec, rec_w, in_w, mix_w, out_w, gain_mix, gain, c_in, *refs):
+    mlp_in, outs, scratch = (refs[:3], refs[3:17], refs[17:])
+    full, resid_mid, c_all = outs[:3]
+    mlp_all, kept_out = (outs[3:6], outs[6:])
+    kept, (tail, carry, parts), (*buffers, mine, kept_sem, send, recv) = (
+        scratch[:8],
+        scratch[8:11],
+        scratch[11:],
+    )
+    normed, pre, mixed, *saved = kept
+    z, r, c = here()
+    greet((*near(), (z, flip(across(r)), c), (flip(z), r, c)))
     copies = Copies(send, recv)
-    total = reduce_shards(copies, parts, *buffers)
+    rows, columns = c_in.shape
+    moves = Moves(copies, mlp_matrices(mlp_in, mlp_all), 2)
+    moves.step()
+    moves.step()
+    tail[...] = jnp.zeros_like(tail)
+    carry[...] = jnp.zeros_like(carry)
+
+    def block(index, nothing):
+        start = pl.multiple_of(index * BLOCK, BLOCK)
+        rows = pl.ds(start, BLOCK)
+
+        def norm(at):
+            strip = pl.ds(start + at, STRIP)
+            values = x_all[strip, :].astype(jnp.float32)
+            scale = lax.rsqrt(jnp.mean(values * values, axis=1, keepdims=True) + EPS)
+            normed[strip, :] = (values * scale * gain_mix[...]).astype(jnp.bfloat16)
+
+        strips(BLOCK, norm)
+        pre[rows, :] = jnp.dot(normed[rows, :], mix_w[...], preferred_element_type=jnp.float32)
+        mixer_forward_step(
+            pre.at[rows, :],
+            masks[rows, :],
+            vec,
+            rec_w,
+            in_w,
+            mixed.at[rows, :],
+            *[ref.at[rows, :] for ref in saved],
+            tail,
+            carry,
+        )
+        width = rec_w.shape[0]
+        parts[rows, :] = jnp.dot(
+            mixed[rows, :width], out_w[...], preferred_element_type=jnp.float32
+        ).astype(jnp.bfloat16)
+        return nothing
+
+    lax.fori_loop(0, 3, block, 0)
+    moves.step()
+    lax.fori_loop(3, 6, block, 0)
+    moves.step()
+    lax.fori_loop(6, x_all.shape[0] // BLOCK, block, 0)
+    keeping = [
+        pltpu.make_async_copy(source, target, kept_sem.at[place])
+        for place, (source, target) in enumerate(zip(kept, kept_out))
+    ]
+    for copy in keeping:
+        copy.start()
+    total = reduce_shards(copies, parts, *buffers, between=moves.step)
+    size = mine.shape[0]
+    start = pl.multiple_of(token_shard(r, c) * size, size)
 
     def body(at):
         rows = pl.ds(at, STRIP)
-        values = resid[rows, :].astype(jnp.float32) + total(at)
+        values = x_all[pl.ds(start + at, STRIP), :].astype(jnp.float32) + total(at)
         resid_mid[rows, :] = values
         scale = lax.rsqrt(jnp.mean(values * values, axis=1, keepdims=True) + EPS)
         mine[rows, :] = (values * scale * gain[...]).astype(jnp.bfloat16)
 
-    strips(mine.shape[0], body)
-    spread_rows(copies, mine, full)
+    strips(size, body)
+    spread_rows(copies, mine, full, moves.step)
+    local = copies.go(c_in, block_of(c_all, rows, columns)(r, c), None)
+    late = spread(copies, c_in, block_of(c_all, rows, columns), halves_of(rows), moves.step)
+    for copy in late:
+        arrived(copy)
+    local.wait()
+    moves.finish()
+    for copy in keeping:
+        copy.wait()
     copies.finish()
 
 
@@ -999,10 +1067,11 @@
     copies.finish()
 
 
-def vmem_call(kernel, name, place, arrays, outs, spaces, scratch, count):
+def vmem_call(kernel, name, place, arrays, outs, spaces, scratch, count, loose=()):
     return pl.pallas_call(
         kernel,
-        in_specs=[pl.BlockSpec(memory_space=pltpu.VMEM)] * len(arrays),
+        in_specs=[pl.BlockSpec(memory_space=pltpu.VMEM)] * len(arrays)
+        + [pl.BlockSpec(memory_space=pl.ANY)] * len(loose),
         out_specs=[pl.BlockSpec(memory_space=space) for space in spaces],
         out_shape=outs,
         scratch_shapes=scratch
@@ -1011,54 +1080,85 @@
             collective_id=place, has_side_effects=True, vmem_limit_bytes=VMEM_BYTES
         ),
         name=name,
-    )(*arrays)
+    )(*arrays, *loose)
 
 
 CHUNK = 16
 
 
 def reduce_kernel(count, *refs):
-    sources, (out, own, left, right, move_send, move_recv) = (refs[:count], refs[count : count + 6])
+    sources, (gates, vec, gain) = (refs[:count], refs[count : count + 3])
+    out, out_gates, out_vec, out_gain = refs[count + 3 : count + 7]
+    own, left, right, vec_z, gain_z, vec_sum, gain_sum, vec_in, gain_in = refs[count + 7 : count + 16]
+    move_send, move_recv, gate_sem, small_send, small_recv = refs[count + 16 : count + 21]
     end_send, low_recv, high_recv, out_recv, mid_send, first_send, last_send, local, on_send = refs[
-        count + 6 :
+        count + 21 :
     ]
     z, r, c = here()
     twin, side, cross = ((z, flip(r), c), (z, across(r), c), (z, flip(across(r)), c))
     is_end = (z == 0) | (z == 3)
     near_z = jnp.where(z == 0, 1, 2)
     end_z = jnp.where(z == 1, 0, 3)
-    barrier = pltpu.get_barrier_semaphore()
-    for peer in (twin, side, cross):
-        pl.semaphore_signal(barrier, inc=1, device_id=peer, device_id_type=MESH)
-
-    @pl.when(is_end)
-    def _():
-        pl.semaphore_signal(barrier, inc=1, device_id=(near_z, r, c), device_id_type=MESH)
-        pl.semaphore_wait(barrier, 4)
-
-    @pl.when(jnp.logical_not(is_end))
-    def _():
-        pl.semaphore_signal(barrier, inc=1, device_id=(end_z, r, c), device_id_type=MESH)
-        pl.semaphore_signal(barrier, inc=1, device_id=(3 - z, r, c), device_id_type=MESH)
-        pl.semaphore_wait(barrier, 5)
+    lines = [((z + step) % 4, r, c) for step in (1, 2, 3)]
+    plane = [
+        (z, (r + step) % 4, (c + turn) % 2) for turn in (0, 1) for step in range(4) if step or turn
+    ]
+    greet(lines + plane)
 
     rows = own.shape[1]
     half = rows // 2
     per = half // CHUNK
-    chunks = 4 * per
+    chunks = 4 * per + 1
+
+    def remote(source, target, sender, receiver, device):
+        return pltpu.make_async_remote_copy(
+            src_ref=source,
+            dst_ref=target,
+            send_sem=sender,
+            recv_sem=receiver,
+            device_id=device,
+            device_id_type=MESH,
+        )
+
+    small = [
+        [
+            remote(
+                source,
+                target.at[3 - step],
+                small_send.at[kind, step - 1],
+                small_recv.at[kind, 3 - step],
+                lines[step - 1],
+            )
+            for step in (1, 2, 3)
+        ]
+        for kind, (source, target) in enumerate(((vec, vec_z), (gain, gain_z)))
+    ]
+    for kind in small:
+        for copy in kind:
+            copy.start()
+    packed = []
+    width = gates.shape[1]
+    for tile in range(gates.shape[0] // CHUNK):
+        which, place = (tile // 5, tile % 5)
+        copy = pltpu.make_async_copy(
+            gates.at[pl.ds(tile * CHUNK, CHUNK), :],
+            own.at[4, pl.ds(which * half, CHUNK), pl.ds(place * width, width)],
+            gate_sem.at[tile],
+        )
+        copy.start()
+        packed.append(copy)
     moves = []
     for which, peer in ((1, twin), (2, side), (3, cross)):
         start = 0
         group = []
         for place, source in enumerate(sources):
             width = source.shape[1]
-            copy = pltpu.make_async_remote_copy(
-                src_ref=source.at[pl.ds(pl.multiple_of(peer[1] * rows, rows), rows), :],
-                dst_ref=own.at[r, :, pl.ds(start, width)],
-                send_sem=move_send.at[which, place],
-                recv_sem=move_recv.at[which, place],
-                device_id=peer,
-                device_id_type=MESH,
+            copy = remote(
+                source.at[pl.ds(pl.multiple_of(peer[1] * rows, rows), rows), :],
+                own.at[r, :, pl.ds(start, width)],
+                move_send.at[which, place],
+                move_recv.at[which, place],
+                peer,
             )
             copy.start()
             group.append(copy)
@@ -1076,26 +1176,29 @@
         copy.start()
         group.append(copy)
         start += width
+    for copy in packed:
+        copy.wait()
 
     def piece_arrived(index):
-        @pl.when(index == 0)
+        @pl.when(index == 1)
         def _():
             for copy in group:
                 copy.wait()
 
         for which in (1, 2, 3):
 
-            @pl.when(index == which * per)
+            @pl.when(index == 1 + which * per)
             def _():
                 for copy in moves[which - 1]:
                     copy.wait_recv()
 
     def slot(index):
-        step = index // per
-        return (r // 2 + step // 2) % 2 * 2 + (r % 2 + step % 2) % 2
+        step = (index + per - 1) // per - 1
+        turned = (r // 2 + step // 2) % 2 * 2 + (r % 2 + step % 2) % 2
+        return jnp.where(index == 0, 4, turned)
 
     def strip_of(index):
-        return pl.multiple_of(index % per * CHUNK, CHUNK)
+        return pl.multiple_of((index + per - 1) % per * CHUNK * jnp.where(index == 0, 0, 1), CHUNK)
 
     def own_at(index, part):
         return own.at[slot(index), pl.ds(part * half + strip_of(index), CHUNK), :]
@@ -1103,22 +1206,61 @@
     def out_at(index, part):
         return out.at[slot(index), pl.ds(part * half + strip_of(index), CHUNK), :]
 
-    def remote(source, target, sender, receiver, device):
-        return pltpu.make_async_remote_copy(
-            src_ref=source,
-            dst_ref=target,
-            send_sem=sender,
-            recv_sem=receiver,
-            device_id=device,
-            device_id_type=MESH,
-        )
-
-    def loop(count, body):
+    def loop(first, last, body):
         def run(index, nothing):
             body(index)
             return nothing
 
-        lax.fori_loop(0, count, run, 0)
+        lax.fori_loop(first, last, run, 0)
+
+    spread_out = [
+        [
+            remote(
+                source,
+                target.at[6 - step],
+                small_send.at[kind, 3 + step],
+                small_recv.at[kind, 3 + 6 - step],
+                peer,
+            )
+            for step, peer in enumerate(
+                [(z, (r + turn % 4) % 4, (c + turn // 4) % 2) for turn in range(1, 8)]
+            )
+        ]
+        for kind, (source, target) in enumerate(((vec_sum, vec_in), (gain_sum, gain_in)))
+    ]
+
+    def small_middle():
+        for kind in small:
+            for copy in kind:
+                copy.wait_recv()
+        vec_sum[...] = vec[...] + vec_z[0] + vec_z[1] + vec_z[2]
+        gain_sum[...] = gain[...] + gain_z[0] + gain_z[1] + gain_z[2]
+        for kind in spread_out:
+            for copy in kind:
+                copy.start()
+
+    gate_moves = []
+    for which, peer in enumerate((twin, side, cross)):
+        for part in (0, 1):
+            gate_moves.append(
+                remote(
+                    out.at[4, pl.ds(part * half, CHUNK), :],
+                    out_gates.at[r, part],
+                    small_send.at[0, 10 + 2 * which + part],
+                    small_recv.at[0, 10 + 2 * which + part],
+                    peer,
+                )
+            )
+    gate_local = [
+        pltpu.make_async_copy(
+            out.at[4, pl.ds(part * half, CHUNK), :], out_gates.at[r, part], gate_sem.at[part]
+        )
+        for part in (0, 1)
+    ]
+
+    def gates_out():
+        for copy in gate_moves + gate_local:
+            copy.start()
 
     @pl.when(is_end)
     def _():
@@ -1157,8 +1299,11 @@
                     spot, spot, end_send.at[0, index], out_recv.at[part, index], peer
                 ).wait_recv()
 
-        loop(chunks, begin)
-        loop(chunks, end)
+        loop(0, chunks, begin)
+        small_middle()
+        loop(0, 1, end)
+        gates_out()
+        loop(1, chunks, end)
 
     @pl.when(jnp.logical_not(is_end))
     def _():
@@ -1239,37 +1384,81 @@
 
         def end(index):
             to_other(index).wait_send()
-            here_copy, first, last = final(index)
-            here_copy.wait()
+            _, first, last = final(index)
             first.wait_send()
             last.wait_send()
             onward(index).wait_send()
 
-        loop(chunks + 4, step)
-        loop(chunks, end)
-
-    for moved in moves:
-        for copy in moved:
+        def end_local(index):
+            final(index)[0].wait()
+
+        loop(0, 32, step)
+        small_middle()
+        end_local(0)
+        gates_out()
+        loop(32, chunks + 4, step)
+        loop(1, chunks, end_local)
+        loop(0, chunks, end)
+
+    for kind in spread_out:
+        for copy in kind:
+            copy.wait_recv()
+    out_gain[...] = (
+        gain_sum[...]
+        + gain_in[0]
+        + gain_in[1]
+        + gain_in[2]
+        + gain_in[3]
+        + gain_in[4]
+        + gain_in[5]
+        + gain_in[6]
+    )
+    out_vec[...] = jnp.zeros_like(out_vec)
+    out_vec[r] = vec_sum[...]
+    for step in (0, 1, 2):
+        out_vec[(r + 3 - step) % 4] = vec_in[6 - step]
+    for copy in gate_moves:
+        copy.wait_recv()
+    for copy in gate_local:
+        copy.wait()
+    for group in small + spread_out + moves + [gate_moves]:
+        for copy in group:
             copy.wait_send()
 
 
-def reduce_grads(sources):
+def reduce_grads(sources, gates, vec, gain):
     rows = sources[0].shape[0] // 4
     width = sum(source.shape[1] for source in sources)
-    chunks = 4 * (rows // 2 // CHUNK)
+    chunks = 4 * (rows // 2 // CHUNK) + 1
     dma = pltpu.SemaphoreType.DMA
     count = len(sources)
+    vmem = pl.BlockSpec(memory_space=pltpu.VMEM)
+    loose = pl.BlockSpec(memory_space=pl.ANY)
     return pl.pallas_call(
         functools.partial(reduce_kernel, count),
-        in_specs=[pl.BlockSpec(memory_space=pl.ANY)] * count,
-        out_specs=pl.BlockSpec(memory_space=pl.ANY),
-        out_shape=jax.ShapeDtypeStruct((4, rows, width), jnp.bfloat16),
+        in_specs=[loose] * (count + 1) + [vmem, vmem],
+        out_specs=[loose, loose, vmem, vmem],
+        out_shape=[
+            jax.ShapeDtypeStruct((5, rows, width), jnp.bfloat16),
+            jax.ShapeDtypeStruct((4, 2, CHUNK, width), jnp.bfloat16),
+            jax.ShapeDtypeStruct((4, *vec.shape), jnp.float32),
+            jax.ShapeDtypeStruct(gain.shape, jnp.float32),
+        ],
         scratch_shapes=[
-            pltpu.VMEM((4, rows, width), jnp.bfloat16),
+            pltpu.VMEM((5, rows, width), jnp.bfloat16),
             pltpu.VMEM((chunks, CHUNK, width), jnp.bfloat16),
             pltpu.VMEM((2, chunks, CHUNK, width), jnp.bfloat16),
+            pltpu.VMEM((3, *vec.shape), jnp.float32),
+            pltpu.VMEM((3, *gain.shape), jnp.float32),
+            pltpu.VMEM(vec.shape, jnp.float32),
+            pltpu.VMEM(gain.shape, jnp.float32),
+            pltpu.VMEM((7, *vec.shape), jnp.float32),
+            pltpu.VMEM((7, *gain.shape), jnp.float32),
             dma((4, count)),
             dma((4, count)),
+            dma((10,)),
+            dma((2, 16)),
+            dma((2, 16)),
             dma((2, chunks)),
             dma((chunks,)),
             dma((2, chunks)),
@@ -1284,7 +1473,7 @@
             collective_id=REDUCE_ID, has_side_effects=True, vmem_limit_bytes=VMEM_BYTES
         ),
         name="reduce_grads",
-    )(*sources)
+    )(*sources, gates, vec, gain)
 
 
 def dot(left, right, dims, kind=jnp.float32):
@@ -1328,14 +1517,11 @@
         [x_proj.reshape(depth, 4, rec), y_proj.reshape(depth, 4, rec)], axis=2
     ).transpose(1, 0, 2)
     flags = jnp.pad(starts.astype(jnp.float32).reshape(-1, 128), ((0, 6), (0, 0)))
-    x_all, c_all, s_all, mix_w, out_w, gate_w, up_w, down_w = gather(
-        inputs.T, cotangent.T, flags, mix_in, out_proj, (gate_proj, up_proj, down_proj)
+    x_all, s_all, g_all, mix_w, out_w = gather(
+        inputs.T, flags, jnp.stack([mix_gain, mlp_gain]), mix_in, out_proj
     )
     tokens, model = x_all.shape
-    gain_mix, gain_mlp = (
-        lax.all_gather(mix_gain, "row", axis=0, tiled=True)[None, :],
-        lax.all_gather(mlp_gain, "row", axis=0, tiled=True)[None, :],
-    )
+    gain_mix, gain_mlp = (g_all[0:1], g_all[1:2])
     fresh = s_all[:, :2, :].reshape(tokens)
     stale = 1.0 - fresh
     stale_one = jnp.concatenate([jnp.zeros((1,), jnp.float32), stale[:-1]])
@@ -1366,32 +1552,49 @@
         return jnp.concatenate(rows, axis=0)
 
     rec_w, in_w = (diagonal(rec_gate_w), diagonal(in_gate_w))
-    values = x_all.astype(jnp.float32)
-    scale = lax.rsqrt(jnp.mean(values * values, axis=1, keepdims=True) + EPS)
-    normed_mix = (values * scale * gain_mix).astype(low)
-    pre = dot(normed_mix, mix_w, CONTRACT_PLAIN)
-    mixed, x_pre, conv, rec_gate, in_gate, states = mixer_forward(
-        pre, masks, vec, rec_w, in_w, padded
-    )
     size = tokens // 8
     shard = token_shard(r, c) * size
     resid = lax.dynamic_slice_in_dim(x_all, shard, size, 0)
-    cot = lax.dynamic_slice_in_dim(c_all, shard, size, 0)
     full = jax.ShapeDtypeStruct((tokens, model), low)
     part = jax.ShapeDtypeStruct((size, model), jnp.float32)
     line = jax.ShapeDtypeStruct((1, model), jnp.float32)
     piece = pltpu.VMEM((size, model), low)
     block = jax.ShapeDtypeStruct((inputs.shape[1], inputs.shape[0]), low)
-    normed_mlp, resid_mid = vmem_call(
+    weights = (gate_proj, up_proj, down_proj)
+    slices = jax.ShapeDtypeStruct((4 * depth, width), low)
+    kept = [((tokens, model), low), ((tokens, 2 * rec), jnp.float32), ((tokens, padded), low)]
+    kept += [((tokens, rec), kind) for kind in (jnp.float32, low) + (jnp.float32,) * 3]
+    row8 = pltpu.VMEM((8, rec), jnp.float32)
+    (
+        normed_mlp,
+        resid_mid,
+        c_all,
+        gate_w,
+        up_w,
+        down_w,
+        normed_mix,
+        pre,
+        mixed,
+        x_pre,
+        conv,
+        rec_gate,
+        in_gate,
+        states,
+    ) = vmem_call(
         forward_kernel,
-        "forward_norm",
+        "forward",
         FORWARD_ID,
-        (dot(mixed[:, :rec], out_w, CONTRACT_PLAIN, low), resid, gain_mlp),
-        [full, part],
-        [pl.ANY, pltpu.VMEM],
-        reduce_scratch(size, model) + [piece],
-        24,
-    )
+        (x_all, masks, vec, rec_w, in_w, mix_w, out_w, gain_mix, gain_mlp),
+        [full, part, full] + [slices] * 3 + [jax.ShapeDtypeStruct(*item) for item in kept],
+        [pl.ANY, pltpu.VMEM] + [pl.ANY] * 12,
+        [pltpu.VMEM(*item) for item in kept]
+        + [row8, row8, pltpu.VMEM((tokens, model), low)]
+        + reduce_scratch(size, model)
+        + [piece, pltpu.SemaphoreType.DMA((8,))],
+        80,
+        (cotangent.T, *weights),
+    )
+    cot = lax.dynamic_slice_in_dim(c_all, shard, size, 0)
     gate = dot(normed_mlp, gate_w, CONTRACT_PLAIN)
     up = dot(normed_mlp, up_w, CONTRACT_PLAIN)
     d_activ = dot(c_all, down_w, CONTRACT_PLAIN)
@@ -1433,48 +1636,42 @@
         reduce_scratch(size, model) * 2 + [piece, piece],
         40,
     )
-    grads = reduce_grads(
+    gate_grads = dot(conv, d_gates, CONTRACT_ROWS, low)
+    gates = jnp.concatenate(
+        [
+            gate_grads[i * head : (i + 1) * head, first + i * head : first + (i + 1) * head]
+            for first in (0, rec)
+            for i in range(heads)
+        ],
+        axis=1,
+    )
+    grads, gates, vec_sums, gains = reduce_grads(
         (
             dot(normed_mlp, d_gate, CONTRACT_ROWS, low),
             dot(normed_mlp, d_up, CONTRACT_ROWS, low),
             dot(c_all, activ, CONTRACT_ROWS, low),
             dot(normed_mix, d_pre, CONTRACT_ROWS, low),
             dot(d_branch, mixed, CONTRACT_ROWS, low),
-        )
-    )
-    gate_grads = dot(conv, d_gates, CONTRACT_ROWS, low)
-
-    def spots(array, axis):
-        shape = list(array.shape)
-        length = shape[axis]
-        shape[axis] = 4 * length
-        return lax.dynamic_update_slice_in_dim(
-            jnp.zeros(shape, array.dtype), array, r * length, axis
-        )
-
-    def blocks(array):
-        return jnp.stack(
-            [array[i * head : (i + 1) * head, i * head : (i + 1) * head] for i in range(heads)]
-        )
-
-    grad_rec_w = spots(blocks(gate_grads[:, :rec]), 0)
-    grad_in_w = spots(blocks(gate_grads[:, rec:]), 0)
-    vec_sums, grad_rec_w, grad_in_w = (
-        item.astype(jnp.float32)
-        for item in lax.psum((spots(sums.astype(low), 1), grad_rec_w, grad_in_w), ("dp", "row"))
-    )
-    gains = lax.psum(
-        jnp.concatenate([grad_mix_gain, grad_mlp_gain], axis=0), ("dp", "row", "col")
-    )
+        ),
+        gates,
+        sums,
+        jnp.concatenate([grad_mix_gain, grad_mlp_gain], axis=0),
+    )
+    gates = gates[:, :, :, : 5 * 4 * head].reshape(4, 2, CHUNK, 5, 2, heads, head)
+    gates = gates.transpose(4, 0, 5, 1, 3, 2, 6).reshape(2, 4 * heads, head, head)
+    gates = gates.astype(jnp.float32)
+    vec_sums = vec_sums.transpose(1, 0, 2).reshape(vec_sums.shape[1], 4 * rec)
     gains = lax.dynamic_slice_in_dim(gains, r * depth, depth, 1)
 
     def columns(first, length):
-        piece = grads[:, :, first : first + length].astype(jnp.float32)
-        return piece.transpose(1, 0, 2).reshape(depth, 4 * length)
+        return jnp.concatenate(
+            [grads[i, :, first : first + length] for i in range(4)], axis=1
+        ).astype(jnp.float32)
 
     after = 3 * width
-    grad_out = grads[:, :, after + 2 * rec : after + 3 * rec].astype(jnp.float32)
-    grad_out = grad_out.transpose(0, 2, 1).reshape(4 * rec, depth)
+    grad_out = jnp.concatenate(
+        [grads[i, :, after + 2 * rec : after + 3 * rec].T for i in range(4)], axis=0
+    ).astype(jnp.float32)
     return (
         output.T,
         grad_in.astype(jnp.float32).T,
@@ -1490,8 +1687,8 @@
         vec_sums[1],
         vec_sums[2:6],
         vec_sums[6],
-        grad_rec_w,
-        grad_in_w,
+        gates[0],
+        gates[1],
         vec_sums[7],
         vec_sums[8],
         vec_sums[9],

time: 968 us -> 790 us (0.82)
  blocking collectives: 108 us -> 0 us
  Pallas kernels: 650 us -> 627 us
  matrix products: 82.4 us -> 62.8 us
  between operations: 15.2 us -> 1.68 us
  local copies, waits for them, and re-layouts: 75.6 us -> 63.2 us
    psum x2 -> x0, blocking collectives: 97.4 us -> none  [the longest x1 60 us: local_plane(): lax.psum((spots(sums.astype(low), 1), grad_rec_w, grad_in_w), ('dp', 'row'))]
    pallas_call x1, Pallas kernels: 138 us -> 51 us  [gather(): pl.pallas_call(gather_kernel, in_specs=[pl.BlockSpec(memory_space=pl.ANY)...]
    pallas_call x3, Pallas kernels: 158 us -> 229 us  [vmem_call(): pl.pallas_call(kernel, in_specs=[pl.BlockSpec(memory_space=pltpu.VMEM)] *...]
    reshape x6 -> x0, local copies, waits for them, and re-layouts: 26.4 us -> none  [the longest x5 24.2 us: columns(): return piece.transpose(1, 0, 2).reshape(depth, 4 * length)]
    unnamed x95 -> x77, local copies, waits for them, and re-layouts: 38.1 us -> 13 us
    dot_general x14 -> x12, matrix products: 74 us -> 54.3 us  [dot(): lax.dot_general(left, right, dims, preferred_element_type=jnp.float32)]
    reshape x2 -> x0, other arithmetic: 15.9 us -> none  [the longest x1 9.19 us: columns(): return piece.transpose(1, 0, 2).reshape(depth, 4 * length)]
    all_gather x2 -> x0, blocking collectives: 10.8 us -> none  [the longest x1 5.6 us: local_plane(): lax.all_gather(mlp_gain, 'row', axis=0, tiled=True)[None, :]]
  transfers between devices with their start and end apart: 1 -> 0, of which waited for: 0 -> 0; matrix products, arithmetic and copies ran while one was open for 12% -> 0% of each run, Pallas kernels for 41% -> 0%
where the time goes in v2:
time: 790 us; the launch traced here: 780 us
  Pallas kernels  627 us (79%)
  local copies, waits for them, and re-layouts  63.2 us (8%)
  matrix products  62.8 us (8%)
  other arithmetic  26.1 us (3%)
    pallas_call x1, Pallas kernels, reduce_grads(): pl.pallas_call(functools.partial(reduce_kernel, count), in_specs=[loose]...  335 us
    pallas_call x3, Pallas kernels, vmem_call(): pl.pallas_call(kernel, in_specs=[pl.BlockSpec(memory_space=pltpu.VMEM)] *...  229 us
    dot_general x12, matrix products, dot(): lax.dot_general(left, right, dims, preferred_element_type=jnp.float32)  54.3 us
    pallas_call x1, Pallas kernels, gather(): pl.pallas_call(gather_kernel, in_specs=[pl.BlockSpec(memory_space=pl.ANY)...  51 us

profile of v2, /device:TPU:0, one launch (start us, length us, event | category | flops | bytes accessed | tf_op | source)
XLA Modules:
  0.0 780.3 jit_solution(13437453050380349271)
XLA Ops:
  0.7 0.8 convert_bitcast_fusion.1
  2.1 1.3 pad_maximum_fusion.2.g_in
  3.4 0.7 broadcast_in_dim.20
  4.8 0.7 broadcast_in_dim.22
  6.9 0.7 divide_multiply_fusion
  7.7 0.8 concatenate.58
  9.2 1.0 dynamic-slice_bitcast_fusion.1
  10.2 0.8 fusion.5.in_w
  11.0 0.8 fusion.4.rec_w
  11.8 2.0 copy.64
  13.8 1.0 copy.69
  15.5 0.9 copy.67
  16.3 2.4 copy.66
  18.8 1.8 copy.68
  20.6 2.5 maximum_bitcast_fusion.mix_in
  23.1 51.0 %gather.1 = (bf16[1024,2048]{1,0:T(8,128)(2,1)}, f32[4,8,128]{2,1,0:T(8,128)}, f32[2,2048]{1,0:T(2,128)}, bf16[2048,640]{1,0:T(8,128)(2,1)}, bf16[320,2048]{1,0:T(8,128)(2,1)}) custom-call(bf16[512,512]{1,0:T(8,128)(2,1)} %bitcast.123, f32[8,128]{1,0:T(8,128)} %pad.19.s_in, f32[2,512]{1,0:T(2,128)} %pad_maximum_fusion.2.g_in, ...), custom_call_target="tpu_custom_call" | custom-call | tf_op jit(solution)/shard_map/gather/pallas_call | solution.py:783
  74.1 0.7 broadcast_subtract_fusion
  75.0 1.4 fusion.11
  76.4 1.0 copy.70.masks
  77.4 1.9 constant_dynamic-slice_fusion.1.resid
  79.3 120.4 %forward.1 = (bf16[1024,2048]{1,0:T(8,128)(2,1)}, f32[128,2048]{1,0:T(8,128)}, bf16[1024,2048]{1,0:T(8,128)(2,1)}, bf16[2048,768]{1,0:T(8,128)(2,1)}, bf16[2048,...) custom-call(bf16[1024,2048]{1,0:T(8,128)(2,1)} %get-tuple-element.51, ...), custom_call_target="tpu_custom_call" | custom-call | tf_op jit(solution)/shard_map/forward/pallas_call | solution.py:1071
  199.7 1.9 constant_dynamic-slice_fusion.2.cot
  201.6 6.7 fusion.12
  208.4 3.4 fusion.13
  211.8 5.1 multiply_convert_fusion
  217.0 5.0 convolution_convert_fusion.2.refs_2_
  222.0 5.0 convolution_convert_fusion.1.out_parts
  227.0 5.0 convolution_convert_fusion.4.refs_0_
  231.9 5.2 convolution_convert_fusion.3.refs_1_
  237.1 3.4 fusion.14
  240.5 5.0 add_convert_fusion.parts
  245.5 49.1 %backward_norm.1 = (bf16[1024,2048]{1,0:T(8,128)(2,1)}, f32[128,2048]{1,0:T(8,128)}, f32[1,2048]{1,0:T(1,128)}) custom-call(bf16[1024,2048]{1,0:T(8,128)(2,1)} %add_convert_fusion.parts, f32[128,2048]{1,0:T(8,128)} %get-tuple-element.61.resid_mid, bf16[128,2048]{1,0:T(8,128)(2,1)} %constant_dynamic-slice_fusion.2.cot, f32[1,2048]{1,0:T(1,128)} %get-tuple-element.185.gain), custom_call_target="tpu_custom_call" | custom-call | tf_op jit(solution)/shard_map/backward_norm/pallas_call | solution.py:1071
  294.8 4.7 fusion.15.d_mixed
  300.0 11.6 %mixer_backward.1 = (bf16[1024,640]{1,0:T(8,128)(2,1)S(1)}, bf16[1024,640]{1,0:T(8,128)(2,1)S(1)}, f32[16,320]{1,0:T(8,128)S(1)}) custom-call(f32[1024,320]{1,0:T(8,128)S(1)} %fusion.15.d_mixed, f32[1024,640]{1,0:T(8,128)S(1)} %copy-done.3, f32[1024,8]{1,0:T(8,128)S(1)} %copy-done.2, f32[16,320]{1,0:T(8,128)S(1)} %copy-done.9, ...), custom_call_target="tpu_custom_call" | custom-call | tf_op jit(solution)/shard_map/mixer_backward/pallas_call | solution.py:545
  311.7 3.5 convolution_convert_fusion.6.refs_4_
  315.2 5.0 convolution_convert_fusion.5.refs_3_
  320.2 0.7 convolution_convert_fusion.7
  321.1 0.8 pad_maximum_fusion.refs_5_
  322.0 5.0 convolution_convert_fusion.parts
  327.0 59.1 %finish_norm.1 = (bf16[512,512]{1,0:T(8,128)(2,1)}, bf16[512,512]{1,0:T(8,128)(2,1)}, f32[1,2048]{1,0:T(1,128)}) custom-call(bf16[1024,2048]{1,0:T(8,128)(2,1)} %convolution_convert_fusion.parts, bf16[1024,2048]{1,0:T(8,128)(2,1)} %convolution_convert_fusion.1.out_parts, bf16[128,2048]{1,0:T(8,128)(2,1)} %constant_dynamic-slice_fusion.1.resid, ...), custom_call_target="tpu_custom_call" | custom-call | tf_op jit(solution)/shard_map/finish_norm/pallas_call | solution.py:1071
  386.1 2.0 copy.76
  388.1 1.3 pad_maximum_fusion.1.refs_7_
  389.5 1.2 convert_bitcast_fusion
  390.6 1.3 copy.77
  392.0 335.3 %reduce_grads.1 = (bf16[5,512,3328]{2,1,0:T(8,128)(2,1)}, bf16[4,2,16,3328]{3,2,1,0:T(8,128)(2,1)}, f32[4,16,320]{2,1,0:T(8,128)}, f32[2,2048]{1,0:T(2,128)}) custom-call(bf16[2048,768]{1,0:T(8,128)(2,1)} %convolution_convert_fusion.4.refs_0_, bf16[2048,768]{1,0:T(8,128)(2,1)} %convolution_convert_fusion.3.refs_1_, ...), custom_call_target="tpu_custom_call" | custom-call | tf_op jit(solution)/shard_map/reduce_grads/pallas_call | solution.py:1437
  727.2 1.4 fusion.10
  728.7 0.8 slice.214
  729.5 1.1 slice_reduce_fusion
  735.3 2.4 slice_convert_fusion
  737.7 5.2 reshape.118
  742.9 1.3 fusion.8
  744.3 1.3 copy.75
  745.5 1.3 copy.74
  746.8 6.0 slice_bitcast_fusion.12
  752.8 3.2 slice_bitcast_fusion.3
  756.0 2.8 concatenate.65
  758.8 1.9 copy.78
  760.6 2.8 concatenate.64
  763.4 1.7 convert_element_type.90
  765.1 2.6 concatenate.63
  767.8 1.7 convert_element_type.89
  770.6 3.1 maximum_convert_fusion.2
  773.7 3.1 maximum_convert_fusion.1
  776.8 3.1 maximum_convert_fusion
  (92 shorter events, 10.8 us)
Async XLA Ops:
  0.7 14.2 %copy-start.24 = (bf16[512,1280]{1,0:T(8,128)(2,1)S(1)}, bf16[512,1280]{1,0:T(8,128)(2,1)}, u32[]{:S(2)}) copy-start(bf16[512,1280]{1,0:T(8,128)(2,1)} %param.23) | copy-start | bytes 3932164
  0.7 13.2 %copy-start.25 = (bf16[512,512]{1,0:T(8,128)(2,1)S(1)}, bf16[512,512]{1,0:T(8,128)(2,1)}, u32[]{:S(2)}) copy-start(bf16[512,512]{1,0:T(8,128)(2,1)} %param.21) | copy-start | bytes 1572868
  201.6 6.8 copy-start.29
  201.6 6.8 copy-start.32
  208.3 3.4 copy-start.31
  211.8 5.2 copy-start.26
  217.0 5.0 copy-start.33
  245.5 49.2 %copy-start.23 = (bf16[320,2048]{1,0:T(8,128)(2,1)S(1)}, bf16[320,2048]{1,0:T(8,128)(2,1)}, u32[]{:S(2)}) copy-start(bf16[320,2048]{1,0:T(8,128)(2,1)} %get-tuple-element.54.out_w) | copy-start | bytes 3932164
  294.7 4.8 copy-start
  294.7 4.8 copy-start.1
  294.7 4.8 copy-start.2
  294.7 4.8 copy-start.3
  294.7 4.8 copy-start.4
  294.8 4.8 copy-start.5
  294.8 4.8 copy-start.6
  294.8 5.1 copy-start.7
  294.8 5.2 copy-start.8
  294.8 5.2 copy-start.9
  300.0 11.6 %copy-start.30 = (bf16[1024,2048]{1,0:T(8,128)(2,1)S(1)}, bf16[1024,2048]{1,0:T(8,128)(2,1)}, u32[]{:S(2)}) copy-start(bf16[1024,2048]{1,0:T(8,128)(2,1)} %get-tuple-element.62) | copy-start | bytes 12582916
  300.0 11.6 %copy-start.34 = (bf16[1024,384]{1,0:T(8,128)(2,1)S(1)}, bf16[1024,384]{1,0:T(8,128)(2,1)}, u32[]{:S(2)}) copy-start(bf16[1024,384]{1,0:T(8,128)(2,1)} %get-tuple-element.74) | copy-start | bytes 2359300
  311.6 3.6 copy-start.10
  311.7 3.5 copy-start.28
  320.2 1.7 copy-start.22
  327.0 61.2 %copy-start.27 = (f32[1,2048]{1,0:T(1,128)S(1)}, f32[1,2048]{1,0:T(1,128)}, u32[]{:S(2)}) copy-start(f32[1,2048]{1,0:T(1,128)} %get-tuple-element.78) | copy-start | bytes 24580
  742.9 9.9 %copy-start.11 = (bf16[5,512,3328]{2,1,0:T(8,128)(2,1)S(1)}, bf16[5,512,3328]{2,1,0:T(8,128)(2,1)}, u32[]{:S(2)}) copy-start(bf16[5,512,3328]{2,1,0:T(8,128)(2,1)} %get-tuple-element.79) | copy-start | bytes 51118084
  767.7 1.7 copy-start.18
  767.8 1.9 copy-start.19
  767.8 2.5 copy-start.20
  767.8 2.8 copy-start.21
  770.5 3.1 copy-start.14
  770.5 3.1 copy-start.15
  770.6 3.1 copy-start.16
  770.6 3.1 copy-start.17
  773.7 3.1 copy-start.12
  773.7 3.1 copy-start.13

commit v3 on v2

--- a/solution.py
+++ b/solution.py
@@ -329,9 +329,9 @@
     )
 
 
-GATHER_ID, FORWARD_ID, BACKWARD_ID, FINISH_ID, REDUCE_ID = (0, 1, 2, 3, 4)
+GATHER_ID, FORWARD_ID, BACKWARD_ID, REDUCE_ID = (0, 1, 2, 3)
 BLOCK = 128
-VMEM_BYTES = 56 << 20
+VMEM_BYTES = 60 << 20
 
 
 def one_minus_exp(rate):
@@ -432,10 +432,10 @@
     mixed[:, width:] = jnp.zeros((BLOCK, mixed.shape[1] - width), jnp.bfloat16)
 
 
-def mixer_backward_kernel(
-    d_mixed,
+def mixer_backward_step(
+    incoming,
     pre,
-    masks,
+    marks,
     vec,
     rec_w,
     in_w,
@@ -453,20 +453,11 @@
     carry,
 ):
     width = x_pre.shape[1]
-
-    @pl.when(pl.program_id(0) == 0)
-    def _():
-        edge[...] = jnp.zeros_like(edge)
-        carry[...] = jnp.zeros_like(carry)
-        sums[...] = jnp.zeros_like(sums)
-
     position = lax.broadcasted_iota(jnp.int32, (BLOCK, width), 0)
-    marks = masks[...]
     fresh = marks[:, 0:1]
     stale = 1.0 - fresh
     gelu, slope = gelu_both(pre[:, width:] + vec[1:2, :])
     state = states[...]
-    incoming = d_mixed[...]
     d_y = (incoming * state * slope).astype(jnp.bfloat16)
     rec, inn = (rec_gate[...], in_gate[...])
     conv_vals = conv[...].astype(jnp.float32)
@@ -505,15 +496,15 @@
     d_x = d_conv * vec[2:3, :]
     taps = [column(d_conv * x)]
     for tap in range(1, 4):
-        part = marks[:, tap : tap + 1] * d_conv
-        taps.append(column(part * down_rows(longer, tap)[8:]))
-        beyond = jnp.concatenate([part, edge[8 * tap - 8 : 8 * tap, :]], axis=0)
+        piece = marks[:, tap : tap + 1] * d_conv
+        taps.append(column(piece * down_rows(longer, tap)[8:]))
+        beyond = jnp.concatenate([piece, edge[8 * tap - 8 : 8 * tap, :]], axis=0)
         d_x = d_x + vec[2 + tap : 3 + tap, :] * up_rows(beyond, tap)[:BLOCK]
-        edge[8 * tap - 8 : 8 * tap, :] = part[:8]
+        edge[8 * tap - 8 : 8 * tap, :] = piece[:8]
     d_x = d_x.astype(jnp.bfloat16)
     d_pre[:, :width] = d_x
     d_pre[:, width:] = d_y
-    parts = (
+    pieces = (
         [column(d_x.astype(jnp.float32)), column(d_y.astype(jnp.float32))]
         + taps
         + [
@@ -523,53 +514,8 @@
             column(d_log * rec) * vec[10:11, :],
         ]
     )
-    for place, part in enumerate(parts):
-        sums[place : place + 1, :] += part
-
-
-def mixer_backward(d_mixed, pre, masks, vec, rec_w, in_w, x_pre, conv, rec_gate, in_gate, states):
-    tokens, width = x_pre.shape
-    last = tokens // BLOCK - 1
-
-    def block(columns):
-        return pl.BlockSpec((BLOCK, columns), lambda i: (last - i, 0))
-
-    def before():
-        return pl.BlockSpec(
-            (8, width), lambda i: (jnp.maximum((last - i) * (BLOCK // 8) - 1, 0), 0)
-        )
-
-    def whole(array):
-        return pl.BlockSpec(array.shape, lambda i: (0, 0))
-
-    return pl.pallas_call(
-        mixer_backward_kernel,
-        grid=(tokens // BLOCK,),
-        in_specs=[
-            block(width),
-            block(2 * width),
-            block(8),
-            whole(vec),
-            whole(rec_w),
-            whole(in_w),
-            block(width),
-            before(),
-            block(width),
-            block(width),
-            block(width),
-            block(width),
-            before(),
-        ],
-        out_specs=[block(2 * width), block(2 * width), pl.BlockSpec((16, width), lambda i: (0, 0))],
-        out_shape=[
-            jax.ShapeDtypeStruct((tokens, 2 * width), jnp.bfloat16),
-            jax.ShapeDtypeStruct((tokens, 2 * width), jnp.bfloat16),
-            jax.ShapeDtypeStruct((16, width), jnp.float32),
-        ],
-        scratch_shapes=[pltpu.VMEM((24, width), jnp.float32), pltpu.VMEM((8, width), jnp.float32)],
-        compiler_params=pltpu.CompilerParams(vmem_limit_bytes=32 << 20),
-        name="mixer_backward",
-    )(d_mixed, pre, masks, vec, rec_w, in_w, x_pre, x_pre, conv, rec_gate, in_gate, states, states)
+    for place, piece in enumerate(pieces):
+        sums[place : place + 1, :] += piece
 
 
 def here():
@@ -620,6 +566,7 @@
     def finish(self):
         for copy in self.sent:
             copy.wait_send()
+        self.sent = []
 
 
 def arrived(copy):
@@ -1000,73 +947,6 @@
     return (grad, jnp.sum(incoming * values * scale, axis=0, keepdims=True))
 
 
-def backward_kernel(parts, resid_mid, cot, gain, full, d_resid, gain_grad, *scratch):
-    *buffers, mine, send, recv = scratch
-    greet(near())
-    copies = Copies(send, recv)
-    total = reduce_shards(copies, parts, *buffers)
-    gain_grad[...] = jnp.zeros_like(gain_grad)
-
-    def body(at):
-        rows = pl.ds(at, STRIP)
-        grad, part = norm_pull(resid_mid[rows, :], gain[...], total(at))
-        grad = grad + cot[rows, :].astype(jnp.float32)
-        gain_grad[...] += part
-        d_resid[rows, :] = grad
-        mine[rows, :] = grad.astype(jnp.bfloat16)
-
-    strips(mine.shape[0], body)
-    spread_rows(copies, mine, full)
-    copies.finish()
-
-
-def finish_kernel(
-    parts, out_parts, resid, resid_mid, d_resid, gain, grad, output, gain_grad, *scratch
-):
-    buffers, more = (scratch[:5], scratch[5:10])
-    mine, mine_out, send, recv = scratch[10:]
-    z, r, c = here()
-    twin, side, top = near()
-    cross = (z, flip(across(r)), c)
-    greet((twin, side, top, cross))
-    copies = Copies(send, recv)
-    columns = grad.shape[1]
-    size = mine.shape[0]
-    gain_grad[...] = jnp.zeros_like(gain_grad)
-
-    def hand_out(source, target):
-        def piece(row):
-            return source.at[:, pl.ds(pl.multiple_of(row * columns, columns), columns)]
-
-        spot = target.at[pl.ds(pl.multiple_of(r * size, size), size), :]
-        waits = [copies.go(piece(peer[1]), spot, peer) for peer in (side, cross, twin)]
-        return (copies.go(piece(r), spot, None), waits)
-
-    total = reduce_shards(copies, out_parts, *more)
-
-    def body_out(at):
-        rows = pl.ds(at, STRIP)
-        mine_out[rows, :] = (resid_mid[rows, :] + total(at)).astype(jnp.bfloat16)
-
-    strips(size, body_out)
-    moves = [hand_out(mine_out, output)]
-    total_back = reduce_shards(copies, parts, *buffers)
-
-    def body(at):
-        rows = pl.ds(at, STRIP)
-        values, part = norm_pull(resid[rows, :].astype(jnp.float32), gain[...], total_back(at))
-        gain_grad[...] += part
-        mine[rows, :] = (d_resid[rows, :] + values).astype(jnp.bfloat16)
-
-    strips(size, body)
-    moves.append(hand_out(mine, grad))
-    for local, waits in moves:
-        for copy in waits:
-            arrived(copy)
-        local.wait()
-    copies.finish()
-
-
 def vmem_call(kernel, name, place, arrays, outs, spaces, scratch, count, loose=()):
     return pl.pallas_call(
         kernel,
@@ -1083,43 +963,540 @@
     )(*arrays, *loose)
 
 
-CHUNK = 16
-
-
-def reduce_kernel(count, *refs):
-    sources, (gates, vec, gain) = (refs[:count], refs[count : count + 3])
-    out, out_gates, out_vec, out_gain = refs[count + 3 : count + 7]
-    own, left, right, vec_z, gain_z, vec_sum, gain_sum, vec_in, gain_in = refs[count + 7 : count + 16]
-    move_send, move_recv, gate_sem, small_send, small_recv = refs[count + 16 : count + 21]
-    end_send, low_recv, high_recv, out_recv, mid_send, first_send, last_send, local, on_send = refs[
-        count + 21 :
+AHEAD = 3
+DEPTH = 4
+HAND_LAG = 4
+LAG = 6
+
+
+def run_loop(first, last, body):
+    def run(index, nothing):
+        body(index)
+        return nothing
+
+    lax.fori_loop(first, last, run, 0)
+
+
+def remote(source, target, sender, receiver, device):
+    return pltpu.make_async_remote_copy(
+        src_ref=source,
+        dst_ref=target,
+        send_sem=sender,
+        recv_sem=receiver,
+        device_id=device,
+        device_id_type=MESH,
+    )
+
+
+class Line:
+    def __init__(self, sources, own, left, right, out, sems, lead):
+        self.own, self.left, self.right, self.out, self.lead = (own, left, right, out, lead)
+        (
+            self.load_sem,
+            self.end_send,
+            self.low_recv,
+            self.high_recv,
+            self.out_recv,
+            self.mid_send,
+            self.first_send,
+            self.last_send,
+            self.hand_send,
+            self.on_send,
+        ) = sems
+        z, r, c = here()
+        self.chunk = left.shape[1]
+        self.rows = out.shape[1]
+        self.half = self.rows // 2
+        self.per = self.half // self.chunk
+        self.chunks = 4 * self.per + lead
+        self.total = self.chunks + LAG
+        self.at = 0
+        self.ahead = 0
+        self.is_end = (z == 0) | (z == 3)
+        self.near_z = (jnp.where(z == 0, 1, 2), r, c)
+        self.outer = (jnp.where(z == 1, 0, 3), r, c)
+        self.other = (3 - z, r, c)
+        self.loads = []
+        start = 0
+        for place, source in enumerate(sources):
+            width = source.shape[1]
+            self.loads.append(
+                pltpu.make_async_copy(
+                    source,
+                    own.at[pl.ds(0, 4 * self.rows), pl.ds(start, width)],
+                    self.load_sem.at[place],
+                )
+            )
+            start += width
+
+    def spot(self, index):
+        step = (index - self.lead + self.per) // self.per - 1
+        strip = (index - self.lead + self.per) % self.per
+        if self.lead:
+            strip = strip - jnp.where(step < 0, self.per - self.lead, 0)
+        return (step, strip)
+
+    def peer_row(self, index):
+        r = here()[1]
+        step = jnp.maximum(self.spot(index)[0], 0)
+        return (r // 2 + step // 2) % 2 * 2 + (r % 2 + step % 2) % 2
+
+    def stays(self, index):
+        return self.spot(index)[0] <= 0
+
+    def span(self, index, which):
+        step, strip = self.spot(index)
+        start = self.peer_row(index) * self.rows + which * self.half
+        if self.lead:
+            start = jnp.where(
+                step < 0, 4 * self.rows + which * self.lead * self.chunk, start
+            )
+        return pl.ds(pl.multiple_of(start + strip * self.chunk, self.chunk), self.chunk)
+
+    def own_at(self, index, which):
+        return self.own.at[self.span(index, which), :]
+
+    def out_at(self, index, which, row):
+        step, strip = self.spot(index)
+        if self.lead:
+            row = jnp.where(step < 0, 4, row)
+        start = pl.multiple_of(which * self.half + strip * self.chunk, self.chunk)
+        return self.out.at[row, pl.ds(start, self.chunk), :]
+
+    def end_sends(self, index):
+        low = here()[0] // 3
+        return (
+            remote(
+                self.own_at(index, low),
+                self.left.at[index],
+                self.end_send.at[0, index],
+                self.low_recv.at[index],
+                self.near_z,
+            ),
+            remote(
+                self.own_at(index, 1 - low),
+                self.right.at[1, index],
+                self.end_send.at[1, index],
+                self.high_recv.at[1, index],
+                self.near_z,
+            ),
+        )
+
+    def to_other(self, index):
+        low = here()[0] - 1
+        return remote(
+            self.own_at(index, 1 - low),
+            self.right.at[0, index],
+            self.mid_send.at[index],
+            self.high_recv.at[0, index],
+            self.other,
+        )
+
+    def from_outer(self, index):
+        low = here()[0] - 1
+        return (
+            remote(
+                self.own_at(index, low),
+                self.left.at[index],
+                self.mid_send.at[index],
+                self.low_recv.at[index],
+                self.outer,
+            ),
+            remote(
+                self.own_at(index, 1 - low),
+                self.right.at[1, index],
+                self.mid_send.at[index],
+                self.high_recv.at[1, index],
+                self.outer,
+            ),
+        )
+
+    def hand(self, index):
+        z, r, c = here()
+        low = z - 1
+        mine, spot = (self.own_at(index, low), self.out_at(index, low, r))
+        return (
+            pltpu.make_async_copy(mine, spot, self.out_recv.at[low, index]),
+            remote(
+                mine,
+                spot,
+                self.hand_send.at[index],
+                self.out_recv.at[low, index],
+                (z, self.peer_row(index), c),
+            ),
+        )
+
+    def along(self, index):
+        low = here()[0] - 1
+        spot = self.out_at(index, low, self.peer_row(index))
+        return (
+            remote(
+                spot, spot, self.first_send.at[index], self.out_recv.at[low, index], self.outer
+            ),
+            remote(spot, spot, self.last_send.at[index], self.out_recv.at[low, index], self.other),
+        )
+
+    def onward(self, index):
+        low = here()[0] - 1
+        spot = self.out_at(index, 1 - low, self.peer_row(index))
+        return remote(
+            spot, spot, self.on_send.at[index], self.out_recv.at[1 - low, index], self.outer
+        )
+
+    def end_step(self, index):
+        @pl.when(index < self.chunks)
+        def _():
+            @pl.when(index >= DEPTH)
+            def _():
+                for copy in self.end_sends(index - DEPTH):
+                    copy.wait_send()
+
+            for copy in self.end_sends(index):
+                copy.start()
+
+    def mid_step(self, index):
+        own, left, right, low = (self.own, self.left, self.right, here()[0] - 1)
+
+        @pl.when(index < self.chunks)
+        def _():
+            self.from_outer(index)[1].wait_recv()
+            span = self.span(index, 1 - low)
+            total = own[span, :].astype(jnp.float32) + right[1, index].astype(jnp.float32)
+            own[span, :] = total.astype(jnp.bfloat16)
+            self.to_other(index).start()
+
+        @pl.when((index >= 2) & (index < self.chunks + 2))
+        def _():
+            back = index - 2
+            self.from_outer(back)[0].wait_recv()
+            self.to_other(back).wait_recv()
+            span = self.span(back, low)
+            total = (
+                own[span, :].astype(jnp.float32)
+                + left[back].astype(jnp.float32)
+                + right[0, back].astype(jnp.float32)
+            )
+            own[span, :] = total.astype(jnp.bfloat16)
+
+            @pl.when(self.stays(back))
+            def _():
+                self.hand(back)[0].start()
+
+            @pl.when(jnp.logical_not(self.stays(back)))
+            def _():
+                self.hand(back)[1].start()
+
+        @pl.when((index >= HAND_LAG) & (index < self.chunks + HAND_LAG))
+        def _():
+            back = index - HAND_LAG
+
+            @pl.when(self.stays(back))
+            def _():
+                self.hand(back)[0].wait()
+
+            @pl.when(jnp.logical_not(self.stays(back)))
+            def _():
+                self.hand(back)[1].wait_recv()
+
+            for copy in self.along(back):
+                copy.start()
+
+        @pl.when(index >= LAG)
+        def _():
+            copy = self.onward(index - LAG)
+            copy.wait_recv()
+            copy.start()
+
+    def begin(self):
+        for copy in self.loads:
+            copy.start()
+
+    def ready(self):
+        for copy in self.loads:
+            copy.wait()
+
+    def advance(self, count):
+        first, last = (self.at, min(self.at + count, self.total))
+        self.at = last
+        if first == last:
+            return
+
+        @pl.when(self.is_end)
+        def _():
+            run_loop(self.ahead, last + AHEAD, self.end_step)
+
+        self.ahead = last + AHEAD
+
+        @pl.when(jnp.logical_not(self.is_end))
+        def _():
+            run_loop(first, last, self.mid_step)
+
+    def one(self, index):
+        @pl.when(self.is_end)
+        def _():
+            self.end_step(index + AHEAD)
+
+        @pl.when(jnp.logical_not(self.is_end))
+        def _():
+            self.mid_step(index)
+
+    def skip(self, count):
+        self.at += count
+        self.ahead += count
+
+    def end_done(self, index):
+        @pl.when(index >= self.chunks - DEPTH)
+        def _():
+            for copy in self.end_sends(index):
+                copy.wait_send()
+
+        for which in (0, 1):
+            spot = self.out_at(index, which, self.peer_row(index))
+            remote(
+                spot, spot, self.end_send.at[0, index], self.out_recv.at[which, index], self.near_z
+            ).wait_recv()
+
+    def mid_done(self, index):
+        self.to_other(index).wait_send()
+
+        @pl.when(jnp.logical_not(self.stays(index)))
+        def _():
+            self.hand(index)[1].wait_send()
+
+        for copy in self.along(index):
+            copy.wait_send()
+        self.onward(index).wait_send()
+
+    def settle(self, first, last):
+        @pl.when(self.is_end)
+        def _():
+            run_loop(first, last, self.end_done)
+
+        @pl.when(jnp.logical_not(self.is_end))
+        def _():
+            run_loop(first, last, self.mid_done)
+
+    def finish(self, first):
+        self.advance(self.total)
+        self.settle(first, self.chunks)
+
+
+def line_scratch(count, rows, width, chunk, lead):
+    dma = pltpu.SemaphoreType.DMA
+    chunks = 4 * (rows // 2 // chunk) + lead
+    return [
+        pltpu.VMEM((4 * rows + 2 * lead * chunk, width), jnp.bfloat16),
+        pltpu.VMEM((chunks, chunk, width), jnp.bfloat16),
+        pltpu.VMEM((2, chunks, chunk, width), jnp.bfloat16),
+        dma((count,)),
+        dma((2, chunks)),
+        dma((chunks,)),
+        dma((2, chunks)),
+        dma((2, chunks)),
+        dma((chunks,)),
+        dma((chunks,)),
+        dma((chunks,)),
+        dma((chunks,)),
+        dma((chunks,)),
     ]
+
+
+LINE_REFS = 13
+PACK = 32
+BACK_CHUNK = 32
+LAST_CHUNK = 16
+
+
+def z_peers():
     z, r, c = here()
-    twin, side, cross = ((z, flip(r), c), (z, across(r), c), (z, flip(across(r)), c))
-    is_end = (z == 0) | (z == 3)
-    near_z = jnp.where(z == 0, 1, 2)
-    end_z = jnp.where(z == 1, 0, 3)
-    lines = [((z + step) % 4, r, c) for step in (1, 2, 3)]
-    plane = [
-        (z, (r + step) % 4, (c + turn) % 2) for turn in (0, 1) for step in range(4) if step or turn
+    return [((z + step) % 4, r, c) for step in (1, 2, 3)]
+
+
+def plane_peers():
+    z, r, c = here()
+    return [(z, (r + turn % 4) % 4, (c + turn // 4) % 2) for turn in range(1, 8)]
+
+
+def hand_out(copies, source, target):
+    z, r, c = here()
+    twin, side, _ = near()
+    cross = (z, flip(across(r)), c)
+    columns = target.shape[1]
+    size = source.shape[0]
+
+    def piece(row):
+        return source.at[:, part(row, columns, columns)]
+
+    spot = target.at[part(r, size, size), :]
+    waits = [copies.go(piece(peer[1]), spot, peer) for peer in (side, cross, twin)]
+    local = copies.go(piece(r), spot, None)
+
+    def done():
+        for copy in waits:
+            arrived(copy)
+        local.wait()
+
+    return done
+
+
+def backward_kernel(resid_mid, gain, gain_mix, masks, vec, rec_w, in_w, mix_w, out_w, *refs):
+    parts_in, c_all, x_all, *kept_in = refs[:9]
+    sources, outs, scratch = (refs[9:11], refs[11:19], refs[19:])
+    branch_out, d_pre_out, d_gates_out, grad, grads, sums, gain_grad, gain_mix_grad = outs
+    line_refs, scratch = (scratch[:LINE_REFS], scratch[LINE_REFS:])
+    parts, cot, resid, branch, d_resid, d_pre, d_gates, edge, carry = scratch[:9]
+    kept, scratch = (scratch[9:15], scratch[15:])
+    *buffers, mine, load_sem, send, recv = scratch
+    pre, x_pre, conv, rec_gate, in_gate, states = kept
+    z, r, c = here()
+    greet([*near(), (z, flip(across(r)), c), *z_peers()])
+    copies = Copies(send, recv)
+    size = mine.shape[0]
+    shard = part(token_shard(r, c), size, size)
+    loads = [
+        pltpu.make_async_copy(source, target, load_sem.at[place])
+        for place, (source, target) in enumerate(
+            zip(
+                [parts_in, c_all.at[shard, :], x_all.at[shard, :], *kept_in],
+                [parts, cot, resid, *kept],
+            )
+        )
     ]
+    loads[0].start()
+    line = Line(sources, *line_refs[:3], grads, line_refs[3:], 0)
+    line.begin()
+    for copy in loads[1:]:
+        copy.start()
+    gain_grad[...] = jnp.zeros_like(gain_grad)
+    gain_mix_grad[...] = jnp.zeros_like(gain_mix_grad)
+    sums[...] = jnp.zeros_like(sums)
+    edge[...] = jnp.zeros_like(edge)
+    carry[...] = jnp.zeros_like(carry)
+    loads[0].wait()
+    line.ready()
+    pace = iter((4, 4, 4, 2, 2, 2, 4))
+
+    def between():
+        line.advance(next(pace))
+
+    total = reduce_shards(copies, parts, *buffers, between=between)
+    for copy in loads[1:]:
+        copy.wait()
+
+    def body(at):
+        rows = pl.ds(at, STRIP)
+        values, piece = norm_pull(resid_mid[rows, :], gain[...], total(at))
+        values = values + cot[rows, :].astype(jnp.float32)
+        gain_grad[...] += piece
+        d_resid[rows, :] = values
+        mine[rows, :] = values.astype(jnp.bfloat16)
+
+    strips(size, body)
+    spread_rows(copies, mine, branch, between)
+    copies.finish()
+    last = branch.shape[0] // BLOCK - 1
+    width = x_pre.shape[1]
+
+    def block(index, base):
+        start = pl.multiple_of((last - index) * BLOCK, BLOCK)
+        rows = pl.ds(start, BLOCK)
+        before = pl.ds(pl.multiple_of(jnp.maximum(start - 8, 0), 8), 8)
+        mixer_backward_step(
+            lax.dot_general(
+                branch[rows, :], out_w[...], CONTRACT_COLS, preferred_element_type=jnp.float32
+            ),
+            pre.at[rows, :],
+            masks[rows, :],
+            vec,
+            rec_w,
+            in_w,
+            x_pre.at[rows, :],
+            x_pre.at[before, :],
+            conv.at[rows, :],
+            rec_gate.at[rows, :],
+            in_gate.at[rows, :],
+            states.at[rows, :],
+            states.at[before, :],
+            d_pre.at[rows, :],
+            d_gates.at[rows, :],
+            sums,
+            edge,
+            carry,
+        )
+        parts[rows, :] = lax.dot_general(
+            d_pre[rows, :], mix_w[...], CONTRACT_COLS, preferred_element_type=jnp.float32
+        ).astype(jnp.bfloat16)
+
+        line.one(base + index)
+        return base
+
+    lax.fori_loop(0, last + 1, block, line.at)
+    line.skip(last + 1)
+    keeping = [
+        pltpu.make_async_copy(source, target, load_sem.at[place])
+        for place, (source, target) in enumerate(
+            ((branch, branch_out), (d_pre, d_pre_out), (d_gates, d_gates_out))
+        )
+    ]
+    for copy in keeping:
+        copy.start()
+    total_back = reduce_shards(copies, parts, *buffers, between=between)
+
+    def body_back(at):
+        rows = pl.ds(at, STRIP)
+        values, piece = norm_pull(
+            resid[rows, :].astype(jnp.float32), gain_mix[...], total_back(at)
+        )
+        gain_mix_grad[...] += piece
+        mine[rows, :] = (d_resid[rows, :] + values).astype(jnp.bfloat16)
+
+    strips(size, body_back)
+    done = hand_out(copies, mine, grad)
+    line.finish(0)
+    done()
+    for copy in keeping:
+        copy.wait()
+    copies.finish()
+
+
+def gate_tiles(width):
+    tiles = []
+    for tile in range(5):
+        first, rest = (0, width)
+        if tile < 4:
+            tiles.append((tile, 0, width, tile // 2, tile % 2 * width))
+        else:
+            tiles.append((tile, 0, 512, 0, 2 * width))
+            tiles.append((tile, 512, width - 512, 1, 2 * width))
+    return tiles
+
+
+def reduce_kernel(count, resid_mid, vec, gain, *refs):
+    parts_in, gates, sources = (refs[0], refs[1], refs[2 : 2 + count])
+    out, out_gates, output, out_vec, out_gain = refs[2 + count : 7 + count]
+    scratch = refs[7 + count :]
+    line_refs, scratch = (scratch[:LINE_REFS], scratch[LINE_REFS:])
+    vec_z, gain_z, vec_sum, gain_sum, vec_in, gain_in, parts = scratch[:7]
+    *buffers, mine, gate_sem, small_send, small_recv, send, recv = scratch[7:]
+    z, r, c = here()
+    twin, side, top = near()
+    cross = (z, flip(across(r)), c)
+    lines, plane = (z_peers(), plane_peers())
     greet(lines + plane)
-
-    rows = own.shape[1]
-    half = rows // 2
-    per = half // CHUNK
-    chunks = 4 * per + 1
-
-    def remote(source, target, sender, receiver, device):
-        return pltpu.make_async_remote_copy(
-            src_ref=source,
-            dst_ref=target,
-            send_sem=sender,
-            recv_sem=receiver,
-            device_id=device,
-            device_id_type=MESH,
+    copies = Copies(send, recv)
+    load = pltpu.make_async_copy(parts_in, parts, gate_sem.at[8])
+    load.start()
+    line = Line(sources, *line_refs[:3], out, line_refs[3:], PACK // LAST_CHUNK)
+    half = line.half
+    packed = []
+    for place, (tile, first, width, which, spot) in enumerate(gate_tiles(gates.shape[1])):
+        copy = pltpu.make_async_copy(
+            gates.at[pl.ds(tile * PACK, PACK), pl.ds(first, width)],
+            line.own.at[pl.ds(8 * half + which * PACK, PACK), pl.ds(spot, width)],
+            gate_sem.at[place],
         )
-
+        copy.start()
+        packed.append(copy)
     small = [
         [
             remote(
@@ -1136,83 +1513,10 @@
     for kind in small:
         for copy in kind:
             copy.start()
-    packed = []
-    width = gates.shape[1]
-    for tile in range(gates.shape[0] // CHUNK):
-        which, place = (tile // 5, tile % 5)
-        copy = pltpu.make_async_copy(
-            gates.at[pl.ds(tile * CHUNK, CHUNK), :],
-            own.at[4, pl.ds(which * half, CHUNK), pl.ds(place * width, width)],
-            gate_sem.at[tile],
-        )
-        copy.start()
-        packed.append(copy)
-    moves = []
-    for which, peer in ((1, twin), (2, side), (3, cross)):
-        start = 0
-        group = []
-        for place, source in enumerate(sources):
-            width = source.shape[1]
-            copy = remote(
-                source.at[pl.ds(pl.multiple_of(peer[1] * rows, rows), rows), :],
-                own.at[r, :, pl.ds(start, width)],
-                move_send.at[which, place],
-                move_recv.at[which, place],
-                peer,
-            )
-            copy.start()
-            group.append(copy)
-            start += width
-        moves.append(group)
-    start = 0
-    group = []
-    for place, source in enumerate(sources):
-        width = source.shape[1]
-        copy = pltpu.make_async_copy(
-            source.at[pl.ds(pl.multiple_of(r * rows, rows), rows), :],
-            own.at[r, :, pl.ds(start, width)],
-            move_recv.at[0, place],
-        )
-        copy.start()
-        group.append(copy)
-        start += width
+    line.begin()
     for copy in packed:
         copy.wait()
-
-    def piece_arrived(index):
-        @pl.when(index == 1)
-        def _():
-            for copy in group:
-                copy.wait()
-
-        for which in (1, 2, 3):
-
-            @pl.when(index == 1 + which * per)
-            def _():
-                for copy in moves[which - 1]:
-                    copy.wait_recv()
-
-    def slot(index):
-        step = (index + per - 1) // per - 1
-        turned = (r // 2 + step // 2) % 2 * 2 + (r % 2 + step % 2) % 2
-        return jnp.where(index == 0, 4, turned)
-
-    def strip_of(index):
-        return pl.multiple_of((index + per - 1) % per * CHUNK * jnp.where(index == 0, 0, 1), CHUNK)
-
-    def own_at(index, part):
-        return own.at[slot(index), pl.ds(part * half + strip_of(index), CHUNK), :]
-
-    def out_at(index, part):
-        return out.at[slot(index), pl.ds(part * half + strip_of(index), CHUNK), :]
-
-    def loop(first, last, body):
-        def run(index, nothing):
-            body(index)
-            return nothing
-
-        lax.fori_loop(first, last, run, 0)
-
+    line.ready()
     spread_out = [
         [
             remote(
@@ -1222,198 +1526,62 @@
                 small_recv.at[kind, 3 + 6 - step],
                 peer,
             )
-            for step, peer in enumerate(
-                [(z, (r + turn % 4) % 4, (c + turn // 4) % 2) for turn in range(1, 8)]
-            )
+            for step, peer in enumerate(plane)
         ]
         for kind, (source, target) in enumerate(((vec_sum, vec_in), (gain_sum, gain_in)))
     ]
-
-    def small_middle():
-        for kind in small:
-            for copy in kind:
-                copy.wait_recv()
-        vec_sum[...] = vec[...] + vec_z[0] + vec_z[1] + vec_z[2]
-        gain_sum[...] = gain[...] + gain_z[0] + gain_z[1] + gain_z[2]
-        for kind in spread_out:
-            for copy in kind:
-                copy.start()
-
-    gate_moves = []
-    for which, peer in enumerate((twin, side, cross)):
-        for part in (0, 1):
-            gate_moves.append(
-                remote(
-                    out.at[4, pl.ds(part * half, CHUNK), :],
-                    out_gates.at[r, part],
-                    small_send.at[0, 10 + 2 * which + part],
-                    small_recv.at[0, 10 + 2 * which + part],
-                    peer,
-                )
-            )
+    gate_moves = [
+        remote(
+            out.at[4, pl.ds(which * half, PACK), :],
+            out_gates.at[r, which],
+            small_send.at[0, 10 + 2 * place + which],
+            small_recv.at[0, 10 + 2 * place + which],
+            peer,
+        )
+        for place, peer in enumerate((twin, side, cross))
+        for which in (0, 1)
+    ]
     gate_local = [
         pltpu.make_async_copy(
-            out.at[4, pl.ds(part * half, CHUNK), :], out_gates.at[r, part], gate_sem.at[part]
+            out.at[4, pl.ds(which * half, PACK), :], out_gates.at[r, which], gate_sem.at[which]
         )
-        for part in (0, 1)
+        for which in (0, 1)
     ]
-
-    def gates_out():
-        for copy in gate_moves + gate_local:
+    load.wait()
+    pace = iter((4, 6))
+    total = reduce_shards(
+        copies, parts, *buffers, between=lambda: line.advance(next(pace))
+    )
+    size = mine.shape[0]
+
+    def body(at):
+        rows = pl.ds(at, STRIP)
+        mine[rows, :] = (resid_mid[rows, :] + total(at)).astype(jnp.bfloat16)
+
+    strips(size, body)
+    done = hand_out(copies, mine, output)
+    line.advance(6)
+    for kind in small:
+        for copy in kind:
+            copy.wait_recv()
+    vec_sum[...] = vec[...] + vec_z[0] + vec_z[1] + vec_z[2]
+    gain_sum[...] = gain[...] + gain_z[0] + gain_z[1] + gain_z[2]
+    for kind in spread_out:
+        for copy in kind:
             copy.start()
-
-    @pl.when(is_end)
-    def _():
-        low = z // 3
-        peer = (near_z, r, c)
-
-        def send_low(index):
-            return remote(
-                own_at(index, low),
-                left.at[index],
-                end_send.at[0, index],
-                low_recv.at[index],
-                peer,
-            )
-
-        def send_high(index):
-            return remote(
-                own_at(index, 1 - low),
-                right.at[1, index],
-                end_send.at[1, index],
-                high_recv.at[1, index],
-                peer,
-            )
-
-        def begin(index):
-            piece_arrived(index)
-            send_low(index).start()
-            send_high(index).start()
-
-        def end(index):
-            send_low(index).wait_send()
-            send_high(index).wait_send()
-            for part in (0, 1):
-                spot = out_at(index, part)
-                remote(
-                    spot, spot, end_send.at[0, index], out_recv.at[part, index], peer
-                ).wait_recv()
-
-        loop(0, chunks, begin)
-        small_middle()
-        loop(0, 1, end)
-        gates_out()
-        loop(1, chunks, end)
-
-    @pl.when(jnp.logical_not(is_end))
-    def _():
-        low = z - 1
-        other, outer = ((3 - z, r, c), (end_z, r, c))
-
-        def to_other(index):
-            return remote(
-                own_at(index, 1 - low),
-                right.at[0, index],
-                mid_send.at[index],
-                high_recv.at[0, index],
-                other,
-            )
-
-        def from_outer(index):
-            return remote(
-                own_at(index, 1 - low),
-                right.at[1, index],
-                mid_send.at[index],
-                high_recv.at[1, index],
-                outer,
-            )
-
-        def from_low(index):
-            return remote(
-                own_at(index, low), left.at[index], mid_send.at[index], low_recv.at[index], outer
-            )
-
-        def final(index):
-            mine = own_at(index, low)
-            spot = out_at(index, low)
-            return (
-                pltpu.make_async_copy(mine, spot, local.at[index]),
-                remote(mine, spot, first_send.at[index], out_recv.at[low, index], outer),
-                remote(mine, spot, last_send.at[index], out_recv.at[low, index], other),
-            )
-
-        def onward(index):
-            spot = out_at(index, 1 - low)
-            return remote(spot, spot, on_send.at[index], out_recv.at[1 - low, index], outer)
-
-        def rows_at(index, part):
-            return pl.ds(pl.multiple_of(part * half + strip_of(index), CHUNK), CHUNK)
-
-        def step(index):
-            @pl.when(index < chunks)
-            def _():
-                piece_arrived(index)
-                from_outer(index).wait_recv()
-                spot = rows_at(index, 1 - low)
-                total = own[slot(index), spot, :].astype(jnp.float32) + right[1, index].astype(
-                    jnp.float32
-                )
-                own[slot(index), spot, :] = total.astype(jnp.bfloat16)
-                to_other(index).start()
-
-            @pl.when((index >= 2) & (index < chunks + 2))
-            def _():
-                back = index - 2
-                from_low(back).wait_recv()
-                to_other(back).wait_recv()
-                spot = rows_at(back, low)
-                total = (
-                    own[slot(back), spot, :].astype(jnp.float32)
-                    + left[back].astype(jnp.float32)
-                    + right[0, back].astype(jnp.float32)
-                )
-                own[slot(back), spot, :] = total.astype(jnp.bfloat16)
-                for copy in final(back):
-                    copy.start()
-
-            @pl.when(index >= 4)
-            def _():
-                back = index - 4
-                onward(back).wait_recv()
-                onward(back).start()
-
-        def end(index):
-            to_other(index).wait_send()
-            _, first, last = final(index)
-            first.wait_send()
-            last.wait_send()
-            onward(index).wait_send()
-
-        def end_local(index):
-            final(index)[0].wait()
-
-        loop(0, 32, step)
-        small_middle()
-        end_local(0)
-        gates_out()
-        loop(32, chunks + 4, step)
-        loop(1, chunks, end_local)
-        loop(0, chunks, end)
-
+    line.advance(16)
+    line.settle(0, line.lead)
+    for copy in gate_moves + gate_local:
+        copy.start()
+    line.finish(line.lead)
+    done()
     for kind in spread_out:
         for copy in kind:
             copy.wait_recv()
-    out_gain[...] = (
-        gain_sum[...]
-        + gain_in[0]
-        + gain_in[1]
-        + gain_in[2]
-        + gain_in[3]
-        + gain_in[4]
-        + gain_in[5]
-        + gain_in[6]
-    )
-    out_vec[...] = jnp.zeros_like(out_vec)
+    gains = gain_sum[...]
+    for place in range(7):
+        gains = gains + gain_in[place]
+    out_gain[...] = gains
     out_vec[r] = vec_sum[...]
     for step in (0, 1, 2):
         out_vec[(r + 3 - step) % 4] = vec_in[6 - step]
@@ -1421,59 +1589,10 @@
         copy.wait_recv()
     for copy in gate_local:
         copy.wait()
-    for group in small + spread_out + moves + [gate_moves]:
+    for group in small + spread_out + [gate_moves]:
         for copy in group:
             copy.wait_send()
-
-
-def reduce_grads(sources, gates, vec, gain):
-    rows = sources[0].shape[0] // 4
-    width = sum(source.shape[1] for source in sources)
-    chunks = 4 * (rows // 2 // CHUNK) + 1
-    dma = pltpu.SemaphoreType.DMA
-    count = len(sources)
-    vmem = pl.BlockSpec(memory_space=pltpu.VMEM)
-    loose = pl.BlockSpec(memory_space=pl.ANY)
-    return pl.pallas_call(
-        functools.partial(reduce_kernel, count),
-        in_specs=[loose] * (count + 1) + [vmem, vmem],
-        out_specs=[loose, loose, vmem, vmem],
-        out_shape=[
-            jax.ShapeDtypeStruct((5, rows, width), jnp.bfloat16),
-            jax.ShapeDtypeStruct((4, 2, CHUNK, width), jnp.bfloat16),
-            jax.ShapeDtypeStruct((4, *vec.shape), jnp.float32),
-            jax.ShapeDtypeStruct(gain.shape, jnp.float32),
-        ],
-        scratch_shapes=[
-            pltpu.VMEM((5, rows, width), jnp.bfloat16),
-            pltpu.VMEM((chunks, CHUNK, width), jnp.bfloat16),
-            pltpu.VMEM((2, chunks, CHUNK, width), jnp.bfloat16),
-            pltpu.VMEM((3, *vec.shape), jnp.float32),
-            pltpu.VMEM((3, *gain.shape), jnp.float32),
-            pltpu.VMEM(vec.shape, jnp.float32),
-            pltpu.VMEM(gain.shape, jnp.float32),
-            pltpu.VMEM((7, *vec.shape), jnp.float32),
-            pltpu.VMEM((7, *gain.shape), jnp.float32),
-            dma((4, count)),
-            dma((4, count)),
-            dma((10,)),
-            dma((2, 16)),
-            dma((2, 16)),
-            dma((2, chunks)),
-            dma((chunks,)),
-            dma((2, chunks)),
-            dma((2, chunks)),
-            dma((chunks,)),
-            dma((chunks,)),
-            dma((chunks,)),
-            dma((chunks,)),
-            dma((chunks,)),
-        ],
-        compiler_params=pltpu.CompilerParams(
-            collective_id=REDUCE_ID, has_side_effects=True, vmem_limit_bytes=VMEM_BYTES
-        ),
-        name="reduce_grads",
-    )(*sources, gates, vec, gain)
+    copies.finish()
 
 
 def dot(left, right, dims, kind=jnp.float32):
@@ -1553,8 +1672,6 @@
 
     rec_w, in_w = (diagonal(rec_gate_w), diagonal(in_gate_w))
     size = tokens // 8
-    shard = token_shard(r, c) * size
-    resid = lax.dynamic_slice_in_dim(x_all, shard, size, 0)
     full = jax.ShapeDtypeStruct((tokens, model), low)
     part = jax.ShapeDtypeStruct((size, model), jnp.float32)
     line = jax.ShapeDtypeStruct((1, model), jnp.float32)
@@ -1594,7 +1711,6 @@
         80,
         (cotangent.T, *weights),
     )
-    cot = lax.dynamic_slice_in_dim(c_all, shard, size, 0)
     gate = dot(normed_mlp, gate_w, CONTRACT_PLAIN)
     up = dot(normed_mlp, up_w, CONTRACT_PLAIN)
     d_activ = dot(c_all, down_w, CONTRACT_PLAIN)
@@ -1605,36 +1721,54 @@
     d_normed = lax.dot_general(
         d_gate, gate_w, CONTRACT_COLS, preferred_element_type=jnp.float32
     ) + lax.dot_general(d_up, up_w, CONTRACT_COLS, preferred_element_type=jnp.float32)
-    d_branch, d_resid, grad_mlp_gain = vmem_call(
+    def kind_of(array):
+        return pltpu.VMEM(array.shape, array.dtype)
+
+    def like(array):
+        return jax.ShapeDtypeStruct(array.shape, array.dtype)
+
+    both = jax.ShapeDtypeStruct((tokens, 2 * rec), low)
+    held = (pre, x_pre, conv, rec_gate, in_gate, states)
+    d_branch, d_pre, d_gates, grad_in, grads_mlp, sums, grad_mlp_gain, grad_mix_gain = vmem_call(
         backward_kernel,
-        "backward_norm",
+        "backward",
         BACKWARD_ID,
-        (d_normed.astype(low), resid_mid, cot, gain_mlp),
-        [full, part, line],
-        [pl.ANY, pltpu.VMEM, pltpu.VMEM],
-        reduce_scratch(size, model) + [piece],
-        24,
-    )
-    d_mixed = dot(d_branch, out_w, CONTRACT_COLS)
-    d_pre, d_gates, sums = mixer_backward(
-        d_mixed, pre, masks, vec, rec_w, in_w, x_pre, conv, rec_gate, in_gate, states
-    )
-    grad_in, output, grad_mix_gain = vmem_call(
-        finish_kernel,
-        "finish_norm",
-        FINISH_ID,
+        (resid_mid, gain_mlp, gain_mix, masks, vec, rec_w, in_w, mix_w, out_w),
+        [
+            full,
+            both,
+            both,
+            block,
+            jax.ShapeDtypeStruct((4, depth, 2 * width), low),
+            jax.ShapeDtypeStruct((16, rec), jnp.float32),
+            line,
+            line,
+        ],
+        [pl.ANY] * 5 + [pltpu.VMEM] * 3,
+        line_scratch(2, depth, 2 * width, BACK_CHUNK, 0)
+        + [
+            kind_of(full),
+            piece,
+            piece,
+            kind_of(full),
+            kind_of(part),
+            kind_of(both),
+            kind_of(both),
+            pltpu.VMEM((24, rec), jnp.float32),
+            row8,
+        ]
+        + [kind_of(item) for item in held]
+        + reduce_scratch(size, model)
+        + [piece, pltpu.SemaphoreType.DMA((9,))],
+        60,
         (
-            dot(d_pre, mix_w, CONTRACT_COLS, low),
-            dot(activ, down_w, CONTRACT_COLS, low),
-            resid,
-            resid_mid,
-            d_resid,
-            gain_mix,
+            d_normed.astype(low),
+            c_all,
+            x_all,
+            *held,
+            dot(normed_mlp, d_gate, CONTRACT_ROWS, low),
+            dot(normed_mlp, d_up, CONTRACT_ROWS, low),
         ),
-        [block, block, line],
-        [pltpu.VMEM] * 3,
-        reduce_scratch(size, model) * 2 + [piece, piece],
-        40,
     )
     gate_grads = dot(conv, d_gates, CONTRACT_ROWS, low)
     gates = jnp.concatenate(
@@ -1645,42 +1779,70 @@
         ],
         axis=1,
     )
-    grads, gates, vec_sums, gains = reduce_grads(
+    gain_grads = jnp.concatenate([grad_mix_gain, grad_mlp_gain], axis=0)
+    final_width = width + 2 * rec + padded
+    dma = pltpu.SemaphoreType.DMA
+    grads, gates, output, vec_sums, gains = vmem_call(
+        functools.partial(reduce_kernel, 3),
+        "reduce_grads",
+        REDUCE_ID,
+        (resid_mid, sums, gain_grads),
+        [
+            jax.ShapeDtypeStruct((5, depth, final_width), low),
+            jax.ShapeDtypeStruct((4, 2, PACK, final_width), low),
+            block,
+            jax.ShapeDtypeStruct((4, *sums.shape), jnp.float32),
+            like(gain_grads),
+        ],
+        [pl.ANY] * 3 + [pltpu.VMEM] * 2,
+        line_scratch(3, depth, final_width, LAST_CHUNK, PACK // LAST_CHUNK)
+        + [
+            pltpu.VMEM((3, *sums.shape), jnp.float32),
+            pltpu.VMEM((3, *gain_grads.shape), jnp.float32),
+            kind_of(sums),
+            kind_of(gain_grads),
+            pltpu.VMEM((7, *sums.shape), jnp.float32),
+            pltpu.VMEM((7, *gain_grads.shape), jnp.float32),
+            kind_of(full),
+        ]
+        + reduce_scratch(size, model)
+        + [piece, dma((9,)), dma((2, 16)), dma((2, 16))],
+        40,
         (
-            dot(normed_mlp, d_gate, CONTRACT_ROWS, low),
-            dot(normed_mlp, d_up, CONTRACT_ROWS, low),
+            dot(activ, down_w, CONTRACT_COLS, low),
+            gates,
             dot(c_all, activ, CONTRACT_ROWS, low),
             dot(normed_mix, d_pre, CONTRACT_ROWS, low),
             dot(d_branch, mixed, CONTRACT_ROWS, low),
         ),
-        gates,
-        sums,
-        jnp.concatenate([grad_mix_gain, grad_mlp_gain], axis=0),
-    )
-    gates = gates[:, :, :, : 5 * 4 * head].reshape(4, 2, CHUNK, 5, 2, heads, head)
-    gates = gates.transpose(4, 0, 5, 1, 3, 2, 6).reshape(2, 4 * heads, head, head)
-    gates = gates.astype(jnp.float32)
+    )
+    tiles = [[], [], [], [], []]
+    for tile, first, length, which, spot in gate_tiles(2 * heads * head):
+        tiles[tile].append(gates[:, which, :, spot : spot + length])
+    gates = jnp.concatenate([jnp.concatenate(item, axis=2) for item in tiles], axis=1)
+    gates = gates.reshape(4, head, 2, heads, head).transpose(2, 0, 3, 1, 4)
+    gates = gates.reshape(2, 4 * heads, head, head).astype(jnp.float32)
     vec_sums = vec_sums.transpose(1, 0, 2).reshape(vec_sums.shape[1], 4 * rec)
     gains = lax.dynamic_slice_in_dim(gains, r * depth, depth, 1)
 
-    def columns(first, length):
+    def columns(array, first, length):
         return jnp.concatenate(
-            [grads[i, :, first : first + length] for i in range(4)], axis=1
+            [array[i, :, first : first + length] for i in range(4)], axis=1
         ).astype(jnp.float32)
 
-    after = 3 * width
+    after = width
     grad_out = jnp.concatenate(
         [grads[i, :, after + 2 * rec : after + 3 * rec].T for i in range(4)], axis=0
     ).astype(jnp.float32)
     return (
         output.T,
         grad_in.astype(jnp.float32).T,
-        columns(after, rec),
-        columns(after + rec, rec),
+        columns(grads, after, rec),
+        columns(grads, after + rec, rec),
         grad_out,
-        columns(0, width),
-        columns(width, width),
-        columns(2 * width, width),
+        columns(grads_mlp, 0, width),
+        columns(grads_mlp, width, width),
+        columns(grads, 0, width),
         gains[0],
         gains[1],
         vec_sums[0],

time: 790 us -> 700 us (0.89)
  Pallas kernels: 627 us -> 566 us
  local copies, waits for them, and re-layouts: 63.2 us -> 46.9 us
    pallas_call x2 -> x0, Pallas kernels: 347 us -> none  [the longest x1 335 us: reduce_grads(): pl.pallas_call(functools.partial(reduce_kernel, count), in_specs=[loose]...]
    pallas_call x3, Pallas kernels: 229 us -> 515 us  [vmem_call(): pl.pallas_call(kernel, in_specs=[pl.BlockSpec(memory_space=pltpu.VMEM)] *...]
    dot_general x12 -> x10, matrix products: 54.3 us -> 46.9 us  [dot(): lax.dot_general(left, right, dims, preferred_element_type=jnp.float32)]
where the time goes in v3:
time: 700 us; the launch traced here: 691 us
  Pallas kernels  566 us (81%)
  matrix products  55.4 us (8%)
  local copies, waits for them, and re-layouts  46.9 us (7%)
  other arithmetic  21.2 us (3%)
    pallas_call x3, Pallas kernels, vmem_call(): pl.pallas_call(kernel, in_specs=[pl.BlockSpec(memory_space=pltpu.VMEM)] *...  515 us
    pallas_call x1, Pallas kernels, gather(): pl.pallas_call(gather_kernel, in_specs=[pl.BlockSpec(memory_space=pl.ANY)...  51.1 us
    dot_general x10, matrix products, dot(): lax.dot_general(left, right, dims, preferred_element_type=jnp.float32)  46.9 us
    unnamed x69, local copies, waits for them, and re-layouts  15 us

profile of v3, /device:TPU:0, one launch (start us, length us, event | category | flops | bytes accessed | tf_op | source)
XLA Modules:
  0.0 691.4 jit_solution(12189578559757651041)
XLA Ops:
  0.7 1.6 copy.63
  2.3 0.9 copy.65
  3.1 2.4 copy.64
  5.6 1.8 copy.66
  7.4 2.5 maximum_bitcast_fusion.mix_in
  9.9 2.0 copy.62
  12.0 0.6 pad.19.s_in
  12.6 0.6 pad_maximum_fusion.3.g_in
  13.2 51.1 %gather.1 = (bf16[1024,2048]{1,0:T(8,128)(2,1)}, f32[4,8,128]{2,1,0:T(8,128)}, f32[2,2048]{1,0:T(2,128)}, bf16[2048,640]{1,0:T(8,128)(2,1)}, bf16[320,2048]{1,0:T(8,128)(2,1)}) custom-call(bf16[512,512]{1,0:T(8,128)(2,1)} %bitcast.131, f32[8,128]{1,0:T(8,128)} %pad.19.s_in, f32[2,512]{1,0:T(2,128)} %pad_maximum_fusion.3.g_in, ...), custom_call_target="tpu_custom_call" | custom-call | tf_op jit(solution)/shard_map/gather/pallas_call | solution.py:730
  64.3 0.7 broadcast_subtract_fusion
  65.2 1.0 copy.68.masks
  66.2 1.0 dynamic-slice_bitcast_fusion.1
  67.3 0.8 fusion.4.rec_w
  68.1 0.8 fusion.5.in_w
  69.1 0.7 constant_dynamic-slice_fusion.1.vec
  69.8 1.4 fusion.12
  71.2 1.0 copy.67
  72.2 120.4 %forward.1 = (bf16[1024,2048]{1,0:T(8,128)(2,1)}, f32[128,2048]{1,0:T(8,128)}, bf16[1024,2048]{1,0:T(8,128)(2,1)}, bf16[2048,768]{1,0:T(8,128)(2,1)}, bf16[2048,...) custom-call(bf16[1024,2048]{1,0:T(8,128)(2,1)} %get-tuple-element.51, ...), custom_call_target="tpu_custom_call" | custom-call | tf_op jit(solution)/shard_map/forward/pallas_call | solution.py:951
  192.7 6.7 fusion.13
  199.5 3.4 fusion.14
  202.9 5.1 multiply_convert_fusion
  208.1 5.0 convolution_convert_fusion.2.refs_10_
  213.1 5.1 convolution_convert_fusion.3.refs_9_
  218.2 3.4 fusion.15
  221.7 5.0 add_convert_fusion.refs_0_
  226.7 192.7 %backward.1 = (bf16[1024,2048]{1,0:T(8,128)(2,1)}, bf16[1024,640]{1,0:T(8,128)(2,1)}, bf16[1024,640]{1,0:T(8,128)(2,1)}, bf16[512,512]{1,0:T(8,128)(2,1)}, bf16[...) custom-call(f32[128,2048]{1,0:T(8,128)} %get-tuple-element.56.resid_mid, ...), custom_call_target="tpu_custom_call" | custom-call | tf_op jit(solution)/shard_map/backward/pallas_call | solution.py:951
  419.4 5.9 convolution_convert_fusion.5.refs_4_
  425.3 5.0 convolution_convert_fusion.4.refs_3_
  430.3 4.9 convolution_convert_fusion.1.refs_2_
  435.2 0.7 convolution_convert_fusion.6
  436.1 0.8 pad_maximum_fusion.refs_1_
  437.1 5.0 convolution_convert_fusion.refs_0_
  442.1 0.6 pad_maximum_fusion.2.gain
  442.7 202.1 %reduce_grads.1 = (bf16[5,512,1792]{2,1,0:T(8,128)(2,1)}, bf16[4,2,32,1792]{3,2,1,0:T(8,128)(2,1)}, bf16[512,512]{1,0:T(8,128)(2,1)}, f32[4,16,320]{2,1,0:T(8,128)}, f32[2,2048]{1,0:T(2,128)}) custom-call(f32[128,2048]{1,0:T(8,128)} %get-tuple-element.56.resid_mid, f32[16,320]{1,0:T(8,128)} %get-tuple-element.68.vec, f32[2,2048]{1,0:T(2,128)} %pad_maximum_fusion.2.gain, ...), custom_call_target="tpu_custom_call" | custom-call | tf_op jit(solution)/shard_map/reduce_grads/pallas_call | solution.py:951
  644.8 0.9 slice_bitcast_fusion.24
  645.8 0.8 slice_bitcast_fusion.25
  646.8 1.2 fusion.9
  649.9 0.9 convert_bitcast_fusion
  650.8 1.0 fusion.8
  651.8 1.2 copy.71
  653.0 1.2 copy.72
  654.2 1.2 copy-done
  655.6 3.6 maximum_convert_fusion.2
  659.2 1.4 slice-done.1
  660.6 0.4 slice_bitcast_fusion.7
  661.0 3.1 maximum_convert_fusion.1
  664.1 3.1 maximum_convert_fusion
  667.2 2.2 slice_bitcast_fusion.12
  669.4 2.8 concatenate.82
  672.1 1.9 copy.75
  674.0 2.6 concatenate.81
  676.7 1.7 convert_element_type.83
  678.3 2.2 concatenate.80
  680.5 1.7 convert_element_type.82
  682.2 1.0 copy.73
  683.2 0.7 slice.215
  684.0 0.7 squeeze.154
  684.7 0.7 squeeze.155
  685.4 0.7 squeeze.156
  686.1 0.7 squeeze.161
  686.7 0.7 squeeze.162
  687.4 0.7 squeeze.163
  688.1 1.4 fusion.11
  689.6 1.3 copy.74
  (89 shorter events, 3.4 us)
Async XLA Ops:
  7.4 4.6 copy-start.18
  7.4 5.2 copy-start.16
  7.4 5.1 copy-start.17
  13.2 55.7 %copy-start.8 = (f32[1280]{0:T(1024)S(1)}, f32[1280]{0:T(1024)}, u32[]{:S(2)}) copy-start(f32[1280]{0:T(1024)} %param.39) | copy-start | bytes 15364
  13.2 55.7 %copy-start.9 = (f32[1280]{0:T(1024)S(1)}, f32[1280]{0:T(1024)}, u32[]{:S(2)}) copy-start(f32[1280]{0:T(1024)} %param.31) | copy-start | bytes 15364
  13.2 55.7 %copy-start.10 = (f32[1280]{0:T(1024)S(1)}, f32[1280]{0:T(1024)}, u32[]{:S(2)}) copy-start(f32[1280]{0:T(1024)} %param.32) | copy-start | bytes 15364
  13.2 55.8 %copy-start.11 = (f32[1280]{0:T(1024)S(1)}, f32[1280]{0:T(1024)}, u32[]{:S(2)}) copy-start(f32[1280]{0:T(1024)} %param.34) | copy-start | bytes 15364
  13.2 55.8 %copy-start.12 = (f32[1280]{0:T(1024)S(1)}, f32[1280]{0:T(1024)}, u32[]{:S(2)}) copy-start(f32[1280]{0:T(1024)} %param.37) | copy-start | bytes 15364
  13.2 55.8 %copy-start.13 = (f32[1280]{0:T(1024)S(1)}, f32[1280]{0:T(1024)}, u32[]{:S(2)}) copy-start(f32[1280]{0:T(1024)} %param.38) | copy-start | bytes 15364
  13.2 55.8 %copy-start.7 = (f32[4,1280]{1,0:T(4,128)S(1)}, f32[4,1280]{1,0:T(4,128)}, u32[]{:S(2)}) copy-start(f32[4,1280]{1,0:T(4,128)} %param.33) | copy-start | bytes 61444
  13.2 58.0 %copy-start.4 = (bf16[512,512]{1,0:T(8,128)(2,1)S(1)}, bf16[512,512]{1,0:T(8,128)(2,1)}, u32[]{:S(2)}) copy-start(bf16[512,512]{1,0:T(8,128)(2,1)} %param.21) | copy-start | bytes 1572868
  192.7 6.8 copy-start.20
  192.7 6.8 copy-start.23
  199.5 3.4 copy-start.22
  226.7 192.7 %copy-start.26 = (bf16[1024,384]{1,0:T(8,128)(2,1)S(1)}, bf16[1024,384]{1,0:T(8,128)(2,1)}, u32[]{:S(2)}) copy-start(bf16[1024,384]{1,0:T(8,128)(2,1)} %get-tuple-element.75) | copy-start | bytes 2359300
  419.4 5.9 copy-start.19
  419.4 5.9 copy-start.25
  425.3 5.0 copy-start.1
  430.3 4.9 copy-start.2
  430.3 4.9 copy-start.24
  435.2 1.9 copy-start.21
  437.1 5.0 copy-start.14
  437.1 5.0 copy-start.15
  650.8 4.6 copy-start
  655.4 3.8 slice-start
  655.6 5.0 slice-start.1
  678.3 3.9 copy-start.5
  680.5 2.7 copy-start.6
  680.5 9.0 %copy-start.3 = (bf16[512,512]{1,0:T(8,128)(2,1)S(1)}, bf16[512,512]{1,0:T(8,128)(2,1)}, u32[]{:S(2)}) copy-start(bf16[512,512]{1,0:T(8,128)(2,1)} %get-tuple-element.77) | copy-start | bytes 1572868

commit v4 on v3

--- a/solution.py
+++ b/solution.py
@@ -329,7 +329,7 @@
     )
 
 
-GATHER_ID, FORWARD_ID, BACKWARD_ID, REDUCE_ID = (0, 1, 2, 3)
+GATHER_ID, FORWARD_ID, BACKWARD_ID = (0, 1, 2)
 BLOCK = 128
 VMEM_BYTES = 60 << 20
 
@@ -967,6 +967,8 @@
 DEPTH = 4
 HAND_LAG = 4
 LAG = 6
+RING = 16
+SEGMENTS = 2
 
 
 def run_loop(first, last, body):
@@ -989,10 +991,9 @@
 
 
 class Line:
-    def __init__(self, sources, own, left, right, out, sems, lead):
+    def __init__(self, own, left, right, out, sems, lead):
         self.own, self.left, self.right, self.out, self.lead = (own, left, right, out, lead)
         (
-            self.load_sem,
             self.end_send,
             self.low_recv,
             self.high_recv,
@@ -1008,7 +1009,8 @@
         self.rows = out.shape[1]
         self.half = self.rows // 2
         self.per = self.half // self.chunk
-        self.chunks = 4 * self.per + lead
+        self.first = 4 * self.per
+        self.chunks = 4 * SEGMENTS * self.per + lead
         self.total = self.chunks + LAG
         self.at = 0
         self.ahead = 0
@@ -1016,66 +1018,54 @@
         self.near_z = (jnp.where(z == 0, 1, 2), r, c)
         self.outer = (jnp.where(z == 1, 0, 3), r, c)
         self.other = (3 - z, r, c)
-        self.loads = []
-        start = 0
-        for place, source in enumerate(sources):
-            width = source.shape[1]
-            self.loads.append(
-                pltpu.make_async_copy(
-                    source,
-                    own.at[pl.ds(0, 4 * self.rows), pl.ds(start, width)],
-                    self.load_sem.at[place],
-                )
-            )
-            start += width
+
+    def extra(self, index):
+        return (index >= self.first) & (index < self.first + self.lead)
 
     def spot(self, index):
-        step = (index - self.lead + self.per) // self.per - 1
-        strip = (index - self.lead + self.per) % self.per
-        if self.lead:
-            strip = strip - jnp.where(step < 0, self.per - self.lead, 0)
-        return (step, strip)
+        later = index >= self.first + self.lead
+        plain = index - jnp.where(later, self.lead, 0)
+        step = jnp.where(self.extra(index), 0, plain // self.per)
+        strip = jnp.where(self.extra(index), index - self.first, plain % self.per)
+        return (step // 4, step % 4, strip)
 
     def peer_row(self, index):
         r = here()[1]
-        step = jnp.maximum(self.spot(index)[0], 0)
+        step = self.spot(index)[1]
         return (r // 2 + step // 2) % 2 * 2 + (r % 2 + step % 2) % 2
 
     def stays(self, index):
-        return self.spot(index)[0] <= 0
+        return self.spot(index)[1] == 0
 
     def span(self, index, which):
-        step, strip = self.spot(index)
-        start = self.peer_row(index) * self.rows + which * self.half
-        if self.lead:
-            start = jnp.where(
-                step < 0, 4 * self.rows + which * self.lead * self.chunk, start
-            )
+        segment, _, strip = self.spot(index)
+        start = (segment * 4 + self.peer_row(index)) * self.rows + which * self.half
+        outside = SEGMENTS * 4 * self.rows + which * self.lead * self.chunk
+        start = jnp.where(self.extra(index), outside, start)
         return pl.ds(pl.multiple_of(start + strip * self.chunk, self.chunk), self.chunk)
 
     def own_at(self, index, which):
         return self.own.at[self.span(index, which), :]
 
     def out_at(self, index, which, row):
-        step, strip = self.spot(index)
-        if self.lead:
-            row = jnp.where(step < 0, 4, row)
+        segment, _, strip = self.spot(index)
+        place = jnp.where(self.extra(index), 4 * SEGMENTS, segment * 4 + row)
         start = pl.multiple_of(which * self.half + strip * self.chunk, self.chunk)
-        return self.out.at[row, pl.ds(start, self.chunk), :]
+        return self.out.at[place, pl.ds(start, self.chunk), :]
 
     def end_sends(self, index):
         low = here()[0] // 3
         return (
             remote(
                 self.own_at(index, low),
-                self.left.at[index],
+                self.left.at[index % RING],
                 self.end_send.at[0, index],
                 self.low_recv.at[index],
                 self.near_z,
             ),
             remote(
                 self.own_at(index, 1 - low),
-                self.right.at[1, index],
+                self.right.at[1, index % RING],
                 self.end_send.at[1, index],
                 self.high_recv.at[1, index],
                 self.near_z,
@@ -1086,7 +1076,7 @@
         low = here()[0] - 1
         return remote(
             self.own_at(index, 1 - low),
-            self.right.at[0, index],
+            self.right.at[0, index % RING],
             self.mid_send.at[index],
             self.high_recv.at[0, index],
             self.other,
@@ -1097,14 +1087,14 @@
         return (
             remote(
                 self.own_at(index, low),
-                self.left.at[index],
+                self.left.at[index % RING],
                 self.mid_send.at[index],
                 self.low_recv.at[index],
                 self.outer,
             ),
             remote(
                 self.own_at(index, 1 - low),
-                self.right.at[1, index],
+                self.right.at[1, index % RING],
                 self.mid_send.at[index],
                 self.high_recv.at[1, index],
                 self.outer,
@@ -1143,6 +1133,13 @@
             spot, spot, self.on_send.at[index], self.out_recv.at[1 - low, index], self.outer
         )
 
+    def came_back(self, index):
+        for which in (0, 1):
+            spot = self.out_at(index, which, self.peer_row(index))
+            remote(
+                spot, spot, self.end_send.at[0, index], self.out_recv.at[which, index], self.near_z
+            ).wait_recv()
+
     def end_step(self, index):
         @pl.when(index < self.chunks)
         def _():
@@ -1151,6 +1148,10 @@
                 for copy in self.end_sends(index - DEPTH):
                     copy.wait_send()
 
+            @pl.when(index >= RING)
+            def _():
+                self.came_back(index - RING)
+
             for copy in self.end_sends(index):
                 copy.start()
 
@@ -1161,7 +1162,7 @@
         def _():
             self.from_outer(index)[1].wait_recv()
             span = self.span(index, 1 - low)
-            total = own[span, :].astype(jnp.float32) + right[1, index].astype(jnp.float32)
+            total = own[span, :].astype(jnp.float32) + right[1, index % RING].astype(jnp.float32)
             own[span, :] = total.astype(jnp.bfloat16)
             self.to_other(index).start()
 
@@ -1173,8 +1174,8 @@
             span = self.span(back, low)
             total = (
                 own[span, :].astype(jnp.float32)
-                + left[back].astype(jnp.float32)
-                + right[0, back].astype(jnp.float32)
+                + left[back % RING].astype(jnp.float32)
+                + right[0, back % RING].astype(jnp.float32)
             )
             own[span, :] = total.astype(jnp.bfloat16)
 
@@ -1207,14 +1208,6 @@
             copy.wait_recv()
             copy.start()
 
-    def begin(self):
-        for copy in self.loads:
-            copy.start()
-
-    def ready(self):
-        for copy in self.loads:
-            copy.wait()
-
     def advance(self, count):
         first, last = (self.at, min(self.at + count, self.total))
         self.at = last
@@ -1250,11 +1243,9 @@
             for copy in self.end_sends(index):
                 copy.wait_send()
 
-        for which in (0, 1):
-            spot = self.out_at(index, which, self.peer_row(index))
-            remote(
-                spot, spot, self.end_send.at[0, index], self.out_recv.at[which, index], self.near_z
-            ).wait_recv()
+        @pl.when(index >= self.chunks - RING)
+        def _():
+            self.came_back(index)
 
     def mid_done(self, index):
         self.to_other(index).wait_send()
@@ -1267,28 +1258,25 @@
             copy.wait_send()
         self.onward(index).wait_send()
 
-    def settle(self, first, last):
+    def finish(self):
+        self.advance(self.total)
+
         @pl.when(self.is_end)
         def _():
-            run_loop(first, last, self.end_done)
+            run_loop(0, self.chunks, self.end_done)
 
         @pl.when(jnp.logical_not(self.is_end))
         def _():
-            run_loop(first, last, self.mid_done)
-
-    def finish(self, first):
-        self.advance(self.total)
-        self.settle(first, self.chunks)
-
-
-def line_scratch(count, rows, width, chunk, lead):
+            run_loop(0, self.chunks, self.mid_done)
+
+
+def line_scratch(rows, width, chunk, lead):
     dma = pltpu.SemaphoreType.DMA
-    chunks = 4 * (rows // 2 // chunk) + lead
+    chunks = 4 * SEGMENTS * (rows // 2 // chunk) + lead
     return [
-        pltpu.VMEM((4 * rows + 2 * lead * chunk, width), jnp.bfloat16),
-        pltpu.VMEM((chunks, chunk, width), jnp.bfloat16),
-        pltpu.VMEM((2, chunks, chunk, width), jnp.bfloat16),
-        dma((count,)),
+        pltpu.VMEM((4 * SEGMENTS * rows + 2 * lead * chunk, width), jnp.bfloat16),
+        pltpu.VMEM((RING, chunk, width), jnp.bfloat16),
+        pltpu.VMEM((2, RING, chunk, width), jnp.bfloat16),
         dma((2, chunks)),
         dma((chunks,)),
         dma((2, chunks)),
@@ -1301,10 +1289,11 @@
     ]
 
 
-LINE_REFS = 13
+LINE_REFS = 12
 PACK = 32
-BACK_CHUNK = 32
-LAST_CHUNK = 16
+CHUNK = 16
+PACE = (6, 6, 6, 2, 2, 4, 6, 6, 8)
+BLOCK_STEPS = 2
 
 
 def z_peers():
@@ -1339,55 +1328,89 @@
     return done
 
 
+def gate_tiles(width):
+    tiles = []
+    for tile in range(5):
+        first, rest = (0, width)
+        if tile < 4:
+            tiles.append((tile, 0, width, tile // 2, tile % 2 * width))
+        else:
+            tiles.append((tile, 0, 384, 0, 2 * width))
+            tiles.append((tile, 384, width - 384, 1, 2 * width))
+    return tiles
+
+
 def backward_kernel(resid_mid, gain, gain_mix, masks, vec, rec_w, in_w, mix_w, out_w, *refs):
-    parts_in, c_all, x_all, *kept_in = refs[:9]
-    sources, outs, scratch = (refs[9:11], refs[11:19], refs[19:])
-    branch_out, d_pre_out, d_gates_out, grad, grads, sums, gain_grad, gain_mix_grad = outs
+    parts_in, out_parts, c_all, x_all, *kept_in = refs[:12]
+    gate_grad, up_grad, down_grad = refs[12:15]
+    grad, output, grads, out_gates, out_vec, out_gain = refs[15:21]
+    scratch = refs[21:]
     line_refs, scratch = (scratch[:LINE_REFS], scratch[LINE_REFS:])
     parts, cot, resid, branch, d_resid, d_pre, d_gates, edge, carry = scratch[:9]
-    kept, scratch = (scratch[9:15], scratch[15:])
-    *buffers, mine, load_sem, send, recv = scratch
-    pre, x_pre, conv, rec_gate, in_gate, states = kept
+    kept, scratch = (scratch[9:17], scratch[17:])
+    sums, gains, vec_z, gain_z, vec_sum, gain_sum, vec_in, gain_in = scratch[:8]
+    *buffers, mine, mine_out, load_sem, gate_sem, small_send, small_recv, free, send, recv = scratch[8:]
+    normed, pre, mixed, x_pre, conv, rec_gate, in_gate, states = kept
     z, r, c = here()
-    greet([*near(), (z, flip(across(r)), c), *z_peers()])
+    twin, side, top = near()
+    cross = (z, flip(across(r)), c)
+    lines, plane = (z_peers(), plane_peers())
+    greet(lines + plane)
     copies = Copies(send, recv)
+    line = Line(*line_refs[:3], grads, line_refs[3:], PACK // CHUNK)
+    own, half, rows_all = (line.own, line.half, 4 * line.rows)
     size = mine.shape[0]
     shard = part(token_shard(r, c), size, size)
+    width, ff = (x_pre.shape[1], gate_grad.shape[1])
+    head, rest = (own.shape[1] - 2 * ff, 3 * ff - own.shape[1])
+    first, second = (pl.ds(0, rows_all), pl.ds(rows_all, rows_all))
     loads = [
         pltpu.make_async_copy(source, target, load_sem.at[place])
         for place, (source, target) in enumerate(
             zip(
-                [parts_in, c_all.at[shard, :], x_all.at[shard, :], *kept_in],
-                [parts, cot, resid, *kept],
+                [
+                    parts_in,
+                    gate_grad,
+                    up_grad,
+                    down_grad.at[:, pl.ds(0, head)],
+                    down_grad.at[:, pl.ds(head, rest)],
+                    c_all.at[shard, :],
+                    x_all.at[shard, :],
+                    *kept_in,
+                ],
+                [
+                    parts,
+                    own.at[first, pl.ds(0, ff)],
+                    own.at[first, pl.ds(ff, ff)],
+                    own.at[first, pl.ds(2 * ff, head)],
+                    own.at[second, pl.ds(0, rest)],
+                    cot,
+                    resid,
+                    *kept,
+                ],
             )
         )
     ]
-    loads[0].start()
-    line = Line(sources, *line_refs[:3], grads, line_refs[3:], 0)
-    line.begin()
-    for copy in loads[1:]:
+    for copy in loads:
         copy.start()
-    gain_grad[...] = jnp.zeros_like(gain_grad)
-    gain_mix_grad[...] = jnp.zeros_like(gain_mix_grad)
-    sums[...] = jnp.zeros_like(sums)
-    edge[...] = jnp.zeros_like(edge)
-    carry[...] = jnp.zeros_like(carry)
-    loads[0].wait()
-    line.ready()
-    pace = iter((4, 4, 4, 2, 2, 2, 4))
+    for ref in (gains, sums, edge, carry):
+        ref[...] = jnp.zeros_like(ref)
+    for copy in loads[:4]:
+        copy.wait()
+    pace = iter(PACE)
 
     def between():
         line.advance(next(pace))
 
     total = reduce_shards(copies, parts, *buffers, between=between)
-    for copy in loads[1:]:
+    for copy in loads[4:]:
         copy.wait()
 
     def body(at):
         rows = pl.ds(at, STRIP)
         values, piece = norm_pull(resid_mid[rows, :], gain[...], total(at))
         values = values + cot[rows, :].astype(jnp.float32)
-        gain_grad[...] += piece
+        gains[1:2, :] += piece
         d_resid[rows, :] = values
         mine[rows, :] = values.astype(jnp.bfloat16)
 
@@ -1395,7 +1418,6 @@
     spread_rows(copies, mine, branch, between)
     copies.finish()
     last = branch.shape[0] // BLOCK - 1
-    width = x_pre.shape[1]
 
     def block(index, base):
         start = pl.multiple_of((last - index) * BLOCK, BLOCK)
@@ -1426,20 +1448,12 @@
         parts[rows, :] = lax.dot_general(
             d_pre[rows, :], mix_w[...], CONTRACT_COLS, preferred_element_type=jnp.float32
         ).astype(jnp.bfloat16)
-
-        line.one(base + index)
+        for step in range(BLOCK_STEPS):
+            line.one(base + BLOCK_STEPS * index + step)
         return base
 
     lax.fori_loop(0, last + 1, block, line.at)
-    line.skip(last + 1)
-    keeping = [
-        pltpu.make_async_copy(source, target, load_sem.at[place])
-        for place, (source, target) in enumerate(
-            ((branch, branch_out), (d_pre, d_pre_out), (d_gates, d_gates_out))
-        )
-    ]
-    for copy in keeping:
-        copy.start()
+    line.skip(BLOCK_STEPS * (last + 1))
     total_back = reduce_shards(copies, parts, *buffers, between=between)
 
     def body_back(at):
@@ -1447,56 +1461,16 @@
         values, piece = norm_pull(
             resid[rows, :].astype(jnp.float32), gain_mix[...], total_back(at)
         )
-        gain_mix_grad[...] += piece
+        gains[0:1, :] += piece
         mine[rows, :] = (d_resid[rows, :] + values).astype(jnp.bfloat16)
 
     strips(size, body_back)
-    done = hand_out(copies, mine, grad)
-    line.finish(0)
-    done()
-    for copy in keeping:
-        copy.wait()
+    for peer in (twin, side, top):
+        pl.semaphore_signal(free, inc=1, device_id=peer, device_id_type=MESH)
     copies.finish()
-
-
-def gate_tiles(width):
-    tiles = []
-    for tile in range(5):
-        first, rest = (0, width)
-        if tile < 4:
-            tiles.append((tile, 0, width, tile // 2, tile % 2 * width))
-        else:
-            tiles.append((tile, 0, 512, 0, 2 * width))
-            tiles.append((tile, 512, width - 512, 1, 2 * width))
-    return tiles
-
-
-def reduce_kernel(count, resid_mid, vec, gain, *refs):
-    parts_in, gates, sources = (refs[0], refs[1], refs[2 : 2 + count])
-    out, out_gates, output, out_vec, out_gain = refs[2 + count : 7 + count]
-    scratch = refs[7 + count :]
-    line_refs, scratch = (scratch[:LINE_REFS], scratch[LINE_REFS:])
-    vec_z, gain_z, vec_sum, gain_sum, vec_in, gain_in, parts = scratch[:7]
-    *buffers, mine, gate_sem, small_send, small_recv, send, recv = scratch[7:]
-    z, r, c = here()
-    twin, side, top = near()
-    cross = (z, flip(across(r)), c)
-    lines, plane = (z_peers(), plane_peers())
-    greet(lines + plane)
-    copies = Copies(send, recv)
-    load = pltpu.make_async_copy(parts_in, parts, gate_sem.at[8])
+    load = pltpu.make_async_copy(out_parts, parts, load_sem.at[0])
     load.start()
-    line = Line(sources, *line_refs[:3], out, line_refs[3:], PACK // LAST_CHUNK)
-    half = line.half
-    packed = []
-    for place, (tile, first, width, which, spot) in enumerate(gate_tiles(gates.shape[1])):
-        copy = pltpu.make_async_copy(
-            gates.at[pl.ds(tile * PACK, PACK), pl.ds(first, width)],
-            line.own.at[pl.ds(8 * half + which * PACK, PACK), pl.ds(spot, width)],
-            gate_sem.at[place],
-        )
-        copy.start()
-        packed.append(copy)
+    grad_done = hand_out(copies, mine, grad)
     small = [
         [
             remote(
@@ -1508,15 +1482,46 @@
             )
             for step in (1, 2, 3)
         ]
-        for kind, (source, target) in enumerate(((vec, vec_z), (gain, gain_z)))
+        for kind, (source, target) in enumerate(((sums, vec_z), (gains, gain_z)))
     ]
     for kind in small:
         for copy in kind:
             copy.start()
-    line.begin()
-    for copy in packed:
-        copy.wait()
-    line.ready()
+    blocks = lax.dot_general(conv[...], d_gates[...], CONTRACT_ROWS, preferred_element_type=jnp.float32)
+    rows_half = width // 2
+    lane = lax.broadcasted_iota(jnp.int32, (rows_half, 2 * width), 1)
+    mingled = jnp.where(
+        lane // rows_half % 2 == 0, blocks[:rows_half], blocks[rows_half:]
+    ).astype(jnp.bfloat16)
+    for tile, begin, length, which, spot in gate_tiles(2 * width):
+        own[pl.ds(2 * rows_all + which * PACK, PACK), spot : spot + length] = mingled[
+            tile * PACK : (tile + 1) * PACK, begin : begin + length
+        ]
+
+    def weights(index, base):
+        columns = pl.ds(pl.multiple_of(index * 256, 256), 256)
+        rows = pl.ds(pl.multiple_of(rows_all + index * 256, 256), 256)
+        own[rows, rest : rest + 2 * width] = lax.dot_general(
+            normed[:, columns], d_pre[...], CONTRACT_ROWS, preferred_element_type=jnp.float32
+        ).astype(jnp.bfloat16)
+        own[rows, rest + 2 * width :] = lax.dot_general(
+            branch[:, columns], mixed[...], CONTRACT_ROWS, preferred_element_type=jnp.float32
+        ).astype(jnp.bfloat16)
+        line.one(base + index)
+        return base
+
+    lax.fori_loop(0, rows_all // 256, weights, line.at)
+    line.skip(rows_all // 256)
+    load.wait()
+    pl.semaphore_wait(free, 3)
+    total_out = reduce_shards(copies, parts, *buffers, between=between)
+
+    def body_out(at):
+        rows = pl.ds(at, STRIP)
+        mine_out[rows, :] = (resid_mid[rows, :] + total_out(at)).astype(jnp.bfloat16)
+
+    strips(size, body_out)
+    output_done = hand_out(copies, mine_out, output)
     spread_out = [
         [
             remote(
@@ -1530,9 +1535,18 @@
         ]
         for kind, (source, target) in enumerate(((vec_sum, vec_in), (gain_sum, gain_in)))
     ]
+    for kind in small:
+        for copy in kind:
+            copy.wait_recv()
+    vec_sum[...] = sums[...] + vec_z[0] + vec_z[1] + vec_z[2]
+    gain_sum[...] = gains[...] + gain_z[0] + gain_z[1] + gain_z[2]
+    for kind in spread_out:
+        for copy in kind:
+            copy.start()
+    line.advance(max(line.first + line.lead + RING + 2 - line.at, 0))
     gate_moves = [
         remote(
-            out.at[4, pl.ds(which * half, PACK), :],
+            grads.at[4 * SEGMENTS, pl.ds(which * half, PACK), :],
             out_gates.at[r, which],
             small_send.at[0, 10 + 2 * place + which],
             small_recv.at[0, 10 + 2 * place + which],
@@ -1543,48 +1557,27 @@
     ]
     gate_local = [
         pltpu.make_async_copy(
-            out.at[4, pl.ds(which * half, PACK), :], out_gates.at[r, which], gate_sem.at[which]
+            grads.at[4 * SEGMENTS, pl.ds(which * half, PACK), :],
+            out_gates.at[r, which],
+            gate_sem.at[which],
         )
         for which in (0, 1)
     ]
-    load.wait()
-    pace = iter((4, 6))
-    total = reduce_shards(
-        copies, parts, *buffers, between=lambda: line.advance(next(pace))
-    )
-    size = mine.shape[0]
-
-    def body(at):
-        rows = pl.ds(at, STRIP)
-        mine[rows, :] = (resid_mid[rows, :] + total(at)).astype(jnp.bfloat16)
-
-    strips(size, body)
-    done = hand_out(copies, mine, output)
-    line.advance(6)
-    for kind in small:
-        for copy in kind:
-            copy.wait_recv()
-    vec_sum[...] = vec[...] + vec_z[0] + vec_z[1] + vec_z[2]
-    gain_sum[...] = gain[...] + gain_z[0] + gain_z[1] + gain_z[2]
-    for kind in spread_out:
-        for copy in kind:
-            copy.start()
-    line.advance(16)
-    line.settle(0, line.lead)
     for copy in gate_moves + gate_local:
         copy.start()
-    line.finish(line.lead)
-    done()
     for kind in spread_out:
         for copy in kind:
             copy.wait_recv()
-    gains = gain_sum[...]
+    all_gains = gain_sum[...]
     for place in range(7):
-        gains = gains + gain_in[place]
-    out_gain[...] = gains
+        all_gains = all_gains + gain_in[place]
+    out_gain[...] = all_gains
     out_vec[r] = vec_sum[...]
     for step in (0, 1, 2):
         out_vec[(r + 3 - step) % 4] = vec_in[6 - step]
+    line.finish()
+    grad_done()
+    output_done()
     for copy in gate_moves:
         copy.wait_recv()
     for copy in gate_local:
@@ -1674,7 +1667,6 @@
     size = tokens // 8
     full = jax.ShapeDtypeStruct((tokens, model), low)
     part = jax.ShapeDtypeStruct((size, model), jnp.float32)
-    line = jax.ShapeDtypeStruct((1, model), jnp.float32)
     piece = pltpu.VMEM((size, model), low)
     block = jax.ShapeDtypeStruct((inputs.shape[1], inputs.shape[0]), low)
     weights = (gate_proj, up_proj, down_proj)
@@ -1728,24 +1720,30 @@
         return jax.ShapeDtypeStruct(array.shape, array.dtype)
 
     both = jax.ShapeDtypeStruct((tokens, 2 * rec), low)
-    held = (pre, x_pre, conv, rec_gate, in_gate, states)
-    d_branch, d_pre, d_gates, grad_in, grads_mlp, sums, grad_mlp_gain, grad_mix_gain = vmem_call(
+    held = (normed_mix, pre, mixed, x_pre, conv, rec_gate, in_gate, states)
+    wide = (3 * width + 2 * rec + padded) // SEGMENTS
+    sums = pltpu.VMEM((16, rec), jnp.float32)
+    lines = pltpu.VMEM((2, model), jnp.float32)
+    dma = pltpu.SemaphoreType.DMA
+
+    def several(count, kind):
+        return pltpu.VMEM((count, *kind.shape), kind.dtype)
+
+    grad_in, output, grads, gates, vec_sums, gains = vmem_call(
         backward_kernel,
         "backward",
         BACKWARD_ID,
         (resid_mid, gain_mlp, gain_mix, masks, vec, rec_w, in_w, mix_w, out_w),
         [
-            full,
-            both,
-            both,
             block,
-            jax.ShapeDtypeStruct((4, depth, 2 * width), low),
-            jax.ShapeDtypeStruct((16, rec), jnp.float32),
-            line,
-            line,
+            block,
+            jax.ShapeDtypeStruct((4 * SEGMENTS + 1, depth, wide), low),
+            jax.ShapeDtypeStruct((4, 2, PACK, wide), low),
+            jax.ShapeDtypeStruct((4, 16, rec), jnp.float32),
+            jax.ShapeDtypeStruct((2, model), jnp.float32),
         ],
-        [pl.ANY] * 5 + [pltpu.VMEM] * 3,
-        line_scratch(2, depth, 2 * width, BACK_CHUNK, 0)
+        [pl.ANY] * 4 + [pltpu.VMEM] * 2,
+        line_scratch(depth, wide, CHUNK, PACK // CHUNK)
         + [
             kind_of(full),
             piece,
@@ -1758,62 +1756,36 @@
             row8,
         ]
         + [kind_of(item) for item in held]
+        + [
+            sums,
+            lines,
+            several(3, sums),
+            several(3, lines),
+            sums,
+            lines,
+            several(7, sums),
+            several(7, lines),
+        ]
         + reduce_scratch(size, model)
-        + [piece, pltpu.SemaphoreType.DMA((9,))],
-        60,
+        + [
+            piece,
+            piece,
+            dma((15,)),
+            dma((2,)),
+            dma((2, 16)),
+            dma((2, 16)),
+            pltpu.SemaphoreType.REGULAR,
+        ],
+        80,
         (
             d_normed.astype(low),
+            dot(activ, down_w, CONTRACT_COLS, low),
             c_all,
             x_all,
             *held,
             dot(normed_mlp, d_gate, CONTRACT_ROWS, low),
             dot(normed_mlp, d_up, CONTRACT_ROWS, low),
-        ),
-    )
-    gate_grads = dot(conv, d_gates, CONTRACT_ROWS, low)
-    gates = jnp.concatenate(
-        [
-            gate_grads[i * head : (i + 1) * head, first + i * head : first + (i + 1) * head]
-            for first in (0, rec)
-            for i in range(heads)
-        ],
-        axis=1,
-    )
-    gain_grads = jnp.concatenate([grad_mix_gain, grad_mlp_gain], axis=0)
-    final_width = width + 2 * rec + padded
-    dma = pltpu.SemaphoreType.DMA
-    grads, gates, output, vec_sums, gains = vmem_call(
-        functools.partial(reduce_kernel, 3),
-        "reduce_grads",
-        REDUCE_ID,
-        (resid_mid, sums, gain_grads),
-        [
-            jax.ShapeDtypeStruct((5, depth, final_width), low),
-            jax.ShapeDtypeStruct((4, 2, PACK, final_width), low),
-            block,
-            jax.ShapeDtypeStruct((4, *sums.shape), jnp.float32),
-            like(gain_grads),
-        ],
-        [pl.ANY] * 3 + [pltpu.VMEM] * 2,
-        line_scratch(3, depth, final_width, LAST_CHUNK, PACK // LAST_CHUNK)
-        + [
-            pltpu.VMEM((3, *sums.shape), jnp.float32),
-            pltpu.VMEM((3, *gain_grads.shape), jnp.float32),
-            kind_of(sums),
-            kind_of(gain_grads),
-            pltpu.VMEM((7, *sums.shape), jnp.float32),
-            pltpu.VMEM((7, *gain_grads.shape), jnp.float32),
-            kind_of(full),
-        ]
-        + reduce_scratch(size, model)
-        + [piece, dma((9,)), dma((2, 16)), dma((2, 16))],
-        40,
-        (
-            dot(activ, down_w, CONTRACT_COLS, low),
-            gates,
             dot(c_all, activ, CONTRACT_ROWS, low),
-            dot(normed_mix, d_pre, CONTRACT_ROWS, low),
-            dot(d_branch, mixed, CONTRACT_ROWS, low),
         ),
     )
     tiles = [[], [], [], [], []]
@@ -1825,24 +1797,25 @@
     vec_sums = vec_sums.transpose(1, 0, 2).reshape(vec_sums.shape[1], 4 * rec)
     gains = lax.dynamic_slice_in_dim(gains, r * depth, depth, 1)
 
-    def columns(array, first, length):
+    def columns(*spans):
         return jnp.concatenate(
-            [array[i, :, first : first + length] for i in range(4)], axis=1
+            [grads[4 * seg + i, :, a : a + n] for i in range(4) for seg, a, n in spans], axis=1
         ).astype(jnp.float32)
 
-    after = width
+    head_width = wide - 2 * width
+    after = width - head_width
     grad_out = jnp.concatenate(
-        [grads[i, :, after + 2 * rec : after + 3 * rec].T for i in range(4)], axis=0
+        [grads[4 + i, :, after + 2 * rec : after + 3 * rec].T for i in range(4)], axis=0
     ).astype(jnp.float32)
     return (
         output.T,
         grad_in.astype(jnp.float32).T,
-        columns(grads, after, rec),
-        columns(grads, after + rec, rec),
+        columns((1, after, rec)),
+        columns((1, after + rec, rec)),
         grad_out,
-        columns(grads_mlp, 0, width),
-        columns(grads_mlp, width, width),
-        columns(grads, 0, width),
+        columns((0, 0, width)),
+        columns((0, width, width)),
+        columns((0, 2 * width, head_width), (1, 0, after)),
         gains[0],
         gains[1],
         vec_sums[0],

time: 700 us -> 662 us (0.946)
  Pallas kernels: 566 us -> 542 us
  matrix products: 55.4 us -> 43.9 us
    pallas_call x3 -> x2, Pallas kernels: 515 us -> 491 us  [vmem_call(): pl.pallas_call(kernel, in_specs=[pl.BlockSpec(memory_space=pltpu.VMEM)] *...]
    dot_general x10 -> x7, matrix products: 46.9 us -> 35.4 us  [dot(): lax.dot_general(left, right, dims, preferred_element_type=jnp.float32)]
    unnamed x69 -> x58, local copies, waits for them, and re-layouts: 15 us -> 14.4 us
where the time goes in v4:
time: 662 us; the launch traced here: 653 us
  Pallas kernels  542 us (82%)
  local copies, waits for them, and re-layouts  46.2 us (7%)
  matrix products  43.9 us (7%)
  other arithmetic  19.9 us (3%)
    pallas_call x2, Pallas kernels, vmem_call(): pl.pallas_call(kernel, in_specs=[pl.BlockSpec(memory_space=pltpu.VMEM)] *...  491 us
    pallas_call x1, Pallas kernels, gather(): pl.pallas_call(gather_kernel, in_specs=[pl.BlockSpec(memory_space=pl.ANY)...  51.1 us
    dot_general x7, matrix products, dot(): lax.dot_general(left, right, dims, preferred_element_type=jnp.float32)  35.4 us
    unnamed x58, local copies, waits for them, and re-layouts  14.4 us
    convert_element_type x5, other arithmetic, columns(): return jnp.concatenate([grads[4 * seg + i, :, a:a + n] for i in range(4)...  13.3 us

profile of v4, /device:TPU:0, one launch (start us, length us, event | category | flops | bytes accessed | tf_op | source)
XLA Modules:
  0.0 653.3 jit_solution(9905917927335803259)
XLA Ops:
  0.7 1.6 copy.63
  2.3 0.9 copy.65
  3.1 2.4 copy.64
  5.6 1.8 copy.66
  7.4 2.5 maximum_bitcast_fusion.mix_in
  9.9 2.0 copy.62
  12.0 0.6 pad.19.s_in
  12.6 0.6 pad_maximum_fusion.1.g_in
  13.2 51.1 %gather.1 = (bf16[1024,2048]{1,0:T(8,128)(2,1)}, f32[4,8,128]{2,1,0:T(8,128)}, f32[2,2048]{1,0:T(2,128)}, bf16[2048,640]{1,0:T(8,128)(2,1)}, bf16[320,2048]{1,0:T(8,128)(2,1)}) custom-call(bf16[512,512]{1,0:T(8,128)(2,1)} %bitcast.131, f32[8,128]{1,0:T(8,128)} %pad.19.s_in, f32[2,512]{1,0:T(2,128)} %pad_maximum_fusion.1.g_in, ...), custom_call_target="tpu_custom_call" | custom-call | tf_op jit(solution)/shard_map/gather/pallas_call | solution.py:730
  64.3 0.7 broadcast_subtract_fusion
  65.2 1.0 copy.68.masks
  66.2 1.0 dynamic-slice_bitcast_fusion.1
  67.3 0.8 fusion.4.rec_w
  68.1 0.8 fusion.5.in_w
  69.1 0.7 constant_dynamic-slice_fusion.1.vec
  69.8 1.4 fusion.11
  71.2 1.0 copy.67
  72.2 120.4 %forward.1 = (bf16[1024,2048]{1,0:T(8,128)(2,1)}, f32[128,2048]{1,0:T(8,128)}, bf16[1024,2048]{1,0:T(8,128)(2,1)}, bf16[2048,768]{1,0:T(8,128)(2,1)}, bf16[2048,...) custom-call(bf16[1024,2048]{1,0:T(8,128)(2,1)} %get-tuple-element.44, ...), custom_call_target="tpu_custom_call" | custom-call | tf_op jit(solution)/shard_map/forward/pallas_call | solution.py:951
  192.6 6.7 %fusion.12 = f32[1024,768]{1,0:T(8,128)S(1)} fusion(bf16[1024,2048]{1,0:T(8,128)(2,1)} %get-tuple-element.50.refs_2_, bf16[2048,768]{1,0:T(8,128)(2,1)} %get-tuple-element.51), kind=kOutput, calls=%fused_computation.85 | convolution fusion | flops 3221225472 | bytes 10485760 | tf_op jit(solution)/shard_map/dot_general | solution.py:1592
  199.4 3.4 fusion.13
  202.9 5.1 multiply_convert_fusion
  208.0 5.0 convolution_convert_fusion.1.refs_14_
  213.0 5.0 convolution_convert_fusion.2.refs_13_
  218.0 5.1 convolution_convert_fusion.3.refs_12_
  223.2 5.0 convolution_convert_fusion.refs_1_
  228.2 3.4 fusion.14
  231.6 5.0 add_convert_fusion.refs_0_
  236.6 370.2 %backward.1 = (bf16[512,512]{1,0:T(8,128)(2,1)}, bf16[512,512]{1,0:T(8,128)(2,1)}, bf16[9,512,1664]{2,1,0:T(8,128)(2,1)}, bf16[4,2,32,1664]{3,2,1,0:T(8,128)(2,1...) custom-call(f32[128,2048]{1,0:T(8,128)} %get-tuple-element.49.resid_mid, f32[1,2048]{1,0:T(1,128)} %get-tuple-element.167.gain, ...), custom_call_target="tpu_custom_call" | custom-call | tf_op jit(solution)/shard_map/backward/pallas_call | solution.py:951
  606.8 0.9 slice_bitcast_fusion.20
  607.8 0.9 slice_bitcast_fusion.21
  608.6 0.2 concatenate.83
  608.9 1.2 fusion.9
  610.1 0.2 concatenate.78
  610.7 0.2 constant_dynamic-update-slice_fusion.3
  610.9 0.2 concatenate.80
  611.2 0.2 constant_dynamic-update-slice_fusion.2
  611.4 0.2 concatenate.81
  611.6 0.2 constant_dynamic-update-slice_fusion.1
  612.0 0.9 convert_bitcast_fusion
  612.9 1.0 fusion.8
  613.9 1.2 copy.71
  615.1 1.2 copy.72
  616.3 1.6 copy-done
  618.7 3.5 convert_element_type.75
  622.2 0.5 slice_bitcast_fusion.3
  622.6 3.3 maximum_convert_fusion.1
  626.0 3.1 maximum_convert_fusion
  629.1 2.2 slice_bitcast_fusion.8
  631.2 2.8 concatenate.74
  634.0 1.9 copy.75
  635.9 2.6 concatenate.73
  638.5 1.7 convert_element_type.71
  640.2 2.2 concatenate.72
  642.4 1.7 convert_element_type.70
  644.2 1.3 copy.74
  645.5 1.0 copy.73
  646.6 0.7 slice.215
  647.4 0.7 squeeze.170
  648.0 0.7 squeeze.171
  648.7 0.7 squeeze.172
  649.4 0.7 squeeze.177
  650.1 0.7 squeeze.178
  650.7 0.7 squeeze.179
  651.4 1.4 fusion.10
  (70 shorter events, 2.0 us)
Async XLA Ops:
  7.4 4.6 copy-start.15
  7.4 5.2 copy-start.13
  7.4 5.1 copy-start.14
  13.2 55.7 %copy-start.7 = (f32[1280]{0:T(1024)S(1)}, f32[1280]{0:T(1024)}, u32[]{:S(2)}) copy-start(f32[1280]{0:T(1024)} %param.39) | copy-start | bytes 15364
  13.2 55.7 %copy-start.8 = (f32[1280]{0:T(1024)S(1)}, f32[1280]{0:T(1024)}, u32[]{:S(2)}) copy-start(f32[1280]{0:T(1024)} %param.31) | copy-start | bytes 15364
  13.2 55.7 %copy-start.9 = (f32[1280]{0:T(1024)S(1)}, f32[1280]{0:T(1024)}, u32[]{:S(2)}) copy-start(f32[1280]{0:T(1024)} %param.32) | copy-start | bytes 15364
  13.2 55.8 %copy-start.10 = (f32[1280]{0:T(1024)S(1)}, f32[1280]{0:T(1024)}, u32[]{:S(2)}) copy-start(f32[1280]{0:T(1024)} %param.34) | copy-start | bytes 15364
  13.2 55.8 %copy-start.11 = (f32[1280]{0:T(1024)S(1)}, f32[1280]{0:T(1024)}, u32[]{:S(2)}) copy-start(f32[1280]{0:T(1024)} %param.37) | copy-start | bytes 15364
  13.2 55.8 %copy-start.12 = (f32[1280]{0:T(1024)S(1)}, f32[1280]{0:T(1024)}, u32[]{:S(2)}) copy-start(f32[1280]{0:T(1024)} %param.38) | copy-start | bytes 15364
  13.2 55.8 %copy-start.6 = (f32[4,1280]{1,0:T(4,128)S(1)}, f32[4,1280]{1,0:T(4,128)}, u32[]{:S(2)}) copy-start(f32[4,1280]{1,0:T(4,128)} %param.33) | copy-start | bytes 61444
  13.2 58.0 %copy-start.3 = (bf16[512,512]{1,0:T(8,128)(2,1)S(1)}, bf16[512,512]{1,0:T(8,128)(2,1)}, u32[]{:S(2)}) copy-start(bf16[512,512]{1,0:T(8,128)(2,1)} %param.21) | copy-start | bytes 1572868
  192.6 6.8 %copy-start.16 = (bf16[1024,2048]{1,0:T(8,128)(2,1)S(1)}, bf16[1024,2048]{1,0:T(8,128)(2,1)}, u32[]{:S(2)}) copy-start(bf16[1024,2048]{1,0:T(8,128)(2,1)} %get-tuple-element.52) | copy-start | bytes 12582916
  192.6 6.8 %copy-start.18 = (bf16[2048,768]{1,0:T(8,128)(2,1)S(1)}, bf16[2048,768]{1,0:T(8,128)(2,1)}, u32[]{:S(2)}) copy-start(bf16[2048,768]{1,0:T(8,128)(2,1)} %get-tuple-element.54) | copy-start | bytes 9437188
  199.4 3.4 copy-start.17
  202.9 5.2 copy-start.1
  218.0 5.1 copy-start.19
  611.6 6.3 copy-start
  640.2 3.9 copy-start.2
  642.4 3.1 copy-start.4
  644.1 2.5 copy-start.5

commit v5 on v4

--- a/solution.py
+++ b/solution.py
@@ -597,52 +597,81 @@
     return late
 
 
+def spread_tall(copies, own, place, between=lambda: None):
+    z, r, c = here()
+    twin, side, top = ((z, flip(r), c), (z, across(r), c), (z, r, 1 - c))
+    to_side = copies.go(own, place(r, c), side)
+    to_top = copies.go(own, place(r, c), top)
+    late = [copies.go(own, place(r, c), twin)]
+    between()
+    arrived(to_side)
+    from_side = place(across(r), c)
+    on_top = copies.go(from_side, from_side, top)
+    late.append(copies.go(from_side, from_side, twin))
+    between()
+    arrived(to_top)
+    from_top = place(r, 1 - c)
+    late.append(copies.go(from_top, from_top, twin))
+    between()
+    arrived(on_top)
+    far = place(across(r), 1 - c)
+    late.append(copies.go(far, far, twin))
+    return late
+
+
 def part(start, size, step):
     return pl.ds(pl.multiple_of(start * step, step), size)
 
 
 class Moves:
     def __init__(self, copies, matrices, cuts):
-        self.copies = copies
         z, r, c = here()
-        self.mine = z % 2
-        self.sides = ((z, across(r), c), (z, flip(across(r)), c))
-        self.pair = (flip(z), r, c)
-        self.locals, self.late, self.flying = ([], [], [])
-        self.groups = [(matrix, cut) for matrix in matrices for cut in range(cuts)]
-        self.cuts, self.begun = (cuts, 0)
+        mine = z % 2
+        sides = ((z, across(r), c), (z, flip(across(r)), c))
+        pair = (flip(z), r, c)
+        self.groups, self.locals, self.late = ([], [], [])
+        self.begun, self.ended = (0, 0)
+
+        def piece(ref, size, cut):
+            length = size // 2 // cuts
+            return ref.at[part(mine * cuts + cut, length, length), :]
+
+        for source, target, size in matrices:
+            for cut in range(cuts):
+                group = []
+                for peer in sides:
+                    spot = piece(target(peer[1]), size, cut)
+                    group.append(
+                        (
+                            copies.make(
+                                piece(source(peer[1]), size, cut), piece(target(r), size, cut), peer
+                            ),
+                            copies.make(spot, spot, pair),
+                        )
+                    )
+                self.groups.append(group)
         for source, target, size in matrices:
             self.locals.append(copies.go(source(r), target(r), None))
             self.late.append(copies.go(source(flip(r)), target(r), (z, flip(r), c)))
 
-    def piece(self, ref, size, cut):
-        length = size // 2 // self.cuts
-        return ref.at[part(self.mine * self.cuts + cut, length, length), :]
-
     def step(self):
-        if len(self.flying) == 2 or self.begun == len(self.groups):
-            if self.flying:
-                (source, target, size), cut, group = self.flying.pop(0)
-                for peer, copy in zip(self.sides, group):
-                    arrived(copy)
-                    piece = self.piece(target(peer[1]), size, cut)
-                    self.late.append(self.copies.go(piece, piece, self.pair))
+        if self.begun - self.ended == 2 or self.begun == len(self.groups):
+            if self.ended < self.begun:
+                for first, second in self.groups[self.ended]:
+                    arrived(first)
+                    second.start()
+                self.ended += 1
         if self.begun < len(self.groups):
-            (source, target, size), cut = self.groups[self.begun]
+            for first, _ in self.groups[self.begun]:
+                first.start()
             self.begun += 1
-            group = [
-                self.copies.go(
-                    self.piece(source(peer[1]), size, cut),
-                    self.piece(target(here()[1]), size, cut),
-                    peer,
-                )
-                for peer in self.sides
-            ]
-            self.flying.append(((source, target, size), cut, group))
 
     def finish(self):
-        while self.flying:
+        while self.ended < len(self.groups):
             self.step()
+        for group in self.groups:
+            for _, second in group:
+                arrived(second)
         for copy in self.late:
             arrived(copy)
         for copy in self.locals:
@@ -669,7 +698,27 @@
     ]
 
 
-def gather_kernel(x_in, s_in, g_in, mix_in, out_in, x_all, s_all, g_all, mix_all, out_all, send, recv):
+def gather_kernel(
+    x_in,
+    c_in,
+    s_in,
+    g_in,
+    x_proj,
+    y_proj,
+    out_in,
+    x_all,
+    c_all,
+    s_all,
+    g_all,
+    mix_all,
+    out_all,
+    x_here,
+    y_here,
+    mix_in,
+    load_sem,
+    send,
+    recv,
+):
     z, r, c = here()
     twin, side, cross, top, pair = (
         (z, flip(r), c),
@@ -678,6 +727,12 @@
         (z, r, 1 - c),
         (flip(z), r, c),
     )
+    loads = [
+        pltpu.make_async_copy(source, target, load_sem.at[place])
+        for place, (source, target) in enumerate(((x_proj, x_here), (y_proj, y_here)))
+    ]
+    for copy in loads:
+        copy.start()
     greet((twin, side, cross, top, pair))
     copies = Copies(send, recv)
     rows, columns = x_in.shape
@@ -690,22 +745,37 @@
             rec,
         ),
     ]
+    moves = []
+
+    def between():
+        if not moves:
+            for copy in loads:
+                copy.wait()
+
+            def body(at):
+                strip = pl.ds(at, STRIP)
+                x, y = (x_here[strip, :], y_here[strip, :])
+                for to in range(4):
+                    span = slice(to * rec, (to + 1) * rec)
+                    mix_in[to, strip, :] = jnp.concatenate([x[:, span], y[:, span]], axis=1)
+
+            strips(depth, body)
+            moves.append(Moves(copies, matrices, 2))
+        moves[0].step()
+
     small = g_all.at[:, part(r, depth, depth)]
+    late = spread_tall(copies, x_in, block_of(x_all, rows, columns), between)
     locals_ = [
         copies.go(x_in, block_of(x_all, rows, columns)(r, c), None),
+        copies.go(c_in, block_of(c_all, rows, columns)(r, c), None),
         copies.go(s_in, s_all.at[r], None),
         copies.go(g_in, small, None),
     ]
-    late = []
     for peer in (twin, side, cross):
         late.append(copies.go(s_in, s_all.at[r], peer))
         late.append(copies.go(g_in, small, peer))
-    moves = Moves(copies, matrices, 2)
-    moves.step()
-    late.extend(
-        spread(copies, x_in, block_of(x_all, rows, columns), halves_of(rows), moves.step)
-    )
-    moves.finish()
+    late.extend(spread_tall(copies, c_in, block_of(c_all, rows, columns), between))
+    moves[0].finish()
     for copy in late:
         arrived(copy)
     for copy in locals_:
@@ -713,29 +783,40 @@
     copies.finish()
 
 
-def gather(x_in, s_in, g_in, mix_in, out_in):
+def gather(x_in, c_in, s_in, g_in, x_proj, y_proj, out_in):
     rows, columns = x_in.shape
-    depth = mix_in.shape[1]
+    depth, wide = x_proj.shape
 
     def shape(*dims, kind=jnp.bfloat16):
         return jax.ShapeDtypeStruct(dims, kind)
 
     outs = [
+        shape(2 * rows, 4 * columns),
         shape(2 * rows, 4 * columns),
         shape(4, *s_in.shape, kind=s_in.dtype),
         shape(g_in.shape[0], 4 * depth, kind=g_in.dtype),
-        shape(4 * depth, mix_in.shape[2]),
+        shape(4 * depth, wide // 2),
         shape(out_in.shape[0] // 4, 4 * columns),
     ]
+    dma = pltpu.SemaphoreType.DMA
     return pl.pallas_call(
         gather_kernel,
-        in_specs=[pl.BlockSpec(memory_space=pl.ANY)] * 5,
-        out_specs=[pl.BlockSpec(memory_space=pl.ANY)] * 5,
+        in_specs=[pl.BlockSpec(memory_space=pltpu.HBM)] * 7,
+        out_specs=[pl.BlockSpec(memory_space=pltpu.HBM)] * 6,
         out_shape=outs,
-        scratch_shapes=[pltpu.SemaphoreType.DMA((48,)), pltpu.SemaphoreType.DMA((48,))],
-        compiler_params=pltpu.CompilerParams(collective_id=GATHER_ID, has_side_effects=True),
+        scratch_shapes=[
+            pltpu.VMEM((depth, wide), jnp.bfloat16),
+            pltpu.VMEM((depth, wide), jnp.bfloat16),
+            pltpu.VMEM((4, depth, wide // 2), jnp.bfloat16),
+            dma((2,)),
+            dma((64,)),
+            dma((64,)),
+        ],
+        compiler_params=pltpu.CompilerParams(
+            collective_id=GATHER_ID, has_side_effects=True, vmem_limit_bytes=60 << 20
+        ),
         name="gather",
-    )(x_in, s_in, g_in, mix_in, out_in)
+    )(x_in, c_in, s_in, g_in, x_proj, y_proj, out_in)
 
 
 STRIP = 16
@@ -753,7 +834,9 @@
     return col * 4 + row
 
 
-def reduce_shards(copies, parts, twin_in, sums, side_in, top_in, hop_in, between=lambda: None):
+def reduce_shards(
+    copies, parts, twin_in, sums, side_in, top_in, hop_in, between=lambda: None, tall=False
+):
     z, r, c = here()
     twin, side, top = ((z, flip(r), c), (z, across(r), c), (z, r, 1 - c))
     size = side_in.shape[0]
@@ -793,7 +876,31 @@
     def rows_of(ref, which):
         return ref.at[pl.ds(which * half, half), :]
 
+    def total(at):
+        rows = pl.ds(at, STRIP)
+        return (
+            sums[3, rows, :].astype(jnp.float32)
+            + side_in[rows, :].astype(jnp.float32)
+            + top_in[rows, :].astype(jnp.float32)
+        )
+
     add_twin(0)
+    if tall:
+        hops = [copies.go(rows_of(sums.at[0], k), hop_in.at[k], top) for k in (0, 1)]
+        add_twin(2)
+        to_top = copies.go(sums.at[2], top_in, top)
+        add_twin(1)
+        add_twin(3)
+        between()
+        to_side = []
+        for k in (0, 1):
+            arrived(hops[k])
+            add_hop(1, k, k)
+            to_side.append(copies.go(rows_of(sums.at[1], k), rows_of(side_in, k), side))
+        between()
+        for copy in [to_top, *to_side]:
+            arrived(copy)
+        return total
     hop_side = copies.go(rows_of(sums.at[0], 0), hop_in.at[0], side)
     hop_top = copies.go(rows_of(sums.at[0], 1), hop_in.at[1], top)
     add_twin(1)
@@ -811,15 +918,6 @@
     between()
     for copy in waits:
         arrived(copy)
-
-    def total(at):
-        rows = pl.ds(at, STRIP)
-        return (
-            sums[3, rows, :].astype(jnp.float32)
-            + side_in[rows, :].astype(jnp.float32)
-            + top_in[rows, :].astype(jnp.float32)
-        )
-
     return total
 
 
@@ -838,7 +936,7 @@
     return ((z, flip(r), c), (z, across(r), c), (z, r, 1 - c))
 
 
-def spread_rows(copies, mine, full, between=lambda: None):
+def spread_rows(copies, mine, full, between=lambda: None, tall=False):
     z, r, c = here()
     size = mine.shape[0]
     half = size // 2
@@ -847,49 +945,91 @@
         return full.at[pl.ds(pl.multiple_of(token_shard(row, col) * size, size), size), :]
 
     local = copies.go(mine, place(r, c), None)
-    late = spread(
-        copies, mine, place, lambda ref, which: ref.at[pl.ds(which * half, half), :], between
-    )
+    if tall:
+        late = spread_tall(copies, mine, place, between)
+    else:
+        late = spread(
+            copies, mine, place, lambda ref, which: ref.at[pl.ds(which * half, half), :], between
+        )
     for copy in late:
         arrived(copy)
     local.wait()
 
 
-def forward_kernel(x_all, masks, vec, rec_w, in_w, mix_w, out_w, gain_mix, gain, c_in, *refs):
-    mlp_in, outs, scratch = (refs[:3], refs[3:17], refs[17:])
-    full, resid_mid, c_all = outs[:3]
-    mlp_all, kept_out = (outs[3:6], outs[6:])
+def mark_rows(flags, tail):
+    stale = 1.0 - flags
+    longer = jnp.concatenate([tail[...], stale], axis=0)
+    tail[...] = stale[BLOCK - 8 :]
+    pair = stale * down_rows(longer, 1)[8:]
+    triple = pair * down_rows(longer, 2)[8:]
+    lane = lax.broadcasted_iota(jnp.int32, flags.shape, 1)
+    return jnp.where(lane == 0, flags, jnp.where(lane == 1, stale, jnp.where(lane == 2, pair, triple)))
+
+
+def forward_kernel(vec, rec_w, in_w, gains, *refs):
+    x_in, s_in, mix_in, out_in = refs[:4]
+    mlp_in, outs, scratch = (refs[4:7], refs[7:21], refs[21:])
+    full, resid_mid = outs[:2]
+    mlp_all, kept_out = (outs[2:5], outs[5:])
     kept, (tail, carry, parts), (*buffers, mine, kept_sem, send, recv) = (
-        scratch[:8],
-        scratch[8:11],
-        scratch[11:],
-    )
-    normed, pre, mixed, *saved = kept
+        scratch[:9],
+        scratch[9:12],
+        scratch[12:],
+    )
+    x_all, flags, mix_w, out_w, mark_tail, load_sem, *buffers = buffers
+    normed, pre, mixed, *saved, masks = kept
+    loads = [
+        pltpu.make_async_copy(source, target, load_sem.at[8 + place])
+        for place, (source, target) in enumerate(
+            ((mix_in, mix_w), (s_in, flags), (out_in, out_w))
+        )
+    ]
+
+    def load_rows(index):
+        rows = pl.ds(pl.multiple_of(index * BLOCK, BLOCK), BLOCK)
+        return pltpu.make_async_copy(x_in.at[rows, :], x_all.at[rows, :], load_sem.at[index])
+
+    load_rows(0).start()
+    for copy in loads:
+        copy.start()
+    for index in range(1, x_all.shape[0] // BLOCK):
+        load_rows(index).start()
     z, r, c = here()
     greet((*near(), (z, flip(across(r)), c), (flip(z), r, c)))
     copies = Copies(send, recv)
-    rows, columns = c_in.shape
     moves = Moves(copies, mlp_matrices(mlp_in, mlp_all), 2)
     moves.step()
     moves.step()
+    for copy in loads:
+        copy.wait()
+    mark_tail[...] = jnp.zeros_like(mark_tail)
     tail[...] = jnp.zeros_like(tail)
     carry[...] = jnp.zeros_like(carry)
 
     def block(index, nothing):
         start = pl.multiple_of(index * BLOCK, BLOCK)
         rows = pl.ds(start, BLOCK)
+        for turn in (3, 6):
+
+            @pl.when(index == turn)
+            def _():
+                moves.step()
+
+        load_rows(index).wait()
+        marks = mark_rows(flags[rows, :8], mark_tail)
+        masks[rows, :] = marks
 
         def norm(at):
             strip = pl.ds(start + at, STRIP)
             values = x_all[strip, :].astype(jnp.float32)
             scale = lax.rsqrt(jnp.mean(values * values, axis=1, keepdims=True) + EPS)
-            normed[strip, :] = (values * scale * gain_mix[...]).astype(jnp.bfloat16)
+            normed[strip, :] = (values * scale * gains[0:1, :]).astype(jnp.bfloat16)
 
         strips(BLOCK, norm)
         pre[rows, :] = jnp.dot(normed[rows, :], mix_w[...], preferred_element_type=jnp.float32)
         mixer_forward_step(
             pre.at[rows, :],
-            masks[rows, :],
+            marks,
             vec,
             rec_w,
             in_w,
@@ -904,18 +1044,14 @@
         ).astype(jnp.bfloat16)
         return nothing
 
-    lax.fori_loop(0, 3, block, 0)
-    moves.step()
-    lax.fori_loop(3, 6, block, 0)
-    moves.step()
-    lax.fori_loop(6, x_all.shape[0] // BLOCK, block, 0)
+    lax.fori_loop(0, x_all.shape[0] // BLOCK, block, 0)
     keeping = [
         pltpu.make_async_copy(source, target, kept_sem.at[place])
         for place, (source, target) in enumerate(zip(kept, kept_out))
     ]
     for copy in keeping:
         copy.start()
-    total = reduce_shards(copies, parts, *buffers, between=moves.step)
+    total = reduce_shards(copies, parts, *buffers, between=moves.step, tall=True)
     size = mine.shape[0]
     start = pl.multiple_of(token_shard(r, c) * size, size)
 
@@ -924,15 +1060,10 @@
         values = x_all[pl.ds(start + at, STRIP), :].astype(jnp.float32) + total(at)
         resid_mid[rows, :] = values
         scale = lax.rsqrt(jnp.mean(values * values, axis=1, keepdims=True) + EPS)
-        mine[rows, :] = (values * scale * gain[...]).astype(jnp.bfloat16)
+        mine[rows, :] = (values * scale * gains[1:2, :]).astype(jnp.bfloat16)
 
     strips(size, body)
-    spread_rows(copies, mine, full, moves.step)
-    local = copies.go(c_in, block_of(c_all, rows, columns)(r, c), None)
-    late = spread(copies, c_in, block_of(c_all, rows, columns), halves_of(rows), moves.step)
-    for copy in late:
-        arrived(copy)
-    local.wait()
+    spread_rows(copies, mine, full, moves.step, tall=True)
     moves.finish()
     for copy in keeping:
         copy.wait()
@@ -951,7 +1082,7 @@
     return pl.pallas_call(
         kernel,
         in_specs=[pl.BlockSpec(memory_space=pltpu.VMEM)] * len(arrays)
-        + [pl.BlockSpec(memory_space=pl.ANY)] * len(loose),
+        + [pl.BlockSpec(memory_space=pltpu.HBM)] * len(loose),
         out_specs=[pl.BlockSpec(memory_space=space) for space in spaces],
         out_shape=outs,
         scratch_shapes=scratch
@@ -965,9 +1096,10 @@
 
 AHEAD = 3
 DEPTH = 4
-HAND_LAG = 4
-LAG = 6
-RING = 16
+SUM_LAG = 1
+HAND_LAG = 3
+LAG = 4
+RING = 9
 SEGMENTS = 2
 
 
@@ -1166,9 +1298,9 @@
             own[span, :] = total.astype(jnp.bfloat16)
             self.to_other(index).start()
 
-        @pl.when((index >= 2) & (index < self.chunks + 2))
+        @pl.when((index >= SUM_LAG) & (index < self.chunks + SUM_LAG))
         def _():
-            back = index - 2
+            back = index - SUM_LAG
             self.from_outer(back)[0].wait_recv()
             self.to_other(back).wait_recv()
             span = self.span(back, low)
@@ -1207,6 +1339,13 @@
             copy = self.onward(index - LAG)
             copy.wait_recv()
             copy.start()
+
+    def prime(self):
+        @pl.when(self.is_end)
+        def _():
+            run_loop(0, AHEAD, self.end_step)
+
+        self.ahead = AHEAD
 
     def advance(self, count):
         first, last = (self.at, min(self.at + count, self.total))
@@ -1291,9 +1430,9 @@
 
 LINE_REFS = 12
 PACK = 32
-CHUNK = 16
-PACE = (6, 6, 6, 2, 2, 4, 6, 6, 8)
-BLOCK_STEPS = 2
+CHUNK = 32
+PACE = (2, 3, 3, 1, 1, 1, 2, 5, 6)
+BLOCK_STEPS = 1
 
 
 def z_peers():
@@ -1340,7 +1479,7 @@
     return tiles
 
 
-def backward_kernel(resid_mid, gain, gain_mix, masks, vec, rec_w, in_w, mix_w, out_w, *refs):
+def backward_kernel(resid_mid, both_gains, masks, vec, rec_w, in_w, mix_w, out_w, *refs):
     parts_in, out_parts, c_all, x_all, *kept_in = refs[:12]
     gate_grad, up_grad, down_grad = refs[12:15]
     grad, output, grads, out_gates, out_vec, out_gain = refs[15:21]
@@ -1369,20 +1508,20 @@
         for place, (source, target) in enumerate(
             zip(
                 [
-                    parts_in,
                     gate_grad,
                     up_grad,
                     down_grad.at[:, pl.ds(0, head)],
+                    parts_in,
                     down_grad.at[:, pl.ds(head, rest)],
                     c_all.at[shard, :],
                     x_all.at[shard, :],
                     *kept_in,
                 ],
                 [
-                    parts,
                     own.at[first, pl.ds(0, ff)],
                     own.at[first, pl.ds(ff, ff)],
                     own.at[first, pl.ds(2 * ff, head)],
+                    parts,
                     own.at[second, pl.ds(0, rest)],
                     cot,
                     resid,
@@ -1395,8 +1534,10 @@
         copy.start()
     for ref in (gains, sums, edge, carry):
         ref[...] = jnp.zeros_like(ref)
-    for copy in loads[:4]:
+    for copy in loads[:3]:
         copy.wait()
+    line.prime()
+    loads[3].wait()
     pace = iter(PACE)
 
     def between():
@@ -1408,7 +1549,7 @@
 
     def body(at):
         rows = pl.ds(at, STRIP)
-        values, piece = norm_pull(resid_mid[rows, :], gain[...], total(at))
+        values, piece = norm_pull(resid_mid[rows, :], both_gains[1:2, :], total(at))
         values = values + cot[rows, :].astype(jnp.float32)
         gains[1:2, :] += piece
         d_resid[rows, :] = values
@@ -1459,7 +1600,7 @@
     def body_back(at):
         rows = pl.ds(at, STRIP)
         values, piece = norm_pull(
-            resid[rows, :].astype(jnp.float32), gain_mix[...], total_back(at)
+            resid[rows, :].astype(jnp.float32), both_gains[0:1, :], total_back(at)
         )
         gains[0:1, :] += piece
         mine[rows, :] = (d_resid[rows, :] + values).astype(jnp.bfloat16)
@@ -1512,6 +1653,7 @@
 
     lax.fori_loop(0, rows_all // 256, weights, line.at)
     line.skip(rows_all // 256)
+    assert line.at + AHEAD <= line.first + line.lead
     load.wait()
     pl.semaphore_wait(free, 3)
     total_out = reduce_shards(copies, parts, *buffers, between=between)
@@ -1571,7 +1713,8 @@
     all_gains = gain_sum[...]
     for place in range(7):
         all_gains = all_gains + gain_in[place]
-    out_gain[...] = all_gains
+    gain_z[0] = all_gains
+    out_gain[...] = gain_z[0, :, part(r, out_gain.shape[1], out_gain.shape[1])]
     out_vec[r] = vec_sum[...]
     for step in (0, 1, 2):
         out_vec[(r + 3 - step) % 4] = vec_in[6 - step]
@@ -1586,6 +1729,97 @@
         for copy in group:
             copy.wait_send()
     copies.finish()
+
+
+def unpack_kernel(grads, gates, vec, output, grad_in, *outs):
+    out_t, grad_t, x_grad, y_grad, out_grad, gate_grad, up_grad, down_grad, rec_w, in_w = outs[:10]
+    wide, ff, rec = (grads.shape[2], gate_grad.shape[1] // 4, x_grad.shape[1] // 4)
+    head = wide - 2 * ff
+    rest = ff - head
+    out_t[...] = output[...].astype(jnp.float32).T.astype(out_t.dtype)
+    grad_t[...] = grad_in[...].astype(jnp.float32).T
+    for row in range(4):
+        wide_span, span = (slice(row * ff, (row + 1) * ff), slice(row * rec, (row + 1) * rec))
+
+        def body(at):
+            rows = pl.ds(at, STRIP)
+            early = grads[row, rows, :].astype(jnp.float32)
+            late = grads[4 + row, rows, :].astype(jnp.float32)
+            gate_grad[rows, wide_span] = early[:, :ff]
+            up_grad[rows, wide_span] = early[:, ff : 2 * ff]
+            down_grad[rows, row * ff : row * ff + head] = early[:, 2 * ff :]
+            down_grad[rows, row * ff + head : (row + 1) * ff] = late[:, :rest]
+            x_grad[rows, span] = late[:, rest : rest + rec]
+            y_grad[rows, span] = late[:, rest + rec : rest + 2 * rec]
+
+        strips(BLOCK, body)
+        last = grads[4 + row, :, rest + 2 * rec : rest + 3 * rec]
+        out_grad[span, :] = last.astype(jnp.float32).T
+    heads, width = (rec_w.shape[0], rec_w.shape[1])
+    for tile in range(5):
+        spots = [item for item in gate_tiles(2 * rec) if item[0] == tile]
+        values = jnp.concatenate(
+            [gates[0, which, :, spot : spot + length] for _, _, length, which, spot in spots],
+            axis=1,
+        ).astype(jnp.float32)
+        rows = slice(tile * PACK, (tile + 1) * PACK)
+        for place in range(heads):
+            rec_w[place, rows, :] = values[:, place * width : (place + 1) * width]
+            in_w[place, rows, :] = values[:, rec + place * width : rec + (place + 1) * width]
+    line = 0
+    for ref in outs[10:]:
+        for row in range(ref.shape[0]):
+            ref[row : row + 1, :] = jnp.concatenate(
+                [vec[place, line : line + 1, :] for place in range(4)], axis=1
+            )
+            line += 1
+
+
+def unpack(grads, gates, vec, output, grad_in, rec, ff, heads):
+    depth, wide = grads.shape[1:]
+    tokens, head = (output.shape[0], rec // heads)
+
+    def out(*dims, kind=jnp.float32):
+        return jax.ShapeDtypeStruct(dims, kind)
+
+    def rows(columns):
+        return pl.BlockSpec((BLOCK, columns), lambda i: (i, 0))
+
+    def columns(length):
+        return pl.BlockSpec((length, BLOCK), lambda i: (0, i))
+
+    def whole(*dims):
+        return pl.BlockSpec(dims, lambda i: (0,) * len(dims))
+
+    blocks = pl.BlockSpec((heads, head, head), lambda i: (i, 0, 0))
+    lines = (1, 1, 4, 1, 1, 1, 1)
+    return pl.pallas_call(
+        unpack_kernel,
+        grid=(depth // BLOCK,),
+        in_specs=[
+            pl.BlockSpec((8, BLOCK, wide), lambda i: (0, i, 0)),
+            pl.BlockSpec((1, 2, PACK, wide), lambda i: (i, 0, 0, 0)),
+            whole(*vec.shape),
+            columns(tokens),
+            columns(tokens),
+        ],
+        out_specs=[rows(tokens), rows(tokens), rows(4 * rec), rows(4 * rec), columns(4 * rec)]
+        + [rows(4 * ff)] * 3
+        + [blocks] * 2
+        + [whole(count, 4 * rec) for count in lines],
+        out_shape=[
+            out(depth, tokens, kind=output.dtype),
+            out(depth, tokens),
+            out(depth, 4 * rec),
+            out(depth, 4 * rec),
+            out(4 * rec, depth),
+        ]
+        + [out(depth, 4 * ff)] * 3
+        + [out(4 * heads, head, head)] * 2
+        + [out(count, 4 * rec) for count in lines],
+        compiler_params=pltpu.CompilerParams(vmem_limit_bytes=60 << 20),
+        name="unpack",
+    )(grads, gates, vec, output, grad_in)
 
 
 def dot(left, right, dims, kind=jnp.float32):
@@ -1625,23 +1859,17 @@
     def mine(array, size, axis=0):
         return lax.dynamic_slice_in_dim(array, r * size, size, axis)
 
-    mix_in = jnp.concatenate(
-        [x_proj.reshape(depth, 4, rec), y_proj.reshape(depth, 4, rec)], axis=2
-    ).transpose(1, 0, 2)
-    flags = jnp.pad(starts.astype(jnp.float32).reshape(-1, 128), ((0, 6), (0, 0)))
-    x_all, s_all, g_all, mix_w, out_w = gather(
-        inputs.T, flags, jnp.stack([mix_gain, mlp_gain]), mix_in, out_proj
+    flags = jnp.broadcast_to(starts.astype(jnp.float32)[:, None], (starts.shape[0], 128))
+    x_all, c_all, s_all, g_all, mix_w, out_w = gather(
+        inputs.T,
+        cotangent.T,
+        flags,
+        jnp.stack([mix_gain, mlp_gain]),
+        x_proj,
+        y_proj,
+        out_proj,
     )
     tokens, model = x_all.shape
-    gain_mix, gain_mlp = (g_all[0:1], g_all[1:2])
-    fresh = s_all[:, :2, :].reshape(tokens)
-    stale = 1.0 - fresh
-    stale_one = jnp.concatenate([jnp.zeros((1,), jnp.float32), stale[:-1]])
-    stale_two = jnp.concatenate([jnp.zeros((2,), jnp.float32), stale[:-2]])
-    nothing = jnp.zeros_like(fresh)
-    masks = jnp.stack(
-        [fresh, stale, stale * stale_one, stale * stale_one * stale_two] + [nothing] * 4, axis=1
-    )
     vectors = jnp.concatenate(
         [
             x_bias[None],
@@ -1673,11 +1901,11 @@
     slices = jax.ShapeDtypeStruct((4 * depth, width), low)
     kept = [((tokens, model), low), ((tokens, 2 * rec), jnp.float32), ((tokens, padded), low)]
     kept += [((tokens, rec), kind) for kind in (jnp.float32, low) + (jnp.float32,) * 3]
+    kept.append(((tokens, 8), jnp.float32))
     row8 = pltpu.VMEM((8, rec), jnp.float32)
     (
         normed_mlp,
         resid_mid,
-        c_all,
         gate_w,
         up_w,
         down_w,
@@ -1689,19 +1917,28 @@
         rec_gate,
         in_gate,
         states,
+        masks,
     ) = vmem_call(
         forward_kernel,
         "forward",
         FORWARD_ID,
-        (x_all, masks, vec, rec_w, in_w, mix_w, out_w, gain_mix, gain_mlp),
-        [full, part, full] + [slices] * 3 + [jax.ShapeDtypeStruct(*item) for item in kept],
+        (vec, rec_w, in_w, g_all),
+        [full, part] + [slices] * 3 + [jax.ShapeDtypeStruct(*item) for item in kept],
         [pl.ANY, pltpu.VMEM] + [pl.ANY] * 12,
         [pltpu.VMEM(*item) for item in kept]
         + [row8, row8, pltpu.VMEM((tokens, model), low)]
+        + [
+            pltpu.VMEM((tokens, model), low),
+            pltpu.VMEM((tokens, 128), jnp.float32),
+            pltpu.VMEM(mix_w.shape, low),
+            pltpu.VMEM(out_w.shape, low),
+            pltpu.VMEM((8, 8), jnp.float32),
+            pltpu.SemaphoreType.DMA((11,)),
+        ]
         + reduce_scratch(size, model)
-        + [piece, pltpu.SemaphoreType.DMA((8,))],
+        + [piece, pltpu.SemaphoreType.DMA((9,))],
         80,
-        (cotangent.T, *weights),
+        (x_all, s_all.reshape(tokens, 128), mix_w, out_w, *weights),
     )
     gate = dot(normed_mlp, gate_w, CONTRACT_PLAIN)
     up = dot(normed_mlp, up_w, CONTRACT_PLAIN)
@@ -1733,14 +1970,14 @@
         backward_kernel,
         "backward",
         BACKWARD_ID,
-        (resid_mid, gain_mlp, gain_mix, masks, vec, rec_w, in_w, mix_w, out_w),
+        (resid_mid, g_all, masks, vec, rec_w, in_w, mix_w, out_w),
         [
             block,
             block,
             jax.ShapeDtypeStruct((4 * SEGMENTS + 1, depth, wide), low),
             jax.ShapeDtypeStruct((4, 2, PACK, wide), low),
             jax.ShapeDtypeStruct((4, 16, rec), jnp.float32),
-            jax.ShapeDtypeStruct((2, model), jnp.float32),
+            jax.ShapeDtypeStruct((2, depth), jnp.float32),
         ],
         [pl.ANY] * 4 + [pltpu.VMEM] * 2,
         line_scratch(depth, wide, CHUNK, PACK // CHUNK)
@@ -1788,46 +2025,9 @@
             dot(c_all, activ, CONTRACT_ROWS, low),
         ),
     )
-    tiles = [[], [], [], [], []]
-    for tile, first, length, which, spot in gate_tiles(2 * heads * head):
-        tiles[tile].append(gates[:, which, :, spot : spot + length])
-    gates = jnp.concatenate([jnp.concatenate(item, axis=2) for item in tiles], axis=1)
-    gates = gates.reshape(4, head, 2, heads, head).transpose(2, 0, 3, 1, 4)
-    gates = gates.reshape(2, 4 * heads, head, head).astype(jnp.float32)
-    vec_sums = vec_sums.transpose(1, 0, 2).reshape(vec_sums.shape[1], 4 * rec)
-    gains = lax.dynamic_slice_in_dim(gains, r * depth, depth, 1)
-
-    def columns(*spans):
-        return jnp.concatenate(
-            [grads[4 * seg + i, :, a : a + n] for i in range(4) for seg, a, n in spans], axis=1
-        ).astype(jnp.float32)
-
-    head_width = wide - 2 * width
-    after = width - head_width
-    grad_out = jnp.concatenate(
-        [grads[4 + i, :, after + 2 * rec : after + 3 * rec].T for i in range(4)], axis=0
-    ).astype(jnp.float32)
-    return (
-        output.T,
-        grad_in.astype(jnp.float32).T,
-        columns((1, after, rec)),
-        columns((1, after + rec, rec)),
-        grad_out,
-        columns((0, 0, width)),
-        columns((0, width, width)),
-        columns((0, 2 * width, head_width), (1, 0, after)),
-        gains[0],
-        gains[1],
-        vec_sums[0],
-        vec_sums[1],
-        vec_sums[2:6],
-        vec_sums[6],
-        gates[0],
-        gates[1],
-        vec_sums[7],
-        vec_sums[8],
-        vec_sums[9],
-    )
+    done = unpack(grads, gates, vec_sums, output, grad_in, rec, width, heads)
+    lines = [item if item.shape[0] > 1 else item[0] for item in done[10:]]
+    return (*done[:8], gains[0], gains[1], *lines[:4], *done[8:10], *lines[4:])
 
 
 def fits(mesh):

time: 662 us -> 609 us (0.920)
  local copies, waits for them, and re-layouts: 46.2 us -> 11.2 us
  other arithmetic: 19.9 us -> 12.2 us
    pallas_call x2, Pallas kernels: 491 us -> 449 us  [vmem_call(): pl.pallas_call(kernel, in_specs=[pl.BlockSpec(memory_space=pltpu.VMEM)] *...]
    pallas_call x1 -> x2, Pallas kernels: 51.1 us -> 88.5 us  [the longest x1 68.6 us: gather(): pl.pallas_call(gather_kernel, in_specs=[pl.BlockSpec(memory_space=pltpu.H...]
    convert_element_type x6 -> x1, other arithmetic: 14.2 us -> 0.74 us  [local_plane(): starts.astype(jnp.float32)[:, None]]
    unnamed x58 -> x14, local copies, waits for them, and re-layouts: 14.4 us -> 3.07 us
    concatenate x10 -> x0, local copies, waits for them, and re-layouts: 8.98 us -> none  [the longest x3 4.94 us: columns(): jnp.concatenate([grads[4 * seg + i, :, a:a + n] for i in range(4) for seg...]
    pallas_call x0 -> x6, other arithmetic: none -> 7.83 us  [unpack(): pl.pallas_call(unpack_kernel, grid=(depth // BLOCK,), in_specs=[pl.BlockS...]
    slice x10 -> x1, local copies, waits for them, and re-layouts: 8.18 us -> 1.34 us  [local_plane(): return (*done[:8], gains[0], gains[1], *lines[:4], *done[8:10], *lines[4:])]
where the time goes in v5:
time: 609 us; the launch traced here: 605 us
  Pallas kernels  537 us (88%)
  matrix products  43.5 us (7%)
  other arithmetic  12.2 us (2%)
  local copies, waits for them, and re-layouts  11.2 us (2%)
    pallas_call x2, Pallas kernels, vmem_call(): pl.pallas_call(kernel, in_specs=[pl.BlockSpec(memory_space=pltpu.VMEM)] *...  449 us
    pallas_call x1, Pallas kernels, gather(): pl.pallas_call(gather_kernel, in_specs=[pl.BlockSpec(memory_space=pltpu.H...  68.6 us
    dot_general x7, matrix products, dot(): lax.dot_general(left, right, dims, preferred_element_type=jnp.float32)  35.1 us
    pallas_call x1, Pallas kernels, unpack(): pl.pallas_call(unpack_kernel, grid=(depth // BLOCK,), in_specs=[pl.BlockS...  19.9 us

profile of v5, /device:TPU:0, one launch (start us, length us, event | category | flops | bytes accessed | tf_op | source)
XLA Modules:
  0.0 605.0 jit_solution(7068437119561814358)
XLA Ops:
  0.7 0.0 copy-start.1
  0.7 0.7 convert_element_type.33
  1.4 1.3 pad_maximum_fusion.g_in
  2.7 0.7 broadcast_in_dim.26
  3.4 0.7 broadcast_in_dim.27
  4.1 0.7 broadcast_in_dim.28
  4.8 0.7 broadcast_in_dim.29
  5.5 0.7 broadcast_in_dim.30
  6.2 0.7 divide_multiply_fusion
  7.0 0.8 concatenate.9
  7.8 0.7 constant_dynamic-slice_fusion.vec
  8.5 0.8 broadcast_in_dim.32.s_in
  9.2 1.0 dynamic-slice_bitcast_fusion.1
  10.3 0.8 fusion.5.in_w
  11.0 0.8 fusion.4.rec_w
  11.8 2.0 copy.39
  13.9 0.0 copy-done.1
  13.9 1.0 copy.40
  14.9 68.6 %gather.1 = (bf16[1024,2048]{1,0:T(8,128)(2,1)}, bf16[1024,2048]{1,0:T(8,128)(2,1)}, f32[4,256,128]{2,1,0:T(8,128)}, f32[2,2048]{1,0:T(2,128)}, bf16[2048,640]{1,0:T(8,128)(2,1)}, /*index=5*/bf16[320,2048]{1,0:T(8,128)(2,1)}) custom-call(bf16[512,512]{1,0:T(8,128)(2,1)} %bitcast.33, bf16[512,512]{1,0:T(8,128)(2,1)} %bitcast.34, ...), custom_call_target="tpu_custom_call" | custom-call | tf_op jit(solution)/shard_map/gather/pallas_call | solution.py:802
  83.5 93.6 %forward.1 = (bf16[1024,2048]{1,0:T(8,128)(2,1)}, f32[128,2048]{1,0:T(8,128)}, bf16[2048,768]{1,0:T(8,128)(2,1)}, bf16[2048,768]{1,0:T(8,128)(2,1)}, bf16[2048,7...) custom-call(f32[16,320]{1,0:T(8,128)} %constant_dynamic-slice_fusion, ...), custom_call_target="tpu_custom_call" | custom-call | tf_op jit(solution)/shard_map/forward/pallas_call | solution.py:1082
  177.0 0.0 copy-start.2
  177.1 0.0 copy-start.4
  177.1 6.3 %fusion.8 = f32[1024,768]{1,0:T(8,128)S(1)} fusion(bf16[1024,2048]{1,0:T(8,128)(2,1)} %get-tuple-element.69.refs_2_, bf16[2048,768]{1,0:T(8,128)(2,1)} %get-tuple-element.70), kind=kOutput, calls=%fused_computation.28 | convolution fusion | flops 3221225472 | bytes 10485760 | tf_op jit(solution)/shard_map/dot_general | solution.py:1826
  183.4 0.0 copy-done.2
  183.4 0.0 copy-done.4
  183.4 0.0 copy-start.3
  183.4 3.4 fusion.9
  186.8 0.0 copy-done.3
  186.8 0.0 copy-start.5
  186.8 5.1 multiply_convert_fusion
  192.0 0.0 copy-done.5
  192.0 0.0 copy-start
  192.0 5.2 convolution_convert_fusion.refs_1_
  197.2 0.0 copy-done
  197.2 5.0 convolution_convert_fusion.1.refs_14_
  202.2 5.0 convolution_convert_fusion.3.refs_12_
  207.2 5.0 convolution_convert_fusion.2.refs_13_
  212.2 3.4 fusion.10
  215.7 5.0 add_convert_fusion.refs_0_
  220.7 355.2 %backward.1 = (bf16[512,512]{1,0:T(8,128)(2,1)}, bf16[512,512]{1,0:T(8,128)(2,1)}, bf16[9,512,1664]{2,1,0:T(8,128)(2,1)}, bf16[4,2,32,1664]{3,2,1,0:T(8,128)(2,1...) custom-call(f32[128,2048]{1,0:T(8,128)} %get-tuple-element.67.resid_mid, f32[2,2048]{1,0:T(2,128)} %get-tuple-element.62.gains.both_gains, ...), custom_call_target="tpu_custom_call" | custom-call | tf_op jit(solution)/shard_map/backward/pallas_call | solution.py:1082
  575.9 1.3 fusion.7
  577.2 19.9 %unpack.1 = (bf16[512,512]{1,0:T(8,128)(2,1)}, f32[512,512]{1,0:T(8,128)}, f32[512,1280]{1,0:T(8,128)}, f32[512,1280]{1,0:T(8,128)}, f32[1280,512]{1,0:T(8,128)}...) custom-call(bf16[9,512,1664]{2,1,0:T(8,128)(2,1)} %get-tuple-element, ...), custom_call_target="tpu_custom_call" | custom-call | tf_op jit(solution)/shard_map/unpack/pallas_call | solution.py:1796
  597.1 1.3 reduce
  598.4 1.3 reduce.1
  599.7 1.3 reduce.2
  601.1 1.3 reduce.3
  602.4 1.3 reduce.4
  603.7 1.3 reduce.5
  (3 shorter events, 0.0 us)
Async XLA Ops:
  0.7 13.2 %copy-start.1 = (bf16[512,512]{1,0:T(8,128)(2,1)S(1)}, bf16[512,512]{1,0:T(8,128)(2,1)}, u32[]{:S(2)}) copy-start(bf16[512,512]{1,0:T(8,128)(2,1)} %param.21) | copy-start | bytes 1572868
  177.0 6.3 %copy-start.2 = (bf16[1024,2048]{1,0:T(8,128)(2,1)S(1)}, bf16[1024,2048]{1,0:T(8,128)(2,1)}, u32[]{:S(2)}) copy-start(bf16[1024,2048]{1,0:T(8,128)(2,1)} %get-tuple-element.71) | copy-start | bytes 12582916
  177.1 6.3 %copy-start.4 = (bf16[2048,768]{1,0:T(8,128)(2,1)S(1)}, bf16[2048,768]{1,0:T(8,128)(2,1)}, u32[]{:S(2)}) copy-start(bf16[2048,768]{1,0:T(8,128)(2,1)} %get-tuple-element.73) | copy-start | bytes 9437188
  183.4 3.4 copy-start.3
  186.8 5.2 copy-start.5
  192.0 5.2 copy-start

commit v6 on v5

--- a/solution.py
+++ b/solution.py
@@ -772,9 +772,12 @@
         copies.go(g_in, small, None),
     ]
     for peer in (twin, side, cross):
-        late.append(copies.go(s_in, s_all.at[r], peer))
         late.append(copies.go(g_in, small, peer))
+    flags_side = copies.go(s_in, s_all.at[r], side)
+    late.append(copies.go(s_in, s_all.at[r], twin))
     late.extend(spread_tall(copies, c_in, block_of(c_all, rows, columns), between))
+    arrived(flags_side)
+    late.append(copies.go(s_all.at[across(r)], s_all.at[across(r)], twin))
     moves[0].finish()
     for copy in late:
         arrived(copy)
@@ -1016,7 +1019,7 @@
                 moves.step()
 
         load_rows(index).wait()
-        marks = mark_rows(flags[rows, :8], mark_tail)
+        marks = mark_rows(flags[rows, :8].astype(jnp.float32), mark_tail)
         masks[rows, :] = marks
 
         def norm(at):
@@ -1431,7 +1434,7 @@
 LINE_REFS = 12
 PACK = 32
 CHUNK = 32
-PACE = (2, 3, 3, 1, 1, 1, 2, 5, 6)
+PACE = (2, 3, 3, 1, 1, 2, 2, 3, 3)
 BLOCK_STEPS = 1
 
 
@@ -1742,7 +1745,7 @@
         wide_span, span = (slice(row * ff, (row + 1) * ff), slice(row * rec, (row + 1) * rec))
 
         def body(at):
-            rows = pl.ds(at, STRIP)
+            rows = pl.ds(at, 64)
             early = grads[row, rows, :].astype(jnp.float32)
             late = grads[4 + row, rows, :].astype(jnp.float32)
             gate_grad[rows, wide_span] = early[:, :ff]
@@ -1752,7 +1755,8 @@
             x_grad[rows, span] = late[:, rest : rest + rec]
             y_grad[rows, span] = late[:, rest + rec : rest + 2 * rec]
 
-        strips(BLOCK, body)
+        body(0)
+        body(64)
         last = grads[4 + row, :, rest + 2 * rec : rest + 3 * rec]
         out_grad[span, :] = last.astype(jnp.float32).T
     heads, width = (rec_w.shape[0], rec_w.shape[1])
@@ -1859,7 +1863,7 @@
     def mine(array, size, axis=0):
         return lax.dynamic_slice_in_dim(array, r * size, size, axis)
 
-    flags = jnp.broadcast_to(starts.astype(jnp.float32)[:, None], (starts.shape[0], 128))
+    flags = jnp.broadcast_to(starts.astype(low)[:, None], (starts.shape[0], 128))
     x_all, c_all, s_all, g_all, mix_w, out_w = gather(
         inputs.T,
         cotangent.T,
@@ -1929,7 +1933,7 @@
         + [row8, row8, pltpu.VMEM((tokens, model), low)]
         + [
             pltpu.VMEM((tokens, model), low),
-            pltpu.VMEM((tokens, 128), jnp.float32),
+            pltpu.VMEM((tokens, 128), low),
             pltpu.VMEM(mix_w.shape, low),
             pltpu.VMEM(out_w.shape, low),
             pltpu.VMEM((8, 8), jnp.float32),

time: 609 us -> 600 us (0.985)
  Pallas kernels: 537 us -> 528 us
where the time goes in v6:
time: 600 us; the launch traced here: 596 us
  Pallas kernels  528 us (88%)
  matrix products  43.5 us (7%)
  other arithmetic  12.2 us (2%)
  local copies, waits for them, and re-layouts  11.2 us (2%)
    pallas_call x2, Pallas kernels, vmem_call(): pl.pallas_call(kernel, in_specs=[pl.BlockSpec(memory_space=pltpu.VMEM)] *...  447 us
    pallas_call x1, Pallas kernels, gather(): pl.pallas_call(gather_kernel, in_specs=[pl.BlockSpec(memory_space=pltpu.H...  66.6 us
    dot_general x7, matrix products, dot(): lax.dot_general(left, right, dims, preferred_element_type=jnp.float32)  35.1 us
    pallas_call x1, Pallas kernels, unpack(): pl.pallas_call(unpack_kernel, grid=(depth // BLOCK,), in_specs=[pl.BlockS...  14.9 us

profile of v6, /device:TPU:0, one launch (start us, length us, event | category | flops | bytes accessed | tf_op | source)
XLA Modules:
  0.0 595.7 jit_solution(9425552804905277337)
XLA Ops:
  0.7 0.0 copy-start.1
  0.7 0.7 convert_element_type.33
  1.4 1.3 pad_maximum_fusion.g_in
  2.7 0.7 broadcast_in_dim.26
  3.4 0.7 broadcast_in_dim.27
  4.1 0.7 broadcast_in_dim.28
  4.8 0.7 broadcast_in_dim.29
  5.5 0.7 broadcast_in_dim.30
  6.2 0.7 divide_multiply_fusion
  7.0 0.8 concatenate.9
  7.8 0.7 constant_dynamic-slice_fusion.vec
  8.5 0.7 broadcast_in_dim.32.s_in
  9.2 1.0 dynamic-slice_bitcast_fusion.1
  10.2 0.8 fusion.5.in_w
  11.0 0.8 fusion.4.rec_w
  11.8 2.0 copy.39
  13.9 0.0 copy-done.1
  13.9 1.0 copy.40
  14.9 66.6 %gather.1 = (bf16[1024,2048]{1,0:T(8,128)(2,1)}, bf16[1024,2048]{1,0:T(8,128)(2,1)}, bf16[4,256,128]{2,1,0:T(8,128)(2,1)}, f32[2,2048]{1,0:T(2,128)}, bf16[2048,...) custom-call(bf16[512,512]{1,0:T(8,128)(2,1)} %bitcast.33, bf16[512,512]{1,0:T(8,128)(2,1)} %bitcast.34, ...), custom_call_target="tpu_custom_call" | custom-call | tf_op jit(solution)/shard_map/gather/pallas_call | solution.py:805
  81.5 92.2 %forward.1 = (bf16[1024,2048]{1,0:T(8,128)(2,1)}, f32[128,2048]{1,0:T(8,128)}, bf16[2048,768]{1,0:T(8,128)(2,1)}, bf16[2048,768]{1,0:T(8,128)(2,1)}, bf16[2048,7...) custom-call(f32[16,320]{1,0:T(8,128)} %constant_dynamic-slice_fusion, ...), custom_call_target="tpu_custom_call" | custom-call | tf_op jit(solution)/shard_map/forward/pallas_call | solution.py:1085
  173.7 0.0 copy-start.2
  173.7 0.0 copy-start.4
  173.7 6.3 %fusion.8 = f32[1024,768]{1,0:T(8,128)S(1)} fusion(bf16[1024,2048]{1,0:T(8,128)(2,1)} %get-tuple-element.69.refs_2_, bf16[2048,768]{1,0:T(8,128)(2,1)} %get-tuple-element.70), kind=kOutput, calls=%fused_computation.28 | convolution fusion | flops 3221225472 | bytes 10485760 | tf_op jit(solution)/shard_map/dot_general | solution.py:1830
  180.0 0.0 copy-done.2
  180.0 0.0 copy-done.4
  180.0 0.0 copy-start.3
  180.0 3.4 fusion.9
  183.4 0.0 copy-done.3
  183.5 0.0 copy-start.5
  183.5 5.1 multiply_convert_fusion
  188.6 0.0 copy-done.5
  188.6 0.0 copy-start
  188.6 5.2 convolution_convert_fusion.refs_1_
  193.8 0.0 copy-done
  193.8 5.0 convolution_convert_fusion.1.refs_14_
  198.8 5.0 convolution_convert_fusion.3.refs_12_
  203.8 5.0 convolution_convert_fusion.2.refs_13_
  208.9 3.4 fusion.10
  212.3 5.0 add_convert_fusion.refs_0_
  217.3 354.3 %backward.1 = (bf16[512,512]{1,0:T(8,128)(2,1)}, bf16[512,512]{1,0:T(8,128)(2,1)}, bf16[9,512,1664]{2,1,0:T(8,128)(2,1)}, bf16[4,2,32,1664]{3,2,1,0:T(8,128)(2,1...) custom-call(f32[128,2048]{1,0:T(8,128)} %get-tuple-element.67.resid_mid, f32[2,2048]{1,0:T(2,128)} %get-tuple-element.62.gains.both_gains, ...), custom_call_target="tpu_custom_call" | custom-call | tf_op jit(solution)/shard_map/backward/pallas_call | solution.py:1085
  571.7 1.3 fusion.7
  573.0 14.9 %unpack.1 = (bf16[512,512]{1,0:T(8,128)(2,1)}, f32[512,512]{1,0:T(8,128)}, f32[512,1280]{1,0:T(8,128)}, f32[512,1280]{1,0:T(8,128)}, f32[1280,512]{1,0:T(8,128)}...) custom-call(bf16[9,512,1664]{2,1,0:T(8,128)(2,1)} %get-tuple-element, ...), custom_call_target="tpu_custom_call" | custom-call | tf_op jit(solution)/shard_map/unpack/pallas_call | solution.py:1800
  587.9 1.3 reduce
  589.2 1.3 reduce.1
  590.5 1.3 reduce.2
  591.8 1.3 reduce.3
  593.1 1.3 reduce.4
  594.4 1.3 reduce.5
  (3 shorter events, 0.0 us)
Async XLA Ops:
  0.7 13.2 %copy-start.1 = (bf16[512,512]{1,0:T(8,128)(2,1)S(1)}, bf16[512,512]{1,0:T(8,128)(2,1)}, u32[]{:S(2)}) copy-start(bf16[512,512]{1,0:T(8,128)(2,1)} %param.21) | copy-start | bytes 1572868
  173.7 6.3 %copy-start.2 = (bf16[1024,2048]{1,0:T(8,128)(2,1)S(1)}, bf16[1024,2048]{1,0:T(8,128)(2,1)}, u32[]{:S(2)}) copy-start(bf16[1024,2048]{1,0:T(8,128)(2,1)} %get-tuple-element.71) | copy-start | bytes 12582916
  173.7 6.3 %copy-start.4 = (bf16[2048,768]{1,0:T(8,128)(2,1)S(1)}, bf16[2048,768]{1,0:T(8,128)(2,1)}, u32[]{:S(2)}) copy-start(bf16[2048,768]{1,0:T(8,128)(2,1)} %get-tuple-element.73) | copy-start | bytes 9437188
  180.0 3.4 copy-start.3
  183.5 5.2 copy-start.5
  188.6 5.2 copy-start

commit v7 on v6

--- a/solution.py
+++ b/solution.py
@@ -1533,7 +1533,7 @@
             )
         )
     ]
-    for copy in loads:
+    for copy in loads[:4]:
         copy.start()
     for ref in (gains, sums, edge, carry):
         ref[...] = jnp.zeros_like(ref)
@@ -1541,6 +1541,8 @@
         copy.wait()
     line.prime()
     loads[3].wait()
+    for copy in loads[4:]:
+        copy.start()
     pace = iter(PACE)
 
     def between():
@@ -1876,18 +1878,17 @@
     tokens, model = x_all.shape
     vectors = jnp.concatenate(
         [
-            x_bias[None],
-            y_bias[None],
-            conv_w,
-            conv_b[None],
-            rec_gate_b[None],
-            in_gate_b[None],
-            -GATE_C * jax.nn.softplus(decay_param)[None],
-            -GATE_C * jax.nn.sigmoid(decay_param)[None],
-            jnp.zeros((5, x_bias.shape[0]), jnp.float32),
-        ],
-        axis=0,
-    )
+            x_bias,
+            y_bias,
+            conv_w.reshape(-1),
+            conv_b,
+            rec_gate_b,
+            in_gate_b,
+            -GATE_C * jax.nn.softplus(decay_param),
+            -GATE_C * jax.nn.sigmoid(decay_param),
+            jnp.zeros((5 * x_bias.shape[0],), jnp.float32),
+        ]
+    ).reshape(-1, x_bias.shape[0])
     vec = mine(vectors, rec, 1)
 
     def diagonal(blocks):

time: 600 us -> 601 us (level)
  no operation moved by 1% of the time
where the time goes in v7:
time: 601 us; the launch traced here: 596 us
  Pallas kernels  528 us (88%)
  matrix products  43.5 us (7%)
  other arithmetic  12.9 us (2%)
  local copies, waits for them, and re-layouts  11.1 us (2%)
    pallas_call x2, Pallas kernels, vmem_call(): pl.pallas_call(kernel, in_specs=[pl.BlockSpec(memory_space=pltpu.VMEM)] *...  447 us
    pallas_call x1, Pallas kernels, gather(): pl.pallas_call(gather_kernel, in_specs=[pl.BlockSpec(memory_space=pltpu.H...  66.6 us
    dot_general x7, matrix products, dot(): lax.dot_general(left, right, dims, preferred_element_type=jnp.float32)  35.1 us
    pallas_call x1, Pallas kernels, unpack(): pl.pallas_call(unpack_kernel, grid=(depth // BLOCK,), in_specs=[pl.BlockS...  14.9 us

profile of v7, /device:TPU:0, one launch (start us, length us, event | category | flops | bytes accessed | tf_op | source)
XLA Modules:
  0.0 596.4 jit_solution(16228381788190361711)
XLA Ops:
  0.7 0.0 copy-start.1
  0.7 0.7 convert_element_type.33
  1.4 1.3 pad_maximum_fusion.g_in
  2.7 0.7 reshape.48
  3.4 0.7 broadcast_in_dim.10.s_in
  4.2 0.7 constant_dynamic-update-slice_fusion.5
  4.9 0.7 constant_dynamic-update-slice_fusion.4
  5.6 0.7 constant_dynamic-update-slice_fusion.2
  6.3 0.7 constant_dynamic-update-slice_fusion.1
  7.0 0.7 constant_dynamic-update-slice_fusion
  7.7 0.7 fusion.7
  8.4 0.7 multiply_dynamic-update-slice_fusion
  9.2 0.7 constant_dynamic-slice_fusion.vec
  9.9 1.0 dynamic-slice_bitcast_fusion.1
  10.9 0.8 fusion.5.in_w
  11.7 0.8 fusion.4.rec_w
  12.5 2.0 copy.39
  14.5 0.0 copy-done.1
  14.5 1.0 copy.40
  15.5 66.6 %gather.1 = (bf16[1024,2048]{1,0:T(8,128)(2,1)}, bf16[1024,2048]{1,0:T(8,128)(2,1)}, bf16[4,256,128]{2,1,0:T(8,128)(2,1)}, f32[2,2048]{1,0:T(2,128)}, bf16[2048,...) custom-call(bf16[512,512]{1,0:T(8,128)(2,1)} %bitcast.33, bf16[512,512]{1,0:T(8,128)(2,1)} %bitcast.34, ...), custom_call_target="tpu_custom_call" | custom-call | tf_op jit(solution)/shard_map/gather/pallas_call | solution.py:805
  82.1 92.2 %forward.1 = (bf16[1024,2048]{1,0:T(8,128)(2,1)}, f32[128,2048]{1,0:T(8,128)}, bf16[2048,768]{1,0:T(8,128)(2,1)}, bf16[2048,768]{1,0:T(8,128)(2,1)}, bf16[2048,7...) custom-call(f32[16,320]{1,0:T(8,128)} %constant_dynamic-slice_fusion, ...), custom_call_target="tpu_custom_call" | custom-call | tf_op jit(solution)/shard_map/forward/pallas_call | solution.py:1085
  174.3 0.0 copy-start.2
  174.3 0.0 copy-start.4
  174.4 6.3 %fusion.9 = f32[1024,768]{1,0:T(8,128)S(1)} fusion(bf16[1024,2048]{1,0:T(8,128)(2,1)} %get-tuple-element.69.refs_2_, bf16[2048,768]{1,0:T(8,128)(2,1)} %get-tuple-element.70), kind=kOutput, calls=%fused_computation.36 | convolution fusion | flops 3221225472 | bytes 10485760 | tf_op jit(solution)/shard_map/dot_general | solution.py:1832
  180.7 0.0 copy-done.2
  180.7 0.0 copy-done.4
  180.7 0.0 copy-start.3
  180.7 3.4 fusion.10
  184.1 0.0 copy-done.3
  184.1 0.0 copy-start.5
  184.1 5.1 multiply_convert_fusion
  189.3 0.0 copy-done.5
  189.3 0.0 copy-start
  189.3 5.2 convolution_convert_fusion.refs_1_
  194.5 0.0 copy-done
  194.5 5.0 convolution_convert_fusion.1.refs_14_
  199.5 5.0 convolution_convert_fusion.3.refs_12_
  204.5 5.0 convolution_convert_fusion.2.refs_13_
  209.5 3.4 fusion.11
  213.0 5.0 add_convert_fusion.refs_0_
  218.0 354.3 %backward.1 = (bf16[512,512]{1,0:T(8,128)(2,1)}, bf16[512,512]{1,0:T(8,128)(2,1)}, bf16[9,512,1664]{2,1,0:T(8,128)(2,1)}, bf16[4,2,32,1664]{3,2,1,0:T(8,128)(2,1...) custom-call(f32[128,2048]{1,0:T(8,128)} %get-tuple-element.67.resid_mid, f32[2,2048]{1,0:T(2,128)} %get-tuple-element.62.gains.both_gains, ...), custom_call_target="tpu_custom_call" | custom-call | tf_op jit(solution)/shard_map/backward/pallas_call | solution.py:1085
  572.3 1.3 fusion.8
  573.7 14.9 %unpack.1 = (bf16[512,512]{1,0:T(8,128)(2,1)}, f32[512,512]{1,0:T(8,128)}, f32[512,1280]{1,0:T(8,128)}, f32[512,1280]{1,0:T(8,128)}, f32[1280,512]{1,0:T(8,128)}...) custom-call(bf16[9,512,1664]{2,1,0:T(8,128)(2,1)} %get-tuple-element, ...), custom_call_target="tpu_custom_call" | custom-call | tf_op jit(solution)/shard_map/unpack/pallas_call | solution.py:1802
  588.5 1.3 reduce
  589.8 1.3 reduce.1
  591.2 1.3 reduce.2
  592.5 1.3 reduce.3
  593.8 1.3 reduce.4
  595.1 1.3 reduce.5
  (4 shorter events, 0.0 us)
Async XLA Ops:
  0.7 13.9 %copy-start.1 = (bf16[512,512]{1,0:T(8,128)(2,1)S(1)}, bf16[512,512]{1,0:T(8,128)(2,1)}, u32[]{:S(2)}) copy-start(bf16[512,512]{1,0:T(8,128)(2,1)} %param.21) | copy-start | bytes 1572868
  174.3 6.3 %copy-start.2 = (bf16[1024,2048]{1,0:T(8,128)(2,1)S(1)}, bf16[1024,2048]{1,0:T(8,128)(2,1)}, u32[]{:S(2)}) copy-start(bf16[1024,2048]{1,0:T(8,128)(2,1)} %get-tuple-element.71) | copy-start | bytes 12582916
  174.3 6.3 %copy-start.4 = (bf16[2048,768]{1,0:T(8,128)(2,1)S(1)}, bf16[2048,768]{1,0:T(8,128)(2,1)}, u32[]{:S(2)}) copy-start(bf16[2048,768]{1,0:T(8,128)(2,1)} %get-tuple-element.73) | copy-start | bytes 9437188
  180.7 3.4 copy-start.3
  184.1 5.2 copy-start.5
  189.3 5.2 copy-start
